TPU v7x, 32 devices: a whole 2x2x4 slice. The times are simulated.
32 devices in a mesh: gx: 8 (over z, core), gy: 4 (over y, x).
Axes of the slice: x: 2, y: 2, z: 4, core: 2. Of those that a mesh axis runs over, the one named last changes fastest.
Arguments:
- velocity: float32 [2048, 16, 1024], P('gx', None, 'gy'), may hold values from -6 to 6
- lower_x: float32 [2048, 256], P('gx'), may hold values from 0 to 1, as said below
- upper_x: float32 [2048, 256], P('gx'), may hold values from 0 to 1, as said below
- lower_carry_x: float32 [2048], P('gx'), may hold values from 0 to 1.3
- upper_carry_x: float32 [2048], P('gx'), may hold values from 0 to 1.3
- lower_y: float32 [1024, 256], P('gy'), may hold values from 0 to 1, as said below
- upper_y: float32 [1024, 256], P('gy'), may hold values from 0 to 1, as said below
- lower_carry_y: float32 [1024], P('gy'), may hold values from 0 to 1.3
- upper_carry_y: float32 [1024], P('gy'), may hold values from 0 to 1.3
- wall_force: float32 [2048, 16, 128], P(('gx', 'gy')), may hold values from -6 to 6
- wall_owner: int32 [2048, 1], P(('gx', 'gy')), may hold values from 0 to 3; in each aligned block of 64 rows (0 to 63, 64 to 127, ...) at most 32 rows name the same one
- wall_offset: int32 [2048], P(('gx', 'gy')), may hold values from 0 to 511
- solid_mask: int32 [2048, 8], P('gx', 'gy'), may hold values 0 or 1
Outputs:
- advanced: float32 [2048, 16, 1024], P('gx', None, 'gy')
Inputs may be any that keep to these rules, and one draw needn't show every extreme that they name: `wall_owner`: in the rows of one device no tile is named by more than 32 rows, a bound that some block reaches. `wall_offset`: the offset is row * 2 + block within the owner tile. `lower_x`: zero above the diagonal of each block of 256 rows. `upper_x`: zero below the diagonal of each block of 256 rows. `lower_y`: zero above the diagonal of each block of 256 rows. `upper_y`: zero below the diagonal of each block of 256 rows.
All inputs are finite; a program needn't handle non-finite values. No bound on the sum of `solid_mask` on one device may be relied on, other than what follows from the above.
Results may differ from a plain program's by a relative error of at most 0.00013.
Values sent between devices are 32-bit elements; how exact they have to be, the bound alone decides.
No kernel may reach another device: no remote copies, remote signals or barrier semaphores. Data moves between devices by JAX's collectives and lax.ppermute only.
A program may use at most 128 MiB of HBM per device.

v0:
```python
import jax
import jax.numpy as jnp
from jax import lax
from jax.sharding import PartitionSpec as P


def carried_in(value, axis, join, neutral, backward):
    count, mine = (lax.axis_size(axis), lax.axis_index(axis))
    pieces = jax.tree.map(lambda part: lax.all_gather(part, axis), value)
    if backward:
        pieces = jax.tree.map(lambda part: part[::-1], pieces)
        mine = count - 1 - mine
    so_far = jax.tree.map(
        lambda part, zero: jnp.full_like(part, 0) + jnp.asarray(zero, part.dtype), value, neutral
    )

    def hop(position, so_far):
        longer = join(so_far, jax.tree.map(lambda part: part[position], pieces))
        return jax.tree.map(lambda new, old: jnp.where(position < mine, new, old), longer, so_far)

    return lax.fori_loop(0, count - 1, hop, so_far)


def padded_2(shard, sides, width):
    for axis, dim in sides:
        count, length = (lax.axis_size(axis), shard.shape[dim])
        up = [(i, (i + 1) % count) for i in range(count - 1)]
        down = [(j, i) for i, j in up]
        last = lax.slice_in_dim(shard, length - width, length, axis=dim)
        leading = lax.slice_in_dim(shard, 0, width, axis=dim)
        before = lax.ppermute(last, axis, up)
        after = lax.ppermute(leading, axis, down)
        shard = jnp.concatenate([before, shard, after], axis=dim)
    return shard


def combine(earlier, later):
    return (later[0] * earlier[0], later[0] * earlier[1] + later[1])


def x_forward(retain, edge_row):
    return carried_in(
        (retain, edge_row), "gx", combine, (jnp.ones_like(retain), jnp.zeros_like(edge_row)), False
    )[1]


def x_backward(retain, edge_row):
    return carried_in(
        (retain, edge_row), "gx", combine, (jnp.ones_like(retain), jnp.zeros_like(edge_row)), True
    )[1]


def y_forward(retain, edge_row):
    return carried_in(
        (retain, edge_row), "gy", combine, (jnp.ones_like(retain), jnp.zeros_like(edge_row)), False
    )[1]


def y_backward(retain, edge_row):
    return carried_in(
        (retain, edge_row), "gy", combine, (jnp.ones_like(retain), jnp.zeros_like(edge_row)), True
    )[1]


def wall_forcing(wall_force, wall_owner, wall_offset, tile_rows, planes, tile_cols):
    entries, unused, block_width = wall_force.shape
    nblock = tile_cols // block_width
    owner_ids = wall_owner[:, 0]
    gathered, gathered_owner, gathered_offset = (
        lax.all_gather(wall_force, "gy", axis=0, tiled=True),
        lax.all_gather(owner_ids.astype(jnp.float32), "gy", axis=0, tiled=True),
        lax.all_gather(wall_offset.astype(jnp.float32), "gy", axis=0, tiled=True),
    )
    mine_mask = (gathered_owner == lax.axis_index("gy").astype(jnp.float32)).astype(jnp.float32)
    payload = gathered * mine_mask[:, None, None]
    offsets = gathered_offset.astype(jnp.int32)
    row_ids = offsets // nblock
    block_ids = offsets % nblock
    accumulated = (
        jnp.zeros((tile_rows, planes, nblock, block_width), jnp.float32)
        .at[row_ids, :, block_ids, :]
        .add(payload)
    )
    return accumulated.reshape(tile_rows, planes, tile_cols)


def on_device(
    velocity,
    lower_x,
    upper_x,
    lower_carry_x,
    upper_carry_x,
    lower_y,
    upper_y,
    lower_carry_y,
    upper_carry_y,
    wall_force,
    wall_owner,
    wall_offset,
    solid_mask,
):
    tile_rows, planes, tile_cols = velocity.shape
    block_width = wall_force.shape[2]
    nblock = tile_cols // block_width
    forcing = wall_forcing(wall_force, wall_owner, wall_offset, tile_rows, planes, tile_cols)
    padded = padded_2(velocity, (("gy", 2),), 1)
    source_term = velocity + 0.5 * (padded[:, :, 2:] + padded[:, :, :-2] - 2.0 * velocity) + forcing
    flattened = source_term.reshape(tile_rows, planes * tile_cols)
    partial_value = jnp.dot(
        lower_x, flattened, precision=lax.Precision.HIGHEST, preferred_element_type=jnp.float32
    )
    incoming = x_forward(lower_carry_x[-1], partial_value[-1])
    swept = partial_value + lower_carry_x[:, None] * incoming[None, :]
    partial_value = jnp.dot(
        upper_x, swept, precision=lax.Precision.HIGHEST, preferred_element_type=jnp.float32
    )
    incoming = x_backward(upper_carry_x[0], partial_value[0])
    halfway = (partial_value + upper_carry_x[:, None] * incoming[None, :]).reshape(
        tile_rows, planes, tile_cols
    )
    padded = padded_2(halfway, (("gx", 0),), 1)
    source_term = halfway + 0.5 * (padded[2:] + padded[:-2] - 2.0 * halfway)
    flattened = source_term.reshape(tile_rows * planes, tile_cols)
    partial_value = jnp.dot(
        flattened, lower_y.T, precision=lax.Precision.HIGHEST, preferred_element_type=jnp.float32
    )
    incoming = y_forward(lower_carry_y[-1], partial_value[:, -1])
    swept = partial_value + incoming[:, None] * lower_carry_y[None, :]
    partial_value = jnp.dot(
        swept, upper_y.T, precision=lax.Precision.HIGHEST, preferred_element_type=jnp.float32
    )
    incoming = y_backward(upper_carry_y[0], partial_value[:, 0])
    result_field = (partial_value + incoming[:, None] * upper_carry_y[None, :]).reshape(
        tile_rows, planes, nblock, block_width
    )
    fluid = (solid_mask == 0)[:, None, :, None]
    return jnp.where(fluid, result_field, jnp.float32(0.0)).reshape(tile_rows, planes, tile_cols)


def solution(mesh):
    placed = (
        P("gx", None, "gy"),
        P("gx", None),
        P("gx", None),
        P("gx"),
        P("gx"),
        P("gy", None),
        P("gy", None),
        P("gy"),
        P("gy"),
        P(("gx", "gy"), None, None),
        P(("gx", "gy"), None),
        P(("gx", "gy")),
        P("gx", "gy"),
    )
    return jax.shard_map(
        on_device, mesh=mesh, in_specs=placed, out_specs=P("gx", None, "gy"), check_vma=False
    )
```

profile of v0, /device:TPU:0, one launch (start us, length us, event | category | flops | bytes accessed | tf_op | source)
XLA Modules:
  0.0 317.8 jit_solution(13558724673775430342)
XLA Ops:
  7.3 5.3 %copy.50 = f32[256,16,256]{0,2,1:T(8,128)} copy(f32[256,16,256]{2,1,0:T(8,128)} %param.21) | data formatting | bytes 8388608 | tf_op args[0]
  17.0 5.5 %collective-permute-start.1 = (f32[256,16,1]{0,2,1:T(1,128)S(1)}, f32[256,16,1]{0,2,1:T(1,128)S(1)}, u32[]{:S(2)}, u32[]{:S(2)}) collective-permute-start(f32[256,16,1]{0,2,1:T(1,128)S(1)} %get-tuple-element.506), channel_id=1, source_target_pairs={{0,1},{1,2},{2,3},{4,5},{5,6},{6,7},{8,9},{9,10},{10,11},{12,13},{... | collective-permute-start | bytes 49160 | tf_op jit(solution)/shard_map/ppermute | solution.py:31
  22.5 16.6 %all-reduce.6 = (f32[8]{0:T(128)S(1)}, f32[8]{0:T(128)S(1)}) all-reduce(f32[8]{0:T(128)S(1)} %slice_dynamic-update-slice_fusion.3, f32[8]{0:T(128)S(1)} %slice_dynamic-update-slice_fusion.2), channel_id=1, replica_groups=mesh['gx'=8,'gy'=4] {'gx'}, use_global_device_ids=true, to_apply=%add.2 | all-reduce | flops 16 | bytes 128
  42.1 9.8 %all-reduce.7 = (f32[256]{0:T(256)S(1)}, f32[256]{0:T(256)S(1)}, f32[4]{0:T(128)S(1)}, f32[4]{0:T(128)S(1)}) all-reduce(f32[256]{0:T(256)S(1)} %convert_dynamic-update-slice_fusion, f32[256]{0:T(256)S(1)} %bitcast_dynamic-update-slice_fusion, f32[4]{0:T(128)S(1)} %slice_dynamic-update-slice_fusion.1, ...), channel_id=1, replica_groups=mesh['gx'=8,'gy'=4] {'gy'}, use_global_device_ids=true, to_apply=%add | all-reduce | flops 520 | bytes 4160
  56.4 28.4 %scatter_fusion = f32[256,16,2,128]{3,1,2,0:T(8,128)} fusion(f32[256,16,2,128]{3,1,2,0:T(8,128)} %broadcast_in_dim.38, s32[256]{0:T(256)S(1)} %bitcast.60, f32[256,16,128]{2,1,0:T(8,128)S(1)} %broadcast_multiply_fusion), kind=kCustom, calls=%fused_computation | custom fusion | flops 524288 | bytes 6293504 | tf_op jit(solution)/shard_map/scatter-add | solution.py:82
  84.8 5.3 %copy.51 = f32[256,16,2,128]{0,3,2,1:T(8,128)} copy(f32[256,16,2,128]{3,1,2,0:T(8,128)} %scatter_fusion) | data formatting | bytes 8388608 | tf_op jit(solution)/shard_map/scatter-add | solution.py:82
  90.1 6.8 %fusion.8 = f32[256,16,256]{0,2,1:T(8,128)S(1)} fusion(f32[256,16,256]{0,2,1:T(8,128)} %copy.50, f32[256,16,1]{0,2,1:T(1,128)S(1)} %collective-permute-done.1, f32[256,16,1]{0,2,1:T(1,128)S(1)} %collective-permute-done, f32[256,16,2,128]{0,3,2,1:T(8,128)} %copy.51), kind=kLoop, calls=%fused_computation.22 | loop fusion | flops 8388608 | bytes 12615680 | tf_op jit(solution)/shard_map/add | solution.py:107
  97.0 4.2 %convolution_bitcast_fusion.1 = f32[256,4096]{1,0:T(8,128)S(1)} fusion(f32[256,4096]{0,1:T(8,128)S(1)} %bitcast.62, f32[256,256]{1,0:T(8,128)S(1)} %copy-done), kind=kOutput, calls=%fused_computation.10 | convolution fusion | flops 3221225472 | bytes 8650752 | tf_op jit(solution)/shard_map/dot_general | solution.py:109
  103.2 14.0 %all-gather.3 = f32[8,1,4096]{2,1,0:T(1,128)S(1)} all-gather(f32[1,1,4096]{2,1,0:T(1,128)S(1)} %slice_bitcast_fusion.1), channel_id=1, replica_groups=mesh['gx'=8,'gy'=4] {'gx'}, dimensions={0}, use_global_device_ids=true | all-gather | bytes 147456 | tf_op jit(solution)/shard_map/all_gather | solution.py:9
  117.3 9.1 %while.56 = (s32[]{:T(128)}, f32[4096]{0:T(1024)S(1)}, s32[]{:T(128)}, f32[8]{0:T(128)S(1)}, f32[8,4096]{1,0:T(8,128)S(1)}, /*index=5*/s32[]{:T(128)}, s32[]{:T(128)}) while((s32[]{:T(128)}, f32[4096]{0:T(1024)S(1)}, s32[]{:T(128)}, f32[8]{0:T(128)S(1)}, f32[8,4096]{1,0:T(8,128)S(1)}, /*index=5*/s32[]{:T(128)}, s32[]{:T(128)}) %tuple.130), condition=%wide.region_2.3_spmd.clone, body=%wide.region_1.2_spmd.clone.sunk | while | flops 16388 | bytes 82037 | solution.py:21
  126.4 6.1 %convolution_bitcast_fusion = f32[256,4096]{1,0:T(8,128)S(1)} fusion(f32[256,256]{1,0:T(8,128)S(1)} %copy-done.7, f32[256,4096]{1,0:T(8,128)} %copy-done.6, f32[4096]{0:T(1024)S(1)} %get-tuple-element.381, f32[256]{0:T(256)S(1)} %copy-done.11), kind=kOutput, calls=%fused_computation.9 | convolution fusion | flops 3223322624 | bytes 8668160 | tf_op jit(solution)/shard_map/dot_general | solution.py:114
  134.5 14.2 %all-gather.4 = f32[8,1,4096]{2,1,0:T(1,128)S(1)} all-gather(f32[1,1,4096]{2,1,0:T(1,128)S(1)} %slice_bitcast_fusion), channel_id=1, replica_groups=mesh['gx'=8,'gy'=4] {'gx'}, dimensions={0}, use_global_device_ids=true | all-gather | bytes 147456 | tf_op jit(solution)/shard_map/all_gather | solution.py:9
  149.3 9.1 %while.57 = (s32[]{:T(128)}, f32[4096]{0:T(1024)S(1)}, s32[]{:T(128)}, f32[8]{0:T(128)S(1)}, f32[8,4096]{1,0:T(8,128)S(1)}, /*index=5*/s32[]{:T(128)}, s32[]{:T(128)}) while((s32[]{:T(128)}, f32[4096]{0:T(1024)S(1)}, s32[]{:T(128)}, f32[8]{0:T(128)S(1)}, f32[8,4096]{1,0:T(8,128)S(1)}, /*index=5*/s32[]{:T(128)}, s32[]{:T(128)}) %tuple.119), condition=%wide.region_4.5_spmd.clone, body=%wide.region_3.4_spmd.clone.sunk | while | flops 16388 | bytes 82037 | solution.py:21
  164.6 3.0 collective-permute-start.3
  168.0 5.6 %copy.59 = f32[256,4096]{0,1:T(8,128)} copy(f32[256,4096]{1,0:T(8,128)} %copy-done.3) | data formatting | bytes 8388608 | tf_op jit(solution)/shard_map/reshape | solution.py:118
  176.3 9.1 %fusion.3 = f32[256,16,256]{0,2,1:T(8,128)} fusion(f32[256,16,256]{0,2,1:T(8,128)} %bitcast.61, f32[1,16,256]{0,2,1:T(8,128)} %copy.54, f32[1,16,256]{0,2,1:T(8,128)S(1)} %copy.53), kind=kLoop, calls=%fused_computation.15 | loop fusion | flops 7340032 | bytes 8421376 | tf_op jit(solution)/shard_map/add | solution.py:122
  185.3 5.5 %copy.58 = f32[256,16,256]{2,1,0:T(8,128)} copy(f32[256,16,256]{0,2,1:T(8,128)} %fusion.3) | data formatting | bytes 8388608 | tf_op jit(solution)/shard_map/add | solution.py:122
  190.8 5.7 %fusion.20 = f32[4096,256]{0,1:T(8,128)S(1)} fusion(f32[4096,256]{1,0:T(8,128)} %bitcast.64, f32[256,256]{1,0:T(8,128)S(1)} %copy-done.8), kind=kOutput, calls=%fused_computation.65 | convolution fusion | flops 3221225472 | bytes 8650752 | tf_op jit(solution)/shard_map/dot_general | solution.py:124
  198.6 8.2 %all-gather.1 = f32[16384,1]{0,1:T(1,128)S(1)} all-gather(f32[4096,1]{0,1:T(1,128)S(1)} %slice.84), channel_id=3, replica_groups=mesh['gx'=8,'gy'=4] {'gy'}, dimensions={0}, use_global_device_ids=true | all-gather | bytes 81920 | tf_op jit(solution)/shard_map/all_gather | solution.py:9
  208.1 3.9 %while.58 = (s32[]{:T(128)}, f32[4096]{0:T(1024)S(1)}, s32[]{:T(128)}, f32[4]{0:T(128)S(1)}, f32[4,4096]{1,0:T(4,128)S(1)}, /*index=5*/s32[]{:T(128)}, s32[]{:T(128)}) while((s32[]{:T(128)}, f32[4096]{0:T(1024)S(1)}, s32[]{:T(128)}, f32[4]{0:T(128)S(1)}, f32[4,4096]{1,0:T(4,128)S(1)}, /*index=5*/s32[]{:T(128)}, s32[]{:T(128)}) %tuple.122), condition=%wide.region_6.7_spmd.clone, body=%wide.region_5.6_spmd.clone.sunk | while | flops 16388 | bytes 82037 | solution.py:21
  212.0 9.0 %fusion.9 = f32[4096,256]{1,0:T(8,128)S(1)} fusion(f32[256,256]{1,0:T(8,128)S(1)} %copy-done.9, f32[4096,256]{0,1:T(8,128)} %copy-done.4, f32[256]{0:T(256)S(1)} %copy-done.13, f32[4096]{0:T(1024)S(1)} %get-tuple-element.383), kind=kOutput, calls=%fused_computation.25 | convolution fusion | flops 3223322624 | bytes 8668160 | tf_op jit(solution)/shard_map/dot_general | solution.py:129
  223.2 72.9 %all-gather.2 = f32[16384,1]{1,0:T(8,128)} all-gather(f32[4096,1]{1,0:T(8,128)S(1)} %slice.85), channel_id=4, replica_groups=mesh['gx'=8,'gy'=4] {'gy'}, dimensions={0}, use_global_device_ids=true | all-gather | bytes 81920 | tf_op jit(solution)/shard_map/all_gather | solution.py:9
  296.2 4.6 %reduce.3 = f32[16384]{0:T(1024)S(1)} reduce(f32[16384,1]{1,0:T(8,128)} %all-gather.2, f32[]{:T(128)} %constant.197), dimensions={1}, to_apply=%all-gather.2.reduce_sub_computation | reduce | bytes 131076 | tf_op jit(solution)/shard_map/all_gather | solution.py:9
  301.6 3.9 %while.59 = (s32[]{:T(128)}, f32[4096]{0:T(1024)S(1)}, s32[]{:T(128)}, f32[4]{0:T(128)S(1)}, f32[4,4096]{1,0:T(4,128)S(1)}, /*index=5*/s32[]{:T(128)}, s32[]{:T(128)}) while((s32[]{:T(128)}, f32[4096]{0:T(1024)S(1)}, s32[]{:T(128)}, f32[4]{0:T(128)S(1)}, f32[4,4096]{1,0:T(4,128)S(1)}, /*index=5*/s32[]{:T(128)}, s32[]{:T(128)}) %tuple.125), condition=%wide.region_8.9_spmd.clone, body=%wide.region_7.8_spmd.clone.sunk | while | flops 16388 | bytes 82037 | solution.py:21
  (156 shorter events, 62.9 us)
Async XLA Ops:
  6.5 90.4 %copy-start = (f32[256,256]{1,0:T(8,128)S(1)}, f32[256,256]{1,0:T(8,128)}, u32[]{:S(2)}) copy-start(f32[256,256]{1,0:T(8,128)} %param.22) | copy-start | bytes 786436
  6.5 45.5 %all-gather.7.cloned.1.call-start = ((), (), s32[]{:S(2)}) async-start(), calls=%async_computation | async-start | bytes 2621440 | tf_op jit(solution)/shard_map/all_gather | solution.py:70
  7.3 7.7 %copy-start.18 = (u32[32]{0:T(128)S(1)}, u32[32]{0:T(128)}, u32[]{:S(2)}) copy-start(u32[32]{0:T(128)} %constant.170) | copy-start | bytes 388
  7.3 8.3 %copy-start.12 = (f32[256]{0:T(256)S(1)}, f32[256]{0:T(256)}, u32[]{:S(2)}) copy-start(f32[256]{0:T(256)} %param.25) | copy-start | bytes 3076
  7.3 9.0 %copy-start.11 = (f32[256]{0:T(256)S(1)}, f32[256]{0:T(256)}, u32[]{:S(2)}) copy-start(f32[256]{0:T(256)} %param.24) | copy-start | bytes 3076
  7.3 31.8 %copy-start.17 = (u32[32]{0:T(128)S(1)}, u32[32]{0:T(128)}, u32[]{:S(2)}) copy-start(u32[32]{0:T(128)} %constant.160) | copy-start | bytes 388
  7.3 33.1 %copy-start.14 = (f32[256]{0:T(256)S(1)}, f32[256]{0:T(256)}, u32[]{:S(2)}) copy-start(f32[256]{0:T(256)} %param.29) | copy-start | bytes 3076
  7.3 33.8 %copy-start.13 = (f32[256]{0:T(256)S(1)}, f32[256]{0:T(256)}, u32[]{:S(2)}) copy-start(f32[256]{0:T(256)} %param.28) | copy-start | bytes 3076
  7.3 34.6 %copy-start.15 = (s32[64,1]{0,1:T(1,128)S(1)}, s32[64,1]{0,1:T(1,128)}, u32[]{:S(2)}) copy-start(s32[64,1]{0,1:T(1,128)} %param.31) | copy-start | bytes 772
  7.3 34.7 %copy-start.16 = (s32[64]{0:T(128)S(1)}, s32[64]{0:T(128)}, u32[]{:S(2)}) copy-start(s32[64]{0:T(128)} %param.32) | copy-start | bytes 772
  13.6 76.5 %collective-permute-start = (f32[256,16,1]{0,2,1:T(1,128)S(1)}, f32[256,16,1]{0,2,1:T(1,128)S(1)}, u32[]{:S(2)}, u32[]{:S(2)}) collective-permute-start(f32[256,16,1]{0,2,1:T(1,128)S(1)} %get-tuple-element.505), channel_id=1, source_target_pairs={{1,0},{2,1},{3,2},{5,4},{6,5},{7,6},{9,8},{10,9},{11,10},{13,12},{... | collective-permute-start | bytes 49160 | tf_op jit(solution)/shard_map/ppermute | solution.py:32
  17.0 73.1 %collective-permute-start.1 = (f32[256,16,1]{0,2,1:T(1,128)S(1)}, f32[256,16,1]{0,2,1:T(1,128)S(1)}, u32[]{:S(2)}, u32[]{:S(2)}) collective-permute-start(f32[256,16,1]{0,2,1:T(1,128)S(1)} %get-tuple-element.506), channel_id=1, source_target_pairs={{0,1},{1,2},{2,3},{4,5},{5,6},{6,7},{8,9},{9,10},{10,11},{12,13},{... | collective-permute-start | bytes 49160 | tf_op jit(solution)/shard_map/ppermute | solution.py:31
  97.0 29.4 %copy-start.7 = (f32[256,256]{1,0:T(8,128)S(1)}, f32[256,256]{1,0:T(8,128)}, u32[]{:S(2)}) copy-start(f32[256,256]{1,0:T(8,128)} %param.23) | copy-start | bytes 786436
  101.2 2.0 copy-start.6
  132.5 2.0 copy-start.5
  158.4 9.2 %copy-start.10 = (s32[256,2]{0,1:T(2,128)S(1)}, s32[256,2]{0,1:T(2,128)}, u32[]{:S(2)}) copy-start(s32[256,2]{0,1:T(2,128)} %param.33) | copy-start | bytes 6148
  161.2 2.0 copy-start.3
  163.3 10.3 %collective-permute-start.2 = (f32[1,16,256]{2,1,0:T(8,128)S(1)}, f32[1,16,256]{2,1,0:T(8,128)S(1)}, u32[]{:S(2)}, u32[]{:S(2)}) collective-permute-start(f32[1,16,256]{2,1,0:T(8,128)S(1)} %slice.67), channel_id=1, source_target_pairs={{4,0},{8,4},{12,8},{16,12},{20,16},{24,20},{28,24},{5,1},{9,5},{13... | collective-permute-start | bytes 49160 | tf_op jit(solution)/shard_map/ppermute | solution.py:32
  164.6 9.7 %collective-permute-start.3 = (f32[1,16,256]{2,1,0:T(8,128)S(1)}, f32[1,16,256]{2,1,0:T(8,128)S(1)}, u32[]{:S(2)}, u32[]{:S(2)}) collective-permute-start(f32[1,16,256]{2,1,0:T(8,128)S(1)} %slice.70), channel_id=1, source_target_pairs={{0,4},{4,8},{8,12},{12,16},{16,20},{20,24},{24,28},{1,5},{5,9},{9,... | collective-permute-start | bytes 49160 | tf_op jit(solution)/shard_map/ppermute | solution.py:31
  185.3 5.5 %copy-start.8 = (f32[256,256]{1,0:T(8,128)S(1)}, f32[256,256]{1,0:T(8,128)}, u32[]{:S(2)}) copy-start(f32[256,256]{1,0:T(8,128)} %param.26) | copy-start | bytes 786436
  190.8 21.2 %copy-start.9 = (f32[256,256]{1,0:T(8,128)S(1)}, f32[256,256]{1,0:T(8,128)}, u32[]{:S(2)}) copy-start(f32[256,256]{1,0:T(8,128)} %param.27) | copy-start | bytes 786436
  196.6 2.0 copy-start.4
  221.1 2.0 copy-start.2
  308.2 2.8 copy-start.1
Sparse Core Ops, SparseCore 0:
  9.2 38.1 all-gather.6
where the time goes:
time: 320 us; the launch traced here: 318 us
  blocking collectives  136 us (42%)
  other arithmetic  72.7 us (23%)
  local copies, waits for them, and re-layouts  57.6 us (18%)
  matrix products  25 us (8%)
  between operations  14.5 us (5%)
  starting transfers between devices  11.1 us (3%)
    all_gather x4, blocking collectives, carried_in(): pieces = jax.tree.map(lambda part: lax.all_gather(part, axis), value)  109 us
    scatter-add x1, other arithmetic, wall_forcing(): accumulated = jnp.zeros((tile_rows, planes, nblock, block_width), jnp.flo...  28.4 us
    unnamed x2, blocking collectives  26.4 us
    unnamed x55, local copies, waits for them, and re-layouts  19.8 us
    dynamic_slice x40, local copies, waits for them, and re-layouts, hop(): longer = join(so_far, jax.tree.map(lambda part: part[position], pieces))  12.7 us
    select_n x20, other arithmetic, hop(): jnp.where(position < mine, new, old)  12.7 us
    add x1, other arithmetic, on_device(): source_term = halfway + 0.5 * (padded[2:] + padded[:-2] - 2.0 * halfway)  9.05 us
    dot_general x1, matrix products, on_device(): jnp.dot(swept, upper_y.T, precision=lax.Precision.HIGHEST, preferred_elem...  9.01 us
  transfers between devices with their start and end apart: 5, of which 0 were waited for; matrix products, arithmetic and copies ran while one was open for 17% of the time, Pallas kernels for 0%

commit v1 on v0

v1 whole, which is shorter than its diff:
```python
import functools

import jax
import jax.numpy as jnp
from jax import lax
from jax.experimental import pallas as pl
from jax.experimental.pallas import tpu as pltpu
from jax.sharding import PartitionSpec as P

F32 = jnp.float32
BF16 = jnp.bfloat16
HIGHEST = lax.Precision.HIGHEST
VMEM = pl.BlockSpec(memory_space=pltpu.VMEM)
SMEM = pl.BlockSpec(memory_space=pltpu.SMEM)
ANY = pl.BlockSpec(memory_space=pl.ANY)


def f32_dot(left, right, dims):
    return lax.dot_general(left, right, (dims, ((), ())), precision=HIGHEST, preferred_element_type=F32)


def split(value):
    high = value.astype(BF16)
    return high, (value - high.astype(F32)).astype(BF16)


def left_of(value, axis):
    high, low = split(value)
    return jnp.concatenate([high, low, high], axis=axis)


def right_of(value, axis):
    high, low = split(value)
    return jnp.concatenate([high, high, low], axis=axis)


def bf16_dot(left, right, dims):
    return lax.dot_general(left, right, (dims, ((), ())), preferred_element_type=F32)


def params(vmem_mib, side_effects=False):
    return pltpu.CompilerParams(vmem_limit_bytes=vmem_mib << 20)


def call(kernel, out_shape, in_specs, vmem_mib, out_specs=None, scratch=(), flops=0, moved=0, **more):
    if out_specs is None:
        out_specs = jax.tree.map(lambda _: VMEM, out_shape)
    return pl.pallas_call(
        kernel,
        out_shape=out_shape,
        in_specs=in_specs,
        out_specs=out_specs,
        scratch_shapes=list(scratch),
        compiler_params=params(vmem_mib),
        cost_estimate=pl.CostEstimate(flops=flops, bytes_accessed=moved, transcendentals=0),
        **more,
    )


def struct(*shape, dtype=F32):
    return jax.ShapeDtypeStruct(shape, dtype)


def pack_kernel(count, room, me_ref, owner_ref, offset_ref, force_ref, *refs):
    outs, places, taken = refs[:count], refs[count], refs[count + 1]
    walls = force_ref.shape[0]
    for shift in range(count):
        outs[shift][...] = jnp.zeros_like(outs[shift])
        taken[shift] = 0
    places[...] = jnp.full_like(places, -1.0)
    lanes = lax.broadcasted_iota(jnp.int32, places.shape[1:], 1)
    rows = lax.broadcasted_iota(jnp.int32, places.shape[1:], 0)

    def step(entry, carry):
        shift = lax.rem(owner_ref[entry] - me_ref[0] + count, count)
        slot = taken[shift]
        taken[shift] = slot + 1
        for s in range(count):

            @pl.when(shift == s)
            def _():
                outs[s][pl.ds(slot, 1)] = force_ref[pl.ds(entry, 1)]

        here = (lanes == slot) & (rows == 0)
        places[pl.ds(shift, 1)] = jnp.where(here, offset_ref[entry].astype(F32), places[shift])[None]
        return carry

    lax.fori_loop(0, walls, step, 0)


def pack(me, owner, offset, force, count, room):
    shape = (room,) + force.shape[1:]
    return call(
        functools.partial(pack_kernel, count, room),
        [struct(*shape) for _ in range(count)] + [struct(count, 8, 256)],
        [SMEM, SMEM, SMEM, VMEM],
        8,
        scratch=[pltpu.SMEM((count,), jnp.int32)],
        moved=2 * force.size * 4,
    )(me, owner, offset, force)


def row(ref, index):
    base = index // 8 * 8
    return ref[base : base + 8, :][index - base : index - base + 1]


def half_shift_lanes(value):
    length = value.shape[1]
    at = lax.broadcasted_iota(jnp.int32, value.shape, 1)
    before = jnp.where(at == 0, 0.0, pltpu.roll(value, 1, 1))
    after = jnp.where(at == length - 1, 0.0, pltpu.roll(value, length - 1, 1))
    return 0.5 * (before + after)


def half_shift_rows(value):
    length = value.shape[0]
    at = lax.broadcasted_iota(jnp.int32, value.shape, 0)
    before = jnp.where(at == 0, 0.0, pltpu.roll(value, 1, 0))
    after = jnp.where(at == length - 1, 0.0, pltpu.roll(value, length - 1, 0))
    return 0.5 * (before + after)


def factor_kernel(lx, ux, lcx, ucx, ly, uy, lcy, ucy, mx, my, aux, xrows, yrows, frows, scal):
    rows_x, rows_y = lx.shape[0], ly.shape[0]
    both = f32_dot(ux[...], lx[...], ((1,), (0,)))
    mx[...] = left_of(half_shift_rows(both), 1)
    both_y = f32_dot(uy[...], ly[...], ((1,), (0,)))
    my[...] = left_of(both_y.T, 0)
    zero = jnp.zeros((1, rows_x), F32)
    lc, uc = lcx[...], ucx[...]
    pad = jnp.zeros((7, rows_x), F32)
    u_lc = f32_dot(jnp.concatenate([lc, pad], 0), ux[...], ((1,), (1,)))[0:1]
    at = lax.broadcasted_iota(jnp.int32, (1, rows_x), 1)
    c0 = half_shift_lanes(u_lc)
    c1 = half_shift_lanes(uc) + jnp.where(at == rows_x - 1, 0.5, 0.0)
    c2 = jnp.where(at == 0, 0.5, 0.0)
    xrows[...] = jnp.concatenate([c0, c1, c2, zero, zero, zero, zero, zero], 0)
    lcv, ucv = lcy[...], ucy[...]
    pad_y = jnp.zeros((7, rows_y), F32)
    uy_lc = f32_dot(jnp.concatenate([lcv, pad_y], 0), uy[...], ((1,), (1,)))[0:1]
    f0 = row(ly, rows_y - 1)
    f1 = both_y[0:8][0:1]
    zero_y = jnp.zeros((1, rows_y), F32)
    turned = both_y.T
    m0, m1 = 0.5 * turned[0:8][0:1], 0.5 * turned[rows_y - 8 : rows_y][7:8]
    yrows[...] = jnp.concatenate([uy_lc, ucv, m0, m1, f0, f1, zero_y, zero_y], 0)
    lane = lax.broadcasted_iota(jnp.int32, (rows_y, 128), 1)
    cols = jnp.concatenate([f0, f1, pad_y[:6]], 0).T
    aux[...] = left_of(jnp.where(lane < 64, cols[:, 0:1], cols[:, 1:2]), 0)
    frows[...] = jnp.concatenate([row(lx, rows_x - 1), both[0:8][0:1], zero, zero, zero, zero, zero, zero], 0)

    def spread(value, index, width):
        return jnp.broadcast_to(value[:, index : index + 1], (1, width))

    last = row(ux, rows_x - 1)
    scal[0:8, :] = jnp.concatenate(
        [
            spread(lc, rows_x - 1, rows_x),
            spread(u_lc, 0, rows_x),
            spread(uc, 0, rows_x),
            spread(last, rows_x - 1, rows_x),
            spread(uc, rows_x - 1, rows_x),
            zero,
            zero,
            zero,
        ],
        0,
    )
    scal[8:16, :] = jnp.concatenate(
        [
            spread(lcv, rows_y - 1, rows_x),
            spread(uy_lc, 0, rows_x),
            spread(ucv, 0, rows_x),
            zero,
            zero,
            zero,
            zero,
            zero,
        ],
        0,
    )


def factors(lx, ux, lcx, ucx, ly, uy, lcy, ucy):
    rows, cols = lx.shape[0], ly.shape[0]
    return call(
        factor_kernel,
        [
            struct(rows, 3 * rows, dtype=BF16),
            struct(3 * cols, cols, dtype=BF16),
            struct(3 * cols, 128, dtype=BF16),
            struct(8, rows),
            struct(8, cols),
            struct(8, rows),
            struct(16, rows),
        ],
        [VMEM] * 8,
        16,
        flops=6 * 4 * rows**3,
        moved=8 * rows * rows * 4,
    )(lx, ux, lcx[None, :], ucx[None, :], ly, uy, lcy[None, :], ucy[None, :])


def explicit_kernel(chunk, func_ref, v_ref, e_ref, edge_ref):
    step = pl.program_id(0)
    planes, cols = v_ref.shape[1:]

    @pl.when(step == 0)
    def _():
        edge_ref[...] = jnp.zeros_like(edge_ref)

    low, high = edge_ref[0], edge_ref[1]
    for i in range(chunk):
        value = half_shift_lanes(v_ref[i])
        for b in range(e_ref.shape[0]):
            e_ref[b, i * planes : (i + 1) * planes, :] = value[:, b * 128 : (b + 1) * 128]
        low = low + func_ref[0, step * chunk + i] * value
        high = high + func_ref[1, step * chunk + i] * value
    edge_ref[0] = low
    edge_ref[1] = high


def explicit(velocity, func):
    rows, planes, cols = velocity.shape
    chunk = 32
    return pl.pallas_call(
        functools.partial(explicit_kernel, chunk),
        grid=(rows // chunk,),
        out_shape=[struct(cols // 128, rows * planes, 128), struct(2, planes, cols)],
        in_specs=[SMEM, pl.BlockSpec((chunk, planes, cols), lambda i: (i, 0, 0))],
        out_specs=[
            pl.BlockSpec((cols // 128, chunk * planes, 128), lambda i: (0, i, 0)),
            pl.BlockSpec((2, planes, cols), lambda i: (0, 0, 0)),
        ],
        compiler_params=params(8),
        cost_estimate=pl.CostEstimate(flops=8 * velocity.size, bytes_accessed=8 * velocity.size, transcendentals=0),
    )(func, velocity)


def x_edge_kernel(count, me_ref, table_ref, func_ref, edge_ref, frows, scal, halo_l, halo_r, *refs):
    payload, out = refs[:count], refs[count]
    planes, cols = edge_ref.shape[1:]
    width = payload[0].shape[2]
    nblock = cols // width
    room = payload[0].shape[0]
    low, high = edge_ref[0], edge_ref[1]
    at = lax.broadcasted_iota(jnp.int32, (planes, cols), 1)
    f0, f1 = frows[0:1, :], frows[1:2, :]
    keep_l = jnp.where(me_ref[0] > 0, 0.5, 0.0)
    keep_r = jnp.where(me_ref[0] < count - 1, 0.5, 0.0)
    hl, hr = halo_l[0:planes, :], halo_r[0:planes, :]
    for f, which in ((f0, 0), (f1, 1)):
        first = keep_l * jnp.sum(hl * f, axis=1, keepdims=True)
        last = keep_r * jnp.sum(hr * f, axis=1, keepdims=True)
        add = jnp.where(at == 0, first, 0.0) + jnp.where(at == cols - 1, last, 0.0)
        if which == 0:
            low = low + add
        else:
            high = high + add
    out[0:planes, :] = low
    out[planes : 2 * planes, :] = high
    out[2 * planes : 2 * planes + 8, :] = scal[0:8, :]
    for s in range(count):

        def step(slot, carry):
            place = table_ref[s * room + slot]

            @pl.when(place >= 0)
            def _():
                line = place // nblock
                lane = pl.ds(pl.multiple_of((place % nblock) * width, width), width)
                value = payload[s][slot]
                out[0:planes, lane] = out[0:planes, lane] + func_ref[0, line] * value
                out[planes : 2 * planes, lane] = out[planes : 2 * planes, lane] + func_ref[1, line] * value

            return carry

        lax.fori_loop(0, room, step, 0)


def x_edges(me, table, func, edge, frows, scal, halo_l, halo_r, payload):
    planes, cols = edge.shape[1:]
    count = len(payload)
    return call(
        functools.partial(x_edge_kernel, count),
        struct(2 * planes + 8, cols),
        [SMEM, SMEM, SMEM] + [VMEM] * (5 + count),
        8,
        moved=sum(p.size for p in payload) * 4,
    )(me, table, func, edge, frows, scal, halo_l, halo_r, *payload)


def sweep_kernel(count, me_ref, table_ref, mx, my, aux, yrows, halo_l, halo_r, e_hbm, *refs):
    payload, (w_ref, s_ref, zh_ref, e_ref, sem) = refs[:count], refs[count:]
    planes = w_ref.shape[0]
    rows = w_ref.shape[1]
    cols = w_ref.shape[2]
    copy = pltpu.make_async_copy(e_hbm, e_ref, sem)
    copy.start()
    width = payload[0].shape[2]
    nblock = cols // width
    room = payload[0].shape[0]
    keep_l = jnp.where(me_ref[0] > 0, 1.0, 0.0)
    keep_r = jnp.where(me_ref[0] < count - 1, 1.0, 0.0)
    halo = jnp.concatenate([keep_l * halo_l[0:planes, :], keep_r * halo_r[0:planes, :]], 0)
    zh = bf16_dot(right_of(halo, 1), mx[...], ((1,), (1,)))
    zh_ref[...] = zh
    copy.wait()
    for s in range(count):

        def step(slot, carry):
            place = table_ref[s * room + slot]

            @pl.when(place >= 0)
            def _():
                half, base = place % nblock, pl.multiple_of((place // nblock) * planes, planes)
                e_ref[half, pl.ds(base, planes), :] = e_ref[half, pl.ds(base, planes), :] + payload[s][slot]

            return carry

        lax.fori_loop(0, room, step, 0)
    lane = lax.broadcasted_iota(jnp.int32, (rows, 128), 1)

    def plane(p, total):
        here = [e_ref[b, pl.ds(p, rows, stride=planes), :] for b in range(nblock)]
        z = bf16_dot(mx[...], right_of(jnp.concatenate(here, 1), 0), ((1,), (0,)))
        zc = right_of(z, 1)
        w_ref[p] = bf16_dot(zc, my[...], ((1,), (0,)))
        t = bf16_dot(zc, aux[...], ((1,), (0,)))
        return jnp.where((lane == p) | (lane == 64 + p), t, total)

    total = lax.fori_loop(0, planes, plane, jnp.zeros((rows, 128), F32))
    turned = total.T
    low, high = turned[0:planes], turned[64 : 64 + planes]
    f0, f1 = yrows[4:5, :], yrows[5:6, :]
    zl, zr = zh[0:planes], zh[planes : 2 * planes]
    s_ref[0:planes, :] = low + 0.5 * (zl * f0[:, 0:1] + zr * f0[:, cols - 1 : cols])
    s_ref[planes : 2 * planes, :] = high + 0.5 * (zl * f1[:, 0:1] + zr * f1[:, cols - 1 : cols])


def sweep(me, table, mx, my, aux, yrows, halo_l, halo_r, e, payload, shape):
    rows, planes, cols = shape
    count = len(payload)
    return call(
        functools.partial(sweep_kernel, count),
        [struct(planes, rows, cols), struct(2 * planes, rows), struct(2 * planes, rows)],
        [SMEM, SMEM] + [VMEM] * 6 + [ANY] + [VMEM] * count,
        24,
        scratch=[pltpu.VMEM(e.shape, F32), pltpu.SemaphoreType.DMA],
        flops=3 * 2 * 2 * e.size * rows,
        moved=2 * e.size * 4,
    )(me, table, mx, my, aux, yrows, halo_l, halo_r, e, *payload)


def chain(parts, count, me, planes, f_in):
    lanes = parts.shape[2]
    zero = jnp.zeros((planes, lanes), F32)
    f, mine_f = zero, zero
    for k in range(count):
        f_in[k] = f
        mine_f = jnp.where(k == me, f, mine_f)
        scal = parts[k, 2 * planes : 2 * planes + 8, :]
        f = parts[k, 0:planes, :] + scal[0:1] * f
    g, mine_g, before = zero, zero, zero
    for k in range(count - 1, -1, -1):
        scal = parts[k, 2 * planes : 2 * planes + 8, :]
        mine_g = jnp.where(k == me, g, mine_g)
        if k + 1 < count:
            before = jnp.where(k + 1 == me, scal[3:4] * f_in[k + 1] + scal[4:5] * g, before)
        g = parts[k, planes : 2 * planes, :] + scal[1:2] * f_in[k] + scal[2:3] * g
    return mine_f, mine_g, before


def gather_parts(me, parts, received):
    count = len(received)
    for shift in range(count):
        parts[pl.ds(lax.rem(me - shift + count, count), 1)] = received[shift][...][None]


def x_join_kernel(count, me_ref, my, xrows, yrows, scal, s_ref, *refs):
    received, (out, moved, parts, f_in) = refs[:count], refs[count:]
    me = me_ref[0]
    planes = s_ref.shape[0] // 2
    gather_parts(me, parts, received)
    in_f, in_b, before = chain(parts, count, me, planes, f_in)
    low, high = s_ref[0:planes, :], s_ref[planes : 2 * planes, :]
    f0, f1 = yrows[4:5, :], yrows[5:6, :]
    for index, value in enumerate((in_f, in_b, before)):
        c = xrows[index : index + 1, :]
        low = low + jnp.sum(value * f0, axis=1, keepdims=True) * c
        high = high + jnp.sum(value * f1, axis=1, keepdims=True) * c
    out[0:planes, :] = low
    out[planes : 2 * planes, :] = high
    out[2 * planes : 2 * planes + 8, :] = scal[8:16, :]
    moved[...] = bf16_dot(right_of(jnp.concatenate([in_f, in_b, before], 0), 1), my[...], ((1,), (0,)))


def x_join(me, my, xrows, yrows, scal, s, received):
    count = len(received)
    height, cols = received[0].shape
    planes, rows = s.shape[0] // 2, s.shape[1]
    return call(
        functools.partial(x_join_kernel, count),
        [struct(2 * planes + 8, rows), struct(3 * planes, cols)],
        [SMEM] + [VMEM] * (5 + count),
        8,
        scratch=[pltpu.VMEM((count, height, cols), F32), pltpu.VMEM((count, planes, cols), F32)],
        moved=count * height * cols * 4,
    )(me, my, xrows, yrows, scal, s, *received)


def finish_kernel(count, part, me_ref, xrows, yrows, moved, solid, zh_ref, w_hbm, *refs):
    received, (out_hbm, parts, f_in, both, w_ref, out_ref, w_sem, out_sem) = refs[:count], refs[count:]
    me = me_ref[0]
    planes, rows, cols = w_ref.shape
    halves = out_ref.shape[0]

    def w_copy(k):
        span = pl.ds(k * part, part)
        return pltpu.make_async_copy(w_hbm.at[:, span, :], w_ref.at[:, span, :], w_sem.at[k])

    def out_copy(k, b):
        span = pl.ds(k * part * planes, part * planes)
        return pltpu.make_async_copy(out_ref.at[b, span, :], out_hbm.at[span, pl.ds(b * 128, 128)], out_sem.at[k, b])

    steps = rows // part
    for k in range(steps):
        w_copy(k).start()
    gather_parts(me, parts, received)
    in_f, in_b, _ = chain(parts, count, me, planes, f_in)
    both[0] = in_f
    both[1] = in_b
    y = yrows[0:4, :]
    width = cols // solid.shape[1]
    for k in range(steps):
        lo = k * part
        c = xrows[0:3, lo : lo + part]
        fluid = [jnp.broadcast_to(solid[lo : lo + part, b * 128 // width : b * 128 // width + 1] == 0, (part, 128)) for b in range(halves)]
        w_copy(k).wait()
        for p in range(planes):
            left = jnp.concatenate(
                [
                    c,
                    both[0, p : p + 1, lo : lo + part],
                    both[1, p : p + 1, lo : lo + part],
                    zh_ref[p : p + 1, lo : lo + part],
                    zh_ref[planes + p : planes + p + 1, lo : lo + part],
                    jnp.zeros((1, part), F32),
                ],
                0,
            )
            right = jnp.concatenate(
                [
                    moved[p : p + 1, :],
                    moved[planes + p : planes + p + 1, :],
                    moved[2 * planes + p : 2 * planes + p + 1, :],
                    y,
                    jnp.zeros((1, cols), F32),
                ],
                0,
            )
            lh = left.astype(BF16).astype(F32)
            rh = right.astype(BF16).astype(F32)
            lc = jnp.concatenate([lh, lh, left - lh], 0).astype(BF16)
            rc = jnp.concatenate([rh, right - rh, rh], 0).astype(BF16)
            value = w_ref[p, lo : lo + part, :] + bf16_dot(lc, rc, ((0,), (0,)))
            for b in range(halves):
                out_ref[b, pl.ds(lo * planes + p, part, stride=planes), :] = jnp.where(
                    fluid[b], value[:, b * 128 : (b + 1) * 128], 0.0
                )
        for b in range(halves):
            out_copy(k, b).start()
    for k in range(steps):
        for b in range(halves):
            out_copy(k, b).wait()


def finish(me, xrows, yrows, moved, solid, zh, w, received):
    count = len(received)
    height = received[0].shape[0]
    planes, rows, cols = w.shape
    part, halves = 128, cols // 128
    out = call(
        functools.partial(finish_kernel, count, part),
        struct(rows * planes, cols),
        [SMEM] + [VMEM] * 5 + [ANY] + [VMEM] * count,
        20,
        out_specs=ANY,
        scratch=[
            pltpu.VMEM((count, height, rows), F32),
            pltpu.VMEM((count, planes, rows), F32),
            pltpu.VMEM((2, planes, rows), F32),
            pltpu.VMEM((planes, rows, cols), F32),
            pltpu.VMEM((halves, rows * planes, 128), F32),
            pltpu.SemaphoreType.DMA((rows // part,)),
            pltpu.SemaphoreType.DMA((rows // part, halves)),
        ],
        flops=2 * 24 * w.size,
        moved=8 * w.size,
    )(me, xrows, yrows, moved, solid, zh, w, *received)
    return out.reshape(rows, planes, cols)


def rotate(value, axis, shift):
    count = lax.axis_size(axis)
    return lax.ppermute(value, axis, [(i, (i + shift) % count) for i in range(count)])


def on_device(
    velocity,
    lower_x,
    upper_x,
    lower_carry_x,
    upper_carry_x,
    lower_y,
    upper_y,
    lower_carry_y,
    upper_carry_y,
    wall_force,
    wall_owner,
    wall_offset,
    solid_mask,
):
    rows, planes, cols = velocity.shape
    walls = wall_force.shape[0]
    n_x, n_y = lax.axis_size("gx"), lax.axis_size("gy")
    me_x = lax.axis_index("gx").astype(jnp.int32).reshape(1)
    me_y = lax.axis_index("gy").astype(jnp.int32).reshape(1)
    room = 2 * walls // n_y
    *packed, places = pack(me_y, wall_owner[:, 0], wall_offset, wall_force, n_y, room)
    payload = [packed[0]] + [rotate(packed[s], "gy", s) for s in range(1, n_y)]
    first, last = velocity[:, :, 0].T, velocity[:, :, cols - 1].T
    edge_of = {1: last, n_y - 1: first}
    side = [None] + [
        rotate(jnp.concatenate([edge_of.get(s, jnp.zeros_like(first)), places[s]], 0), "gy", s) for s in range(1, n_y)
    ]
    table = jnp.concatenate([places[0, 0, :room]] + [side[s][planes, :room] for s in range(1, n_y)]).astype(jnp.int32)
    halo_l, halo_r = side[1], side[n_y - 1]
    mx, my, aux, xrows, yrows, frows, scal = factors(
        lower_x, upper_x, lower_carry_x, upper_carry_x, lower_y, upper_y, lower_carry_y, upper_carry_y
    )
    func = frows[0:2]
    e, edge = explicit(velocity, func)
    mine = x_edges(me_y, table, func, edge, frows, scal, halo_l, halo_r, payload)
    received = [mine] + [rotate(mine, "gx", s) for s in range(1, n_x)]
    w, s_edge, zh = sweep(me_y, table, mx, my, aux, yrows, halo_l, halo_r, e, payload, velocity.shape)
    mine, moved = x_join(me_x, my, xrows, yrows, scal, s_edge, received)
    received = [mine] + [rotate(mine, "gy", s) for s in range(1, n_y)]
    return finish(me_y, xrows, yrows, moved, solid_mask, zh, w, received)


def solution(mesh):
    placed = (
        P("gx", None, "gy"),
        P("gx", None),
        P("gx", None),
        P("gx"),
        P("gx"),
        P("gy", None),
        P("gy", None),
        P("gy"),
        P("gy"),
        P(("gx", "gy"), None, None),
        P(("gx", "gy"), None),
        P(("gx", "gy")),
        P("gx", "gy"),
    )
    return jax.shard_map(
        on_device, mesh=mesh, in_specs=placed, out_specs=P("gx", None, "gy"), check_vma=False
    )
```

time: 320 us -> 85.7 us (0.27)
  blocking collectives: 136 us -> 0 us
  other arithmetic: 72.7 us -> 0.09 us
  local copies, waits for them, and re-layouts: 57.6 us -> 23.9 us
  Pallas kernels: 0 us -> 31.9 us
  matrix products: 25 us -> 0 us
  between operations: 14.5 us -> 0.23 us
  starting transfers between devices: 11.1 us -> 21.4 us
  waiting for transfers between devices: 0.74 us -> 7.83 us
    all_gather x4 -> x0, blocking collectives: 109 us -> none  [carried_in(): pieces = jax.tree.map(lambda part: lax.all_gather(part, axis), value)]
    pallas_call x0 -> x7, Pallas kernels: none -> 31.9 us  [the longest x1 16.5 us: sweep(): call(functools.partial(sweep_kernel, count), [struct(planes, rows, cols),...]
    scatter-add x1 -> x0, other arithmetic: 28.4 us -> none  [wall_forcing(): accumulated = jnp.zeros((tile_rows, planes, nblock, block_width), jnp.flo...]
    unnamed x2 -> x0, blocking collectives: 26.4 us -> none
    dot_general x4 -> x0, matrix products: 25 us -> none  [the longest x1 9.01 us: on_device(): jnp.dot(swept, upper_y.T, precision=lax.Precision.HIGHEST, preferred_elem...]
    add x4 -> x0, other arithmetic: 21.2 us -> none  [the longest x1 9.05 us: on_device(): source_term = halfway + 0.5 * (padded[2:] + padded[:-2] - 2.0 * halfway)]
    select_n x22 -> x0, other arithmetic: 15.5 us -> none  [the longest x20 12.7 us: hop(): jnp.where(position < mine, new, old)]
    dynamic_slice x40 -> x0, local copies, waits for them, and re-layouts: 12.7 us -> none  [hop(): longer = join(so_far, jax.tree.map(lambda part: part[position], pieces))]
  transfers between devices with their start and end apart: 5 -> 16, of which waited for: 0 -> 4; matrix products, arithmetic and copies ran while one was open for 17% -> 3% of each run, Pallas kernels for 0% -> 25%
where the time goes in v1:
time: 85.7 us; the launch traced here: 85.3 us
  Pallas kernels  31.9 us (37%)
  local copies, waits for them, and re-layouts  23.9 us (28%)
  starting transfers between devices  21.4 us (25%)
  waiting for transfers between devices  7.83 us (9%)
    ppermute x16, starting transfers between devices, rotate(): lax.ppermute(value, axis, [(i, (i + shift) % count) for i in range(count)])  21.4 us
    unnamed x41, local copies, waits for them, and re-layouts  19 us
    pallas_call x1, Pallas kernels, sweep(): call(functools.partial(sweep_kernel, count), [struct(planes, rows, cols),...  16.5 us
    ppermute x16, waiting for transfers between devices, rotate(): lax.ppermute(value, axis, [(i, (i + shift) % count) for i in range(count)])  7.83 us
    slice x1, local copies, waits for them, and re-layouts, on_device(): first, last = (velocity[:, :, 0].T, velocity[:, :, cols - 1].T)  4.9 us
    pallas_call x1, Pallas kernels, x_edges(): call(functools.partial(x_edge_kernel, count), struct(2 * planes + 8, cols...  3.82 us
    pallas_call x1, Pallas kernels, finish(): call(functools.partial(finish_kernel, count, part), struct(rows * planes,...  3.76 us
    pallas_call x1, Pallas kernels, explicit(): pl.pallas_call(functools.partial(explicit_kernel, chunk), grid=(rows // c...  3.68 us
  transfers between devices with their start and end apart: 16, of which 4 were waited for; matrix products, arithmetic and copies ran while one was open for 3% of the time, Pallas kernels for 25%

profile of v1, /device:TPU:0, one launch (start us, length us, event | category | flops | bytes accessed | tf_op | source)
XLA Modules:
  0.0 85.3 jit_solution(6264637786058491718)
XLA Ops:
  2.4 2.8 %shard_map.128 = (f32[32,16,128]{2,1,0:T(8,128)S(1)}, f32[32,16,128]{2,1,0:T(8,128)S(1)}, f32[32,16,128]{2,1,0:T(8,128)S(1)}, f32[32,16,128]{2,1,0:T(8,128)S(1)}, f32[4,8,256]{2,1,0:T(8,128)S(1)}) custom-call(s32[1]{0:T(128)} %bitcast.me_ref, s32[64]{0:T(128)S(1)} %bitcast.28, s32[64]{0:T(128)S(1)} %copy-done.5, f32[64,16,128]{2,1,0:T(8,128)S(1)} %copy-done.3), custom_call_target="tpu_custom_call" | custom-call | bytes 1048576 | tf_op jit(solution)/shard_map/pallas_call | solution.py:93
  5.2 4.9 %fusion = (f32[256,16,1]{2,1,0:T(8,128)}, f32[256,16,1]{2,1,0:T(8,128)}) fusion(f32[256,16,256]{2,1,0:T(8,128)} %v_ref.1), kind=kLoop, calls=%fused_computation.10 | loop fusion | bytes 65536 | tf_op jit(solution)/shard_map/slice | solution.py:533
  10.2 2.6 %copy.18 = f32[256,16,1]{0,1,2:T(8,128)S(1)} copy(f32[256,16,1]{2,1,0:T(8,128)} %get-tuple-element.44) | data formatting | bytes 32768
  12.8 3.9 %collective-permute-start.2 = (f32[24,256]{1,0:T(8,128)S(1)}, f32[24,256]{1,0:T(8,128)S(1)}, u32[]{:S(2)}, u32[]{:S(2)}) collective-permute-start(f32[24,256]{1,0:T(8,128)S(1)} %pad_maximum_fusion.1), channel_id=1, source_target_pairs={{0,3},{1,0},{2,1},{3,2},{4,7},{5,4},{6,5},{7,6},{8,11},{9,8},{10,9... | collective-permute-start | bytes 73736 | tf_op jit(solution)/shard_map/ppermute | solution.py:507
  17.2 2.5 %copy.17 = f32[256,16,1]{0,1,2:T(8,128)S(1)} copy(f32[256,16,1]{2,1,0:T(8,128)} %get-tuple-element.43) | data formatting | bytes 32768
  20.3 2.4 %collective-permute-start.3 = (f32[32,16,128]{2,1,0:T(8,128)S(1)}, f32[32,16,128]{2,1,0:T(8,128)S(1)}, u32[]{:S(2)}, u32[]{:S(2)}) collective-permute-start(f32[32,16,128]{2,1,0:T(8,128)S(1)} %get-tuple-element.34), channel_id=1, source_target_pairs={{0,1},{1,2},{2,3},{3,0},{4,5},{5,6},{6,7},{7,4},{8,9},{9,10},{10,1... | collective-permute-start | bytes 786440 | tf_op jit(solution)/shard_map/ppermute | solution.py:507
  25.1 2.2 %copy-done = f32[256,16,256]{2,1,0:T(8,128)S(1)} copy-done((f32[256,16,256]{2,1,0:T(8,128)S(1)}, f32[256,16,256]{2,1,0:T(8,128)}, u32[]{:S(2)}) %copy-start) | copy-done | bytes 4194328
  27.3 3.7 %shard_map.129 = (f32[2,4096,128]{2,1,0:T(8,128)S(1)}, f32[2,16,256]{2,1,0:T(8,128)S(1)}) custom-call(f32[2,256]{1,0:T(2,128)S(1)} %slice.39.func_ref, f32[256,16,256]{2,1,0:T(8,128)S(1)} %copy-done), custom_call_target="tpu_custom_call" | custom-call | flops 8388608 | bytes 8388608 | tf_op jit(solution)/shard_map/pallas_call | solution.py:227
  31.0 2.0 %copy-done.6 = f32[2,4096,128]{2,1,0:T(8,128)} copy-done((f32[2,4096,128]{2,1,0:T(8,128)}, f32[2,4096,128]{2,1,0:T(8,128)S(1)}, u32[]{:S(2)}) %copy-start.6) | copy-done | bytes 4194328
  34.3 5.4 %collective-permute-done.5.refs_3_ = f32[32,16,128]{2,1,0:T(8,128)S(1)} collective-permute-done((f32[32,16,128]{2,1,0:T(8,128)S(1)}, f32[32,16,128]{2,1,0:T(8,128)S(1)}, u32[]{:S(2)}, u32[]{:S(2)}) %collective-permute-start.5) | collective-permute-done | bytes 262176 | tf_op jit(solution)/shard_map/ppermute | solution.py:507
  39.7 3.8 %shard_map.131.refs_0_ = f32[40,256]{1,0:T(8,128)S(1)} custom-call(s32[1]{0:T(128)} %bitcast.me_ref, s32[128]{0:T(128)S(1)} %maximum_convert_fusion.table_ref, f32[2,256]{1,0:T(2,128)S(1)} %slice.39.func_ref, f32[2,16,256]{2,1,0:T(8,128)S(1)} %get-tuple-element.38.edge_ref, f32[8,256]{1,0:T(8,128)S(1)} %get-tuple-element.31.frows, ...), custom_call_target="tpu_custom_call" | custom-call | bytes 1048576 | tf_op jit(solution)/shard_map/pallas_call | solution.py:285
  43.6 1.6 %collective-permute-start.7 = (f32[40,256]{1,0:T(8,128)S(1)}, f32[40,256]{1,0:T(8,128)S(1)}, u32[]{:S(2)}, u32[]{:S(2)}) collective-permute-start(f32[40,256]{1,0:T(8,128)S(1)} %shard_map.131.refs_0_), channel_id=1, source_target_pairs={{0,8},{4,12},{8,16},{12,20},{16,24},{20,28},{24,0},{28,4},{1,9},{5... | collective-permute-start | bytes 122888 | tf_op jit(solution)/shard_map/ppermute | solution.py:507
  45.1 2.6 %collective-permute-start.8 = (f32[40,256]{1,0:T(8,128)S(1)}, f32[40,256]{1,0:T(8,128)S(1)}, u32[]{:S(2)}, u32[]{:S(2)}) collective-permute-start(f32[40,256]{1,0:T(8,128)S(1)} %shard_map.131.refs_0_), channel_id=1, source_target_pairs={{0,12},{4,16},{8,20},{12,24},{16,28},{20,0},{24,4},{28,8},{1,13},{... | collective-permute-start | bytes 122888 | tf_op jit(solution)/shard_map/ppermute | solution.py:507
  47.7 1.2 %collective-permute-start.9 = (f32[40,256]{1,0:T(8,128)S(1)}, f32[40,256]{1,0:T(8,128)S(1)}, u32[]{:S(2)}, u32[]{:S(2)}) collective-permute-start(f32[40,256]{1,0:T(8,128)S(1)} %shard_map.131.refs_0_), channel_id=1, source_target_pairs={{0,16},{4,20},{8,24},{12,28},{16,0},{20,4},{24,8},{28,12},{1,17},{... | collective-permute-start | bytes 122888 | tf_op jit(solution)/shard_map/ppermute | solution.py:507
  48.9 1.2 %collective-permute-start.10 = (f32[40,256]{1,0:T(8,128)S(1)}, f32[40,256]{1,0:T(8,128)S(1)}, u32[]{:S(2)}, u32[]{:S(2)}) collective-permute-start(f32[40,256]{1,0:T(8,128)S(1)} %shard_map.131.refs_0_), channel_id=1, source_target_pairs={{0,20},{4,24},{8,28},{12,0},{16,4},{20,8},{24,12},{28,16},{1,21},{... | collective-permute-start | bytes 122888 | tf_op jit(solution)/shard_map/ppermute | solution.py:507
  50.1 1.3 %collective-permute-start.11 = (f32[40,256]{1,0:T(8,128)S(1)}, f32[40,256]{1,0:T(8,128)S(1)}, u32[]{:S(2)}, u32[]{:S(2)}) collective-permute-start(f32[40,256]{1,0:T(8,128)S(1)} %shard_map.131.refs_0_), channel_id=1, source_target_pairs={{0,24},{4,28},{8,0},{12,4},{16,8},{20,12},{24,16},{28,20},{1,25},{... | collective-permute-start | bytes 122888 | tf_op jit(solution)/shard_map/ppermute | solution.py:507
  51.5 1.4 %collective-permute-start.12 = (f32[40,256]{1,0:T(8,128)S(1)}, f32[40,256]{1,0:T(8,128)S(1)}, u32[]{:S(2)}, u32[]{:S(2)}) collective-permute-start(f32[40,256]{1,0:T(8,128)S(1)} %shard_map.131.refs_0_), channel_id=1, source_target_pairs={{0,28},{4,0},{8,4},{12,8},{16,12},{20,16},{24,20},{28,24},{1,29},{... | collective-permute-start | bytes 122888 | tf_op jit(solution)/shard_map/ppermute | solution.py:507
  52.9 2.2 %copy-done.7 = f32[2,4096,128]{2,1,0:T(8,128)S(1)} copy-done((f32[2,4096,128]{2,1,0:T(8,128)S(1)}, f32[2,4096,128]{2,1,0:T(8,128)}, u32[]{:S(2)}) %copy-start.7) | copy-done | bytes 4194328
  55.1 16.5 %shard_map.130 = (f32[16,256,256]{2,1,0:T(8,128)S(1)}, f32[32,256]{1,0:T(8,128)S(1)}, f32[32,256]{1,0:T(8,128)S(1)}) custom-call(s32[1]{0:T(128)} %bitcast.me_ref, s32[128]{0:T(128)S(1)} %maximum_convert_fusion.table_ref, bf16[256,768]{1,0:T(8,128)(2,1)S(1)} %copy-done.17, bf16[768,256]{1,0:T(8,128)(2,1)S(1)} %get-tuple-element.26.my, ...), custom_call_target="tpu_custom_call" | custom-call | flops 3221225472 | bytes 8388608 | tf_op jit(solution)/shard_map/pallas_call | solution.py:345
  71.6 2.0 %copy-done.1 = f32[16,256,256]{2,1,0:T(8,128)} copy-done((f32[16,256,256]{2,1,0:T(8,128)}, f32[16,256,256]{2,1,0:T(8,128)S(1)}, u32[]{:S(2)}) %copy-start.1) | copy-done | bytes 4194328
  75.1 1.9 %collective-permute-start.15 = (f32[40,256]{1,0:T(8,128)S(1)}, f32[40,256]{1,0:T(8,128)S(1)}, u32[]{:S(2)}, u32[]{:S(2)}) collective-permute-start(f32[40,256]{1,0:T(8,128)S(1)} %get-tuple-element.42.refs_0_), channel_id=1, source_target_pairs={{0,3},{1,0},{2,1},{3,2},{4,7},{5,4},{6,5},{7,6},{8,11},{9,8},{10,9... | collective-permute-start | bytes 122888 | tf_op jit(solution)/shard_map/ppermute | solution.py:507
  77.1 1.7 %collective-permute-done.13.refs_1_ = f32[40,256]{1,0:T(8,128)S(1)} collective-permute-done((f32[40,256]{1,0:T(8,128)S(1)}, f32[40,256]{1,0:T(8,128)S(1)}, u32[]{:S(2)}, u32[]{:S(2)}) %collective-permute-start.13) | collective-permute-done | bytes 40992 | tf_op jit(solution)/shard_map/ppermute | solution.py:507
  79.4 2.2 %copy-done.2 = f32[16,256,256]{2,1,0:T(8,128)S(1)} copy-done((f32[16,256,256]{2,1,0:T(8,128)S(1)}, f32[16,256,256]{2,1,0:T(8,128)}, u32[]{:S(2)}) %copy-start.2) | copy-done | bytes 4194328
  81.6 3.8 %shard_map.133 = f32[4096,256]{1,0:T(8,128)} custom-call(s32[1]{0:T(128)} %bitcast.me_ref, f32[8,256]{1,0:T(8,128)S(1)} %get-tuple-element.24.xrows, f32[8,256]{1,0:T(8,128)S(1)} %get-tuple-element.25.yrows, f32[48,256]{1,0:T(8,128)S(1)} %get-tuple-element.39.moved, s32[256,2]{1,0:T(8,128)S(1)} %copy.16.solid, f32[32,256]{1,0:T(8,128)S(1)} %get-tuple-element.40.zh_ref, ...), custom_call_target="tpu_custom_call" | custom-call | flops 50331648 | bytes 8388608 | tf_op jit(solution)/shard_map/pallas_call | solution.py:484
  (67 shorter events, 9.4 us)
Async XLA Ops:
  10.1 13.1 %copy-start.9 = (f32[256,256]{1,0:T(8,128)S(1)}, f32[256,256]{1,0:T(8,128)}, u32[]{:S(2)}) copy-start(f32[256,256]{1,0:T(8,128)} %ux.1) | copy-start | bytes 786436
  10.1 13.1 %copy-start.10 = (f32[256,256]{1,0:T(8,128)S(1)}, f32[256,256]{1,0:T(8,128)}, u32[]{:S(2)}) copy-start(f32[256,256]{1,0:T(8,128)} %ly.1) | copy-start | bytes 786436
  10.1 13.1 %copy-start.11 = (f32[256,256]{1,0:T(8,128)S(1)}, f32[256,256]{1,0:T(8,128)}, u32[]{:S(2)}) copy-start(f32[256,256]{1,0:T(8,128)} %uy.1) | copy-start | bytes 786436
  10.1 13.1 %copy-start.12 = (f32[256]{0:T(256)S(1)}, f32[256]{0:T(256)}, u32[]{:S(2)}) copy-start(f32[256]{0:T(256)} %param.16) | copy-start | bytes 3076
  10.1 13.1 %copy-start.13 = (f32[256]{0:T(256)S(1)}, f32[256]{0:T(256)}, u32[]{:S(2)}) copy-start(f32[256]{0:T(256)} %param.17) | copy-start | bytes 3076
  10.1 13.1 %copy-start.14 = (f32[256]{0:T(256)S(1)}, f32[256]{0:T(256)}, u32[]{:S(2)}) copy-start(f32[256]{0:T(256)} %param.20) | copy-start | bytes 3076
  12.8 20.3 %collective-permute-start.2 = (f32[24,256]{1,0:T(8,128)S(1)}, f32[24,256]{1,0:T(8,128)S(1)}, u32[]{:S(2)}, u32[]{:S(2)}) collective-permute-start(f32[24,256]{1,0:T(8,128)S(1)} %pad_maximum_fusion.1), channel_id=1, source_target_pairs={{0,3},{1,0},{2,1},{3,2},{4,7},{5,4},{6,5},{7,6},{8,11},{9,8},{10,9... | collective-permute-start | bytes 73736 | tf_op jit(solution)/shard_map/ppermute | solution.py:507
  16.6 17.4 %collective-permute-start.1 = (f32[24,256]{1,0:T(8,128)S(1)}, f32[24,256]{1,0:T(8,128)S(1)}, u32[]{:S(2)}, u32[]{:S(2)}) collective-permute-start(f32[24,256]{1,0:T(8,128)S(1)} %concatenate.13), channel_id=1, source_target_pairs={{0,2},{1,3},{2,0},{3,1},{4,6},{5,7},{6,4},{7,5},{8,10},{9,11},{10,... | collective-permute-start | bytes 73736 | tf_op jit(solution)/shard_map/ppermute | solution.py:507
  19.7 14.4 %collective-permute-start = (f32[24,256]{1,0:T(8,128)S(1)}, f32[24,256]{1,0:T(8,128)S(1)}, u32[]{:S(2)}, u32[]{:S(2)}) collective-permute-start(f32[24,256]{1,0:T(8,128)S(1)} %pad_maximum_fusion), channel_id=1, source_target_pairs={{0,1},{1,2},{2,3},{3,0},{4,5},{5,6},{6,7},{7,4},{8,9},{9,10},{10,1... | collective-permute-start | bytes 73736 | tf_op jit(solution)/shard_map/ppermute | solution.py:507
  20.3 13.9 %collective-permute-start.3 = (f32[32,16,128]{2,1,0:T(8,128)S(1)}, f32[32,16,128]{2,1,0:T(8,128)S(1)}, u32[]{:S(2)}, u32[]{:S(2)}) collective-permute-start(f32[32,16,128]{2,1,0:T(8,128)S(1)} %get-tuple-element.34), channel_id=1, source_target_pairs={{0,1},{1,2},{2,3},{3,0},{4,5},{5,6},{6,7},{7,4},{8,9},{9,10},{10,1... | collective-permute-start | bytes 786440 | tf_op jit(solution)/shard_map/ppermute | solution.py:507
  22.7 11.6 %collective-permute-start.4 = (f32[32,16,128]{2,1,0:T(8,128)S(1)}, f32[32,16,128]{2,1,0:T(8,128)S(1)}, u32[]{:S(2)}, u32[]{:S(2)}) collective-permute-start(f32[32,16,128]{2,1,0:T(8,128)S(1)} %get-tuple-element.35), channel_id=1, source_target_pairs={{0,2},{1,3},{2,0},{3,1},{4,6},{5,7},{6,4},{7,5},{8,10},{9,11},{10,... | collective-permute-start | bytes 786440 | tf_op jit(solution)/shard_map/ppermute | solution.py:507
  27.3 25.6 %copy-start.17 = (bf16[256,768]{1,0:T(8,128)(2,1)S(1)}, bf16[256,768]{1,0:T(8,128)(2,1)}, u32[]{:S(2)}) copy-start(bf16[256,768]{1,0:T(8,128)(2,1)} %copy-done.16) | copy-start | bytes 1179652
  33.0 6.6 %collective-permute-start.5 = (f32[32,16,128]{2,1,0:T(8,128)S(1)}, f32[32,16,128]{2,1,0:T(8,128)S(1)}, u32[]{:S(2)}, u32[]{:S(2)}) collective-permute-start(f32[32,16,128]{2,1,0:T(8,128)S(1)} %get-tuple-element.36), channel_id=1, source_target_pairs={{0,3},{1,0},{2,1},{3,2},{4,7},{5,4},{6,5},{7,6},{8,11},{9,8},{10,9... | collective-permute-start | bytes 786440 | tf_op jit(solution)/shard_map/ppermute | solution.py:507
  43.5 6.6 %collective-permute-start.6 = (f32[40,256]{1,0:T(8,128)S(1)}, f32[40,256]{1,0:T(8,128)S(1)}, u32[]{:S(2)}, u32[]{:S(2)}) collective-permute-start(f32[40,256]{1,0:T(8,128)S(1)} %shard_map.131.refs_0_), channel_id=1, source_target_pairs={{0,4},{4,8},{8,12},{12,16},{16,20},{20,24},{24,28},{28,0},{1,5},{5... | collective-permute-start | bytes 122888 | tf_op jit(solution)/shard_map/ppermute | solution.py:507
  43.6 7.9 %collective-permute-start.7 = (f32[40,256]{1,0:T(8,128)S(1)}, f32[40,256]{1,0:T(8,128)S(1)}, u32[]{:S(2)}, u32[]{:S(2)}) collective-permute-start(f32[40,256]{1,0:T(8,128)S(1)} %shard_map.131.refs_0_), channel_id=1, source_target_pairs={{0,8},{4,12},{8,16},{12,20},{16,24},{20,28},{24,0},{28,4},{1,9},{5... | collective-permute-start | bytes 122888 | tf_op jit(solution)/shard_map/ppermute | solution.py:507
  45.1 28.4 %collective-permute-start.8 = (f32[40,256]{1,0:T(8,128)S(1)}, f32[40,256]{1,0:T(8,128)S(1)}, u32[]{:S(2)}, u32[]{:S(2)}) collective-permute-start(f32[40,256]{1,0:T(8,128)S(1)} %shard_map.131.refs_0_), channel_id=1, source_target_pairs={{0,12},{4,16},{8,20},{12,24},{16,28},{20,0},{24,4},{28,8},{1,13},{... | collective-permute-start | bytes 122888 | tf_op jit(solution)/shard_map/ppermute | solution.py:507
  47.7 25.9 %collective-permute-start.9 = (f32[40,256]{1,0:T(8,128)S(1)}, f32[40,256]{1,0:T(8,128)S(1)}, u32[]{:S(2)}, u32[]{:S(2)}) collective-permute-start(f32[40,256]{1,0:T(8,128)S(1)} %shard_map.131.refs_0_), channel_id=1, source_target_pairs={{0,16},{4,20},{8,24},{12,28},{16,0},{20,4},{24,8},{28,12},{1,17},{... | collective-permute-start | bytes 122888 | tf_op jit(solution)/shard_map/ppermute | solution.py:507
  48.9 24.7 %collective-permute-start.10 = (f32[40,256]{1,0:T(8,128)S(1)}, f32[40,256]{1,0:T(8,128)S(1)}, u32[]{:S(2)}, u32[]{:S(2)}) collective-permute-start(f32[40,256]{1,0:T(8,128)S(1)} %shard_map.131.refs_0_), channel_id=1, source_target_pairs={{0,20},{4,24},{8,28},{12,0},{16,4},{20,8},{24,12},{28,16},{1,21},{... | collective-permute-start | bytes 122888 | tf_op jit(solution)/shard_map/ppermute | solution.py:507
  50.1 23.5 %collective-permute-start.11 = (f32[40,256]{1,0:T(8,128)S(1)}, f32[40,256]{1,0:T(8,128)S(1)}, u32[]{:S(2)}, u32[]{:S(2)}) collective-permute-start(f32[40,256]{1,0:T(8,128)S(1)} %shard_map.131.refs_0_), channel_id=1, source_target_pairs={{0,24},{4,28},{8,0},{12,4},{16,8},{20,12},{24,16},{28,20},{1,25},{... | collective-permute-start | bytes 122888 | tf_op jit(solution)/shard_map/ppermute | solution.py:507
  51.5 22.1 %collective-permute-start.12 = (f32[40,256]{1,0:T(8,128)S(1)}, f32[40,256]{1,0:T(8,128)S(1)}, u32[]{:S(2)}, u32[]{:S(2)}) collective-permute-start(f32[40,256]{1,0:T(8,128)S(1)} %shard_map.131.refs_0_), channel_id=1, source_target_pairs={{0,28},{4,0},{8,4},{12,8},{16,12},{20,16},{24,20},{28,24},{1,29},{... | collective-permute-start | bytes 122888 | tf_op jit(solution)/shard_map/ppermute | solution.py:507
  55.1 21.9 %copy-start.18 = (s32[256,2]{0,1:T(2,128)S(1)}, s32[256,2]{0,1:T(2,128)}, u32[]{:S(2)}) copy-start(s32[256,2]{0,1:T(2,128)} %param.25) | copy-start | bytes 6148
  73.9 5.0 %collective-permute-start.13 = (f32[40,256]{1,0:T(8,128)S(1)}, f32[40,256]{1,0:T(8,128)S(1)}, u32[]{:S(2)}, u32[]{:S(2)}) collective-permute-start(f32[40,256]{1,0:T(8,128)S(1)} %get-tuple-element.42.refs_0_), channel_id=1, source_target_pairs={{0,1},{1,2},{2,3},{3,0},{4,5},{5,6},{6,7},{7,4},{8,9},{9,10},{10,1... | collective-permute-start | bytes 122888 | tf_op jit(solution)/shard_map/ppermute | solution.py:507
  74.3 4.5 %collective-permute-start.14 = (f32[40,256]{1,0:T(8,128)S(1)}, f32[40,256]{1,0:T(8,128)S(1)}, u32[]{:S(2)}, u32[]{:S(2)}) collective-permute-start(f32[40,256]{1,0:T(8,128)S(1)} %get-tuple-element.42.refs_0_), channel_id=1, source_target_pairs={{0,2},{1,3},{2,0},{3,1},{4,6},{5,7},{6,4},{7,5},{8,10},{9,11},{10,... | collective-permute-start | bytes 122888 | tf_op jit(solution)/shard_map/ppermute | solution.py:507
  75.1 4.3 %collective-permute-start.15 = (f32[40,256]{1,0:T(8,128)S(1)}, f32[40,256]{1,0:T(8,128)S(1)}, u32[]{:S(2)}, u32[]{:S(2)}) collective-permute-start(f32[40,256]{1,0:T(8,128)S(1)} %get-tuple-element.42.refs_0_), channel_id=1, source_target_pairs={{0,3},{1,0},{2,1},{3,2},{4,7},{5,4},{6,5},{7,6},{8,11},{9,8},{10,9... | collective-permute-start | bytes 122888 | tf_op jit(solution)/shard_map/ppermute | solution.py:507
  (11 other events, 39.9 us)

commit v2 on v1

v2 whole, which is shorter than its diff:
```python
import functools

import jax
import jax.numpy as jnp
from jax import lax
from jax.experimental import pallas as pl
from jax.experimental.pallas import tpu as pltpu
from jax.sharding import PartitionSpec as P

F32 = jnp.float32
BF16 = jnp.bfloat16
HIGHEST = lax.Precision.HIGHEST
VMEM = pl.BlockSpec(memory_space=pltpu.VMEM)
SMEM = pl.BlockSpec(memory_space=pltpu.SMEM)
HBM = pl.BlockSpec(memory_space=pltpu.HBM)
LANES = 128


def f32_dot(left, right, dims):
    return lax.dot_general(left, right, (dims, ((), ())), precision=HIGHEST, preferred_element_type=F32)


def split(value):
    high = value.astype(BF16)
    return high, (value - high.astype(F32)).astype(BF16)


def left_of(value, axis):
    high, low = split(value)
    return jnp.concatenate([high, low, high], axis=axis)


def right_of(value, axis):
    high, low = split(value)
    return jnp.concatenate([high, high, low], axis=axis)


def bf16_dot(left, right, dims):
    return lax.dot_general(left, right, (dims, ((), ())), preferred_element_type=F32)


def params(vmem_mib, side_effects=False):
    return pltpu.CompilerParams(vmem_limit_bytes=vmem_mib << 20)


def call(kernel, out_shape, in_specs, vmem_mib, out_specs=None, scratch=(), flops=0, moved=0, **more):
    if out_specs is None:
        out_specs = jax.tree.map(lambda _: VMEM, out_shape)
    return pl.pallas_call(
        kernel,
        out_shape=out_shape,
        in_specs=in_specs,
        out_specs=out_specs,
        scratch_shapes=list(scratch),
        compiler_params=params(vmem_mib),
        cost_estimate=pl.CostEstimate(flops=flops, bytes_accessed=moved, transcendentals=0),
        **more,
    )


def struct(*shape, dtype=F32):
    return jax.ShapeDtypeStruct(shape, dtype)


def sort_walls(count, room, me, owner_ref, value_of, table, taken):
    for shift in range(count):
        taken[shift] = shift * room

    def step(entry, carry):
        shift = owner_ref[entry] - me
        shift = jnp.where(shift < 0, shift + count, shift)
        slot = taken[shift]
        taken[shift] = slot + 1
        table[slot] = value_of(entry)
        return carry

    lax.fori_loop(0, owner_ref.shape[0], step, 0, unroll=8)


def extras(rows, shift, count):
    return (rows // LANES if shift in (1, count - 1) else 0) + 1


def pack_kernel(count, room, chunk, owner_ref, offset_ref, force_hbm, v_hbm, *refs):
    outs, (force_ref, v_ref, table, taken, sem, v_sem) = refs[:count], refs[count:]
    walls = owner_ref.shape[0]
    rows, planes, cols = v_ref.shape
    me = lax.axis_index("gy")
    steps = rows // chunk
    copy = pltpu.make_async_copy(force_hbm, force_ref.at[pl.ds(0, walls)], sem)
    copy.start()

    def v_copy(k):
        span = pl.ds(k * chunk, chunk)
        return pltpu.make_async_copy(v_hbm.at[span], v_ref.at[span], v_sem.at[k])

    for k in range(steps):
        v_copy(k).start()
    force_ref[walls] = jnp.zeros(force_ref.shape[1:], F32)
    for slot in range(count * room):
        table[slot] = walls
    sort_walls(count, room, me, owner_ref, lambda entry: entry, table, taken)
    copy.wait()
    lane = lax.broadcasted_iota(jnp.int32, (planes, LANES), 1)
    for shift in list(range(1, count)) + [0]:
        places = jnp.full((planes, LANES), -1, jnp.int32)
        for slot in range(room):
            entry = table[shift * room + slot]
            outs[shift][slot] = force_ref[entry]
            place = jnp.where(entry < walls, offset_ref[jnp.minimum(entry, walls - 1)], -1)
            places = jnp.where(lane == slot, place, places)
        outs[shift][outs[shift].shape[0] - 1] = places.astype(F32)
    for block in range(rows // LANES):
        first, last = jnp.zeros((planes, LANES), F32), jnp.zeros((planes, LANES), F32)
        for x in range(LANES):
            at = block * LANES + x
            if at % chunk == 0:
                v_copy(at // chunk).wait()
            first = jnp.where(lane == x, pltpu.roll(v_ref[at, :, 0:LANES], x, 1), first)
            last = jnp.where(lane == x, pltpu.roll(v_ref[at, :, cols - LANES : cols], (x + 1) % LANES, 1), last)
        outs[1][room + block] = last
        outs[count - 1][room + block] = first


def pack(owner, offset, force, velocity, count, room):
    walls, planes, width = force.shape
    rows = velocity.shape[0]
    chunk = 64
    return call(
        functools.partial(pack_kernel, count, room, chunk),
        [struct(room + extras(rows, s, count), planes, width) for s in range(count)],
        [SMEM, SMEM, HBM, HBM],
        8,
        scratch=[
            pltpu.VMEM((walls + 1, planes, width), F32),
            pltpu.VMEM(velocity.shape, F32),
            pltpu.SMEM((count * room,), jnp.int32),
            pltpu.SMEM((count,), jnp.int32),
            pltpu.SemaphoreType.DMA,
            pltpu.SemaphoreType.DMA((rows // chunk,)),
        ],
    )(owner, offset, force, velocity)


def row(ref, index):
    base = index // 8 * 8
    return ref[base : base + 8, :][index - base : index - base + 1]


def half_shift_lanes(value):
    length = value.shape[1]
    at = lax.broadcasted_iota(jnp.int32, value.shape, 1)
    before = jnp.where(at == 0, 0.0, pltpu.roll(value, 1, 1))
    after = jnp.where(at == length - 1, 0.0, pltpu.roll(value, length - 1, 1))
    return 0.5 * (before + after)


def half_shift_rows(value):
    length = value.shape[0]
    at = lax.broadcasted_iota(jnp.int32, value.shape, 0)
    before = jnp.where(at == 0, 0.0, pltpu.roll(value, 1, 0))
    after = jnp.where(at == length - 1, 0.0, pltpu.roll(value, length - 1, 0))
    return 0.5 * (before + after)


def factor_kernel(lx, ux, lcx, ucx, ly, uy, lcy, ucy, mx, my, aux, my_t, aux_t, xrows, yrows, frows, scal):
    rows_x, rows_y = lx.shape[0], ly.shape[0]
    both = f32_dot(ux[...], lx[...], ((1,), (0,)))
    mx[...] = left_of(half_shift_rows(both), 1)
    both_y = f32_dot(uy[...], ly[...], ((1,), (0,)))
    turned = both_y.T
    my[...] = left_of(turned, 0)
    my_t[...] = left_of(half_shift_rows(turned), 0)
    zero = jnp.zeros((1, rows_x), F32)
    lc, uc = lcx[...], ucx[...]
    pad = jnp.zeros((7, rows_x), F32)
    u_lc = f32_dot(jnp.concatenate([lc, pad], 0), ux[...], ((1,), (1,)))[0:1]
    at = lax.broadcasted_iota(jnp.int32, (1, rows_x), 1)
    c0 = half_shift_lanes(u_lc)
    c1 = half_shift_lanes(uc) + jnp.where(at == rows_x - 1, 0.5, 0.0)
    c2 = jnp.where(at == 0, 0.5, 0.0)
    xrows[...] = jnp.concatenate([c0, c1, c2, zero, zero, zero, zero, zero], 0)
    lcv, ucv = lcy[...], ucy[...]
    pad_y = jnp.zeros((7, rows_y), F32)
    uy_lc = f32_dot(jnp.concatenate([lcv, pad_y], 0), uy[...], ((1,), (1,)))[0:1]
    f0 = row(ly, rows_y - 1)
    f1 = both_y[0:8][0:1]
    zero_y = jnp.zeros((1, rows_y), F32)
    m0, m1 = 0.5 * turned[0:8][0:1], 0.5 * turned[rows_y - 8 : rows_y][7:8]
    yrows[...] = jnp.concatenate([uy_lc, ucv, m0, m1, f0, f1, zero_y, zero_y], 0)
    lane = lax.broadcasted_iota(jnp.int32, (rows_y, 128), 1)
    cols = jnp.concatenate([f0, f1, pad_y[:6]], 0).T
    spread_cols = jnp.where(lane < 64, cols[:, 0:1], cols[:, 1:2])
    aux[...] = left_of(spread_cols, 0)
    aux_t[...] = left_of(half_shift_rows(spread_cols), 0)
    frows[...] = jnp.concatenate([row(lx, rows_x - 1), both[0:8][0:1], zero, zero, zero, zero, zero, zero], 0)

    def spread(value, index, width):
        return jnp.broadcast_to(value[:, index : index + 1], (1, width))

    last = row(ux, rows_x - 1)
    scal[0:8, :] = jnp.concatenate(
        [
            spread(lc, rows_x - 1, rows_x),
            spread(u_lc, 0, rows_x),
            spread(uc, 0, rows_x),
            spread(last, rows_x - 1, rows_x),
            spread(uc, rows_x - 1, rows_x),
            zero,
            zero,
            zero,
        ],
        0,
    )
    scal[8:16, :] = jnp.concatenate(
        [
            spread(lcv, rows_y - 1, rows_x),
            spread(uy_lc, 0, rows_x),
            spread(ucv, 0, rows_x),
            zero,
            zero,
            zero,
            zero,
            zero,
        ],
        0,
    )


def factors(lx, ux, lcx, ucx, ly, uy, lcy, ucy):
    rows, cols = lx.shape[0], ly.shape[0]
    return call(
        factor_kernel,
        [
            struct(rows, 3 * rows, dtype=BF16),
            struct(3 * cols, cols, dtype=BF16),
            struct(3 * cols, 128, dtype=BF16),
            struct(3 * cols, cols, dtype=BF16),
            struct(3 * cols, 128, dtype=BF16),
            struct(8, rows),
            struct(8, cols),
            struct(8, rows),
            struct(16, rows),
        ],
        [VMEM] * 8,
        8,
    )(lx, ux, lcx[None, :], ucx[None, :], ly, uy, lcy[None, :], ucy[None, :])


def velocity_kernel(func_ref, my_t, aux_t, v_hbm, high_ref, low_ref, s_ref, edge_ref, v_ref, sem):
    rows, planes, cols = v_ref.shape
    steps = sem.shape[0]
    chunk = rows // steps
    group = planes

    def copy(k):
        span = pl.ds(k * chunk, chunk)
        return pltpu.make_async_copy(v_hbm.at[span], v_ref.at[span], sem.at[k])

    for k in range(steps):
        copy(k).start()
    lane = lax.broadcasted_iota(jnp.int32, (group, LANES), 1)
    lower, upper = jnp.zeros((planes, cols), F32), jnp.zeros((planes, cols), F32)
    for k in range(steps):
        copy(k).wait()
        for i in range(k * chunk, (k + 1) * chunk):
            value = v_ref[i]
            lower = lower + func_ref[0, i] * value
            upper = upper + func_ref[1, i] * value
        flat = right_of(v_ref[k * chunk : (k + 1) * chunk].reshape(chunk * planes, cols), 1)
        r = bf16_dot(flat, my_t[...], ((1,), (0,)))
        t = bf16_dot(flat, aux_t[...], ((1,), (0,)))
        for g in range(chunk // group):
            here = slice(g * group * planes, (g + 1) * group * planes)
            x = slice(k * chunk + g * group, k * chunk + (g + 1) * group)
            turned = jnp.swapaxes(r[here].reshape(group, planes, cols), 0, 1)
            high, low = split(turned)
            high_ref[:, x, :] = high
            low_ref[:, x, :] = low
            picked = jnp.swapaxes(t[here].reshape(group, planes, LANES), 0, 1)
            total = jnp.zeros((group, LANES), F32)
            for p in range(planes):
                total = jnp.where((lane == p) | (lane == 64 + p), picked[p], total)
            s_ref[x, :] = total
    edge_ref[0] = half_shift_lanes(lower)
    edge_ref[1] = half_shift_lanes(upper)


def velocity_part(func, my_t, aux_t, velocity):
    rows, planes, cols = velocity.shape
    chunk = 64
    return call(
        velocity_kernel,
        [
            struct(planes, rows, cols, dtype=BF16),
            struct(planes, rows, cols, dtype=BF16),
            struct(rows, LANES),
            struct(2, planes, cols),
        ],
        [SMEM, VMEM, VMEM, HBM],
        16,
        scratch=[pltpu.VMEM(velocity.shape, F32), pltpu.SemaphoreType.DMA((rows // chunk,))],
    )(func, my_t, aux_t, velocity)


def halos(count, room, rows, payload):
    me = lax.axis_index("gy")
    blocks = rows // LANES

    def column(s, there):
        value = jnp.concatenate([payload[s][room + b] for b in range(blocks)], 1)
        return jnp.where(there, value, 0.0)

    return column(1, me > 0), column(count - 1, me < count - 1)


def x_edge_kernel(count, room, table_ref, func_ref, edge_ref, frows, scal, *refs):
    payload, out = refs[:count], refs[count]
    planes, cols = edge_ref.shape[1:]
    width = payload[0].shape[2]
    nblock = cols // width
    low, high = edge_ref[0], edge_ref[1]
    at = lax.broadcasted_iota(jnp.int32, (planes, cols), 1)
    f0, f1 = frows[0:1, :], frows[1:2, :]
    hl, hr = halos(count, room, frows.shape[1], payload)
    for f, which in ((f0, 0), (f1, 1)):
        first = 0.5 * jnp.sum(hl * f, axis=1, keepdims=True)
        last = 0.5 * jnp.sum(hr * f, axis=1, keepdims=True)
        add = jnp.where(at == 0, first, 0.0) + jnp.where(at == cols - 1, last, 0.0)
        if which == 0:
            low = low + add
        else:
            high = high + add
    out[2 * planes : 2 * planes + 8, :] = scal[0:8, :]
    sums = [jnp.zeros((planes, width), F32) for _ in range(2 * nblock)]
    for s in range(count):

        def step(slot, sums):
            sums = list(sums)
            place = jnp.maximum(table_ref[s * room + slot], 0)
            line, half = place // nblock, place % nblock
            value = payload[s][slot]
            for f in range(2):
                weight = func_ref[f, line]
                for b in range(nblock):
                    sums[f * nblock + b] += jnp.where(half == b, weight, 0.0) * value
            return tuple(sums)

        sums = lax.fori_loop(0, room, step, tuple(sums), unroll=8)
    out[0:planes, :] = low + jnp.concatenate(sums[:nblock], 1)
    out[planes : 2 * planes, :] = high + jnp.concatenate(sums[nblock:], 1)


def x_edges(table, func, edge, frows, scal, payload, room):
    planes, cols = edge.shape[1:]
    count = len(payload)
    return call(
        functools.partial(x_edge_kernel, count, room),
        struct(2 * planes + 8, cols),
        [SMEM, SMEM] + [VMEM] * (3 + count),
        8,
    )(table, func, edge, frows, scal, *payload)


def sweep_kernel(count, room, mx, my, aux, yrows, high_ref, low_ref, sv_ref, *refs):
    payload, (w_ref, s_ref, zh_ref, wall_ref) = refs[:count], refs[count:]
    planes, rows, cols = w_ref.shape
    slots, width = wall_ref.shape[1:]
    nblock = cols // width
    hl, hr = halos(count, room, rows, payload)
    m = mx[...]
    zh = bf16_dot(right_of(jnp.concatenate([hl, hr], 0), 1), m, ((1,), (1,)))
    zh_ref[...] = zh
    lane8 = lax.broadcasted_iota(jnp.int32, (8, LANES), 1)
    places = jnp.full((8, slots), -1.0, F32)
    for s in range(count):
        here = payload[s][payload[s].shape[0] - 1][0:8]
        if s:
            here = pltpu.roll(here, s * room, 1)
        places = jnp.where((lane8 >= s * room) & (lane8 < (s + 1) * room), here, places)
    line = jnp.floor(places * (1.0 / nblock))
    half = places - nblock * line
    column = half.T
    row_ids = lax.broadcasted_iota(jnp.int32, (rows, slots), 0).astype(F32)
    chosen = jnp.where(row_ids == line[0:1], 1.0, 0.0).astype(BF16)
    sel_high = bf16_dot(m[:, 0:rows], chosen, ((1,), (0,))).astype(BF16)
    sel_low = bf16_dot(m[:, rows : 2 * rows], chosen, ((1,), (0,))).astype(BF16)
    left = jnp.concatenate([m, sel_high, sel_low, sel_high], 1)
    keep = [jnp.broadcast_to(column[:, 0:1] == b, (slots, width)) for b in range(nblock)]
    for s in range(count):
        step = min(room, 16)
        for g in range(room // step):
            value = jnp.swapaxes(payload[s][g * step : (g + 1) * step], 0, 1)
            wall_ref[:, s * room + g * step : s * room + (g + 1) * step, :] = value
    lane = lax.broadcasted_iota(jnp.int32, (slots, LANES), 1)
    total = jnp.zeros((slots, LANES), F32)
    for p in range(planes):
        wall = wall_ref[p]
        wc = right_of(jnp.concatenate([jnp.where(k, wall, 0.0) for k in keep], 1), 1)
        r = right_of(bf16_dot(wc, my[...], ((1,), (0,))), 0)
        t = bf16_dot(wc, aux[...], ((1,), (0,)))
        total = jnp.where((lane == p) | (lane == 64 + p), t, total)
        high = high_ref[p]
        w_ref[p] = bf16_dot(left, jnp.concatenate([high, high, low_ref[p], r], 0), ((1,), (0,)))
    turned = bf16_dot(left, jnp.concatenate([right_of(sv_ref[...], 0), right_of(total, 0)], 0), ((1,), (0,))).T
    low, high = turned[0:planes], turned[64 : 64 + planes]
    f0, f1 = yrows[4:5, :], yrows[5:6, :]
    zl, zr = zh[0:planes], zh[planes : 2 * planes]
    s_ref[0:planes, :] = low + 0.5 * (zl * f0[:, 0:1] + zr * f0[:, cols - 1 : cols])
    s_ref[planes : 2 * planes, :] = high + 0.5 * (zl * f1[:, 0:1] + zr * f1[:, cols - 1 : cols])


def sweep(mx, my, aux, yrows, high, low, sv, payload, room):
    planes, rows, cols = high.shape
    count, width = len(payload), payload[0].shape[2]
    return call(
        functools.partial(sweep_kernel, count, room),
        [struct(planes, rows, cols), struct(2 * planes, rows), struct(2 * planes, rows)],
        [VMEM] * (7 + count),
        16,
        scratch=[pltpu.VMEM((planes, count * room, width), F32)],
    )(mx, my, aux, yrows, high, low, sv, *payload)


def chain(parts, count, me, planes, f_in):
    lanes = parts.shape[2]
    zero = jnp.zeros((planes, lanes), F32)
    f, mine_f = zero, zero
    for k in range(count):
        f_in[k] = f
        mine_f = jnp.where(k == me, f, mine_f)
        f = parts[k, 0:planes, :] + parts[k, 2 * planes : 2 * planes + 1, :] * f
    g, mine_g = zero, zero
    for k in range(count - 1, -1, -1):
        scal = parts[k, 2 * planes : 2 * planes + 8, :]
        mine_g = jnp.where(k == me, g, mine_g)
        g = parts[k, planes : 2 * planes, :] + scal[1:2] * f_in[k] + scal[2:3] * g
    return mine_f, mine_g


def pair_kernel(mine, other, out):
    planes = (mine.shape[0] - 8) // 2
    odd = lax.rem(lax.axis_index("gx"), 2) == 1
    left = jnp.where(odd, other[...], mine[...])
    right = jnp.where(odd, mine[...], other[...])
    out[...] = joined(left, right, planes)


def joined(left, right, planes):
    a, b, s = left[0:planes], left[planes : 2 * planes], left[2 * planes :]
    c, d, t = right[0:planes], right[planes : 2 * planes], right[2 * planes :]
    l0, c0, u0 = s[0:1], s[1:2], s[2:3]
    l1, c1, u1 = t[0:1], t[1:2], t[2:3]
    return jnp.concatenate(
        [c + l1 * a, b + u0 * (d + c1 * a), l0 * l1, c0 + u0 * c1 * l0, u0 * u1, t[3:8]],
        0,
    )


def pair(mine, other):
    return call(pair_kernel, struct(*mine.shape), [VMEM, VMEM], 8)(mine, other)


def gather_parts(me, parts, received):
    count = len(received)
    for shift in range(count):
        parts[pl.ds(lax.rem(me - shift + count, count), 1)] = received[shift][...][None]


def x_join_kernel(count, my, xrows, yrows, scal, s_ref, mine_ref, other_ref, *refs):
    received, (out, moved, parts, f_in) = refs[:count], refs[count:]
    me = lax.axis_index("gx")
    place = lax.div(me, 2)
    odd = lax.rem(me, 2) == 1
    planes = s_ref.shape[0] // 2
    gather_parts(place, parts, received)
    f, g = chain(parts, count, place, planes, f_in)
    mine, other = mine_ref[...], other_ref[...]
    left, right = jnp.where(odd, other, mine), jnp.where(odd, mine, other)
    a, ls = left[0:planes], left[2 * planes :]
    d, rs = right[planes : 2 * planes], right[2 * planes :]
    f_mid = a + ls[0:1] * f
    g_mid = d + rs[1:2] * f_mid + rs[2:3] * g
    in_f, in_b = jnp.where(odd, f_mid, f), jnp.where(odd, g, g_mid)
    ms = mine[2 * planes :]
    first = mine[planes : 2 * planes] + ms[1:2] * in_f + ms[2:3] * in_b
    before_s = jnp.where(odd, ls, parts[jnp.maximum(place - 1, 0), 2 * planes : 2 * planes + 8, :])
    before = jnp.where(me > 0, before_s[3:4] * in_f + before_s[4:5] * first, 0.0)
    low, high = s_ref[0:planes, :], s_ref[planes : 2 * planes, :]
    f0, f1 = yrows[4:5, :], yrows[5:6, :]
    for index, value in enumerate((in_f, in_b, before)):
        c = xrows[index : index + 1, :]
        low = low + jnp.sum(value * f0, axis=1, keepdims=True) * c
        high = high + jnp.sum(value * f1, axis=1, keepdims=True) * c
    out[0:planes, :] = low
    out[planes : 2 * planes, :] = high
    out[2 * planes : 2 * planes + 8, :] = scal[8:16, :]
    moved[...] = bf16_dot(right_of(jnp.concatenate([in_f, in_b, before], 0), 1), my[...], ((1,), (0,)))


def x_join(my, xrows, yrows, scal, s, mine, other, received):
    count = len(received)
    height, cols = received[0].shape
    planes, rows = s.shape[0] // 2, s.shape[1]
    return call(
        functools.partial(x_join_kernel, count),
        [struct(2 * planes + 8, rows), struct(3 * planes, cols)],
        [VMEM] * (7 + count),
        8,
        scratch=[pltpu.VMEM((count, height, cols), F32), pltpu.VMEM((count, planes, cols), F32)],
    )(my, xrows, yrows, scal, s, mine, other, *received)


def finish_kernel(count, part, xrows, yrows, moved, solid, zh_ref, w_ref, *refs):
    received, (out_hbm, parts, f_in, both, value_ref, out_ref, out_sem) = refs[:count], refs[count:]
    me = lax.axis_index("gy")
    planes, rows, cols = w_ref.shape
    halves = out_ref.shape[0]

    def out_copy(k, b):
        span = pl.ds(k * part * planes, part * planes)
        return pltpu.make_async_copy(out_ref.at[b, span, :], out_hbm.at[span, pl.ds(b * 128, 128)], out_sem.at[k, b])

    steps = rows // part
    gather_parts(me, parts, received)
    in_f, in_b = chain(parts, count, me, planes, f_in)
    both[0] = in_f
    both[1] = in_b
    y = yrows[0:4, :]
    width = cols // solid.shape[0]
    for k in range(steps):
        lo = k * part
        c = xrows[0:3, lo : lo + part]
        marks = jnp.concatenate([solid[:, lo : lo + part].astype(F32), jnp.zeros((8 - solid.shape[0], part), F32)], 0).T
        fluid = [jnp.broadcast_to(marks[:, b * LANES // width : b * LANES // width + 1] == 0.0, (part, LANES)) for b in range(halves)]
        for p in range(planes):
            left = jnp.concatenate(
                [
                    c,
                    both[0, p : p + 1, lo : lo + part],
                    both[1, p : p + 1, lo : lo + part],
                    zh_ref[p : p + 1, lo : lo + part],
                    zh_ref[planes + p : planes + p + 1, lo : lo + part],
                    jnp.zeros((1, part), F32),
                ],
                0,
            )
            right = jnp.concatenate(
                [
                    moved[p : p + 1, :],
                    moved[planes + p : planes + p + 1, :],
                    moved[2 * planes + p : 2 * planes + p + 1, :],
                    y,
                    jnp.zeros((1, cols), F32),
                ],
                0,
            )
            lh = left.astype(BF16).astype(F32)
            rh = right.astype(BF16).astype(F32)
            lc = jnp.concatenate([lh, lh, left - lh], 0).astype(BF16)
            rc = jnp.concatenate([rh, right - rh, rh], 0).astype(BF16)
            value = w_ref[p, lo : lo + part, :] + bf16_dot(lc, rc, ((0,), (0,)))
            for b in range(halves):
                value_ref[b, p] = jnp.where(fluid[b], value[:, b * LANES : (b + 1) * LANES], 0.0)
        for b in range(halves):
            for g in range(part // planes):
                turned = jnp.swapaxes(value_ref[b, :, g * planes : (g + 1) * planes, :], 0, 1)
                at = (lo + g * planes) * planes
                out_ref[b, at : at + planes * planes, :] = turned.reshape(planes * planes, LANES)
        for b in range(halves):
            out_copy(k, b).start()
    for k in range(steps):
        for b in range(halves):
            out_copy(k, b).wait()


def finish(xrows, yrows, moved, solid, zh, w, received):
    count = len(received)
    height = received[0].shape[0]
    planes, rows, cols = w.shape
    part, halves = 128, cols // 128
    out = call(
        functools.partial(finish_kernel, count, part),
        struct(rows * planes, cols),
        [VMEM] * (6 + count),
        12,
        out_specs=HBM,
        scratch=[
            pltpu.VMEM((count, height, rows), F32),
            pltpu.VMEM((count, planes, rows), F32),
            pltpu.VMEM((2, planes, rows), F32),
            pltpu.VMEM((halves, planes, part, LANES), F32),
            pltpu.VMEM((halves, rows * planes, 128), F32),
            pltpu.SemaphoreType.DMA((rows // part, halves)),
        ],
    )(xrows, yrows, moved, solid, zh, w, *received)
    return out.reshape(rows, planes, cols)


def rotate(value, axis, shift):
    count = lax.axis_size(axis)
    return lax.ppermute(value, axis, [(i, (i + shift) % count) for i in range(count)])


def on_device(
    velocity,
    lower_x,
    upper_x,
    lower_carry_x,
    upper_carry_x,
    lower_y,
    upper_y,
    lower_carry_y,
    upper_carry_y,
    wall_force,
    wall_owner,
    wall_offset,
    solid_mask,
):
    rows, planes, cols = velocity.shape
    walls = wall_force.shape[0]
    n_x, n_y = lax.axis_size("gx"), lax.axis_size("gy")
    room = 2 * walls // n_y
    owner = wall_owner[:, 0]
    packed = pack(owner, wall_offset, wall_force, velocity, n_y, room)
    payload = [packed[0]] + [rotate(packed[s], "gy", s) for s in range(1, n_y)]
    table = jnp.concatenate([v[-1, 0, :room] for v in payload]).astype(jnp.int32)
    mx, my, aux, my_t, aux_t, xrows, yrows, frows, scal = factors(
        lower_x, upper_x, lower_carry_x, upper_carry_x, lower_y, upper_y, lower_carry_y, upper_carry_y
    )
    func = frows[0:2]
    high, low, sv, edge = velocity_part(func, my_t, aux_t, velocity)
    mine = x_edges(table, func, edge, frows, scal, payload, room)
    other = lax.ppermute(mine, "gx", [(i, i ^ 1) for i in range(n_x)])
    both = pair(mine, other)
    received = [both] + [rotate(both, "gx", 2 * s) for s in range(1, n_x // 2)]
    w, s_edge, zh = sweep(mx, my, aux, yrows, high, low, sv, payload, room)
    mine, moved = x_join(my, xrows, yrows, scal, s_edge, mine, other, received)
    received = [mine] + [rotate(mine, "gy", s) for s in range(1, n_y)]
    return finish(xrows, yrows, moved, solid_mask.T, zh, w, received)


def solution(mesh):
    placed = (
        P("gx", None, "gy"),
        P("gx", None),
        P("gx", None),
        P("gx"),
        P("gx"),
        P("gy", None),
        P("gy", None),
        P("gy"),
        P("gy"),
        P(("gx", "gy"), None, None),
        P(("gx", "gy"), None),
        P(("gx", "gy")),
        P("gx", "gy"),
    )
    return jax.shard_map(
        on_device, mesh=mesh, in_specs=placed, out_specs=P("gx", None, "gy"), check_vma=False
    )
```

time: 85.7 us -> 50 us (0.58)
  local copies, waits for them, and re-layouts: 23.9 us -> 6.49 us
  Pallas kernels: 31.9 us -> 21.2 us
  starting transfers between devices: 21.4 us -> 16.2 us
  waiting for transfers between devices: 7.83 us -> 5.4 us
    unnamed x41 -> x28, local copies, waits for them, and re-layouts: 19 us -> 6.48 us
    pallas_call x4 -> x5, Pallas kernels: 26.8 us -> 16.7 us  [the longest x1 6.52 us: velocity_part(): call(velocity_kernel, [struct(planes, rows, cols, dtype=BF16), struct(pla...]
    ppermute x16 -> x9, starting transfers between devices: 21.4 us -> 16.2 us  [rotate(): lax.ppermute(value, axis, [(i, (i + shift) % count) for i in range(count)])]
    slice x1 -> x0, local copies, waits for them, and re-layouts: 4.9 us -> none  [on_device(): first, last = (velocity[:, :, 0].T, velocity[:, :, cols - 1].T)]
    ppermute x16 -> x9, waiting for transfers between devices: 7.83 us -> 4.2 us  [rotate(): lax.ppermute(value, axis, [(i, (i + shift) % count) for i in range(count)])]
    ppermute x0 -> x1, waiting for transfers between devices: none -> 1.21 us  [on_device(): other = lax.ppermute(mine, 'gx', [(i, i ^ 1) for i in range(n_x)])]
  transfers between devices with their start and end apart: 16 -> 10, of which waited for: 4 -> 5; matrix products, arithmetic and copies ran while one was open for 3% -> 0% of each run, Pallas kernels for 25% -> 26%
where the time goes in v2:
time: 50 us; the launch traced here: 49.8 us
  Pallas kernels  21.2 us (42%)
  starting transfers between devices  16.2 us (32%)
  local copies, waits for them, and re-layouts  6.49 us (13%)
  waiting for transfers between devices  5.4 us (11%)
    ppermute x9, starting transfers between devices, rotate(): lax.ppermute(value, axis, [(i, (i + shift) % count) for i in range(count)])  16.2 us
    pallas_call x1, Pallas kernels, velocity_part(): call(velocity_kernel, [struct(planes, rows, cols, dtype=BF16), struct(pla...  6.52 us
    unnamed x28, local copies, waits for them, and re-layouts  6.48 us
    pallas_call x1, Pallas kernels, sweep(): call(functools.partial(sweep_kernel, count, room), [struct(planes, rows,...  5.25 us
    ppermute x9, waiting for transfers between devices, rotate(): lax.ppermute(value, axis, [(i, (i + shift) % count) for i in range(count)])  4.2 us
    pallas_call x1, Pallas kernels, finish(): call(functools.partial(finish_kernel, count, part), struct(rows * planes,...  3.17 us
    pallas_call x1, Pallas kernels, pack(): call(functools.partial(pack_kernel, count, room, chunk), [struct(room + e...  3.07 us
    pallas_call x1, Pallas kernels, x_edges(): call(functools.partial(x_edge_kernel, count, room), struct(2 * planes + 8...  1.81 us
  transfers between devices with their start and end apart: 10, of which 5 were waited for; matrix products, arithmetic and copies ran while one was open for 0% of the time, Pallas kernels for 26%

profile of v2, /device:TPU:0, one launch (start us, length us, event | category | flops | bytes accessed | tf_op | source)
XLA Modules:
  0.0 49.8 jit_solution(6448963944478538708)
XLA Ops:
  0.0 2.2 %copy-done = f32[256,16,256]{2,1,0:T(8,128)S(1)} copy-done((f32[256,16,256]{2,1,0:T(8,128)S(1)}, f32[256,16,256]{2,1,0:T(8,128)}, u32[]{:S(2)}) %copy-start) | copy-done | bytes 4194328
  2.2 1.0 %copy-done.2 = f32[64,16,128]{2,1,0:T(8,128)S(1)} copy-done((f32[64,16,128]{2,1,0:T(8,128)S(1)}, f32[64,16,128]{2,1,0:T(8,128)}, u32[]{:S(2)}) %copy-start.2) | copy-done | bytes 524312
  3.9 0.7 %copy-done.13 = s32[64]{0:T(128)S(1)} copy-done((s32[64]{0:T(128)S(1)}, s32[64]{0:T(128)}, u32[]{:S(2)}) %copy-start.13) | copy-done | bytes 280
  4.6 3.1 %shard_map.129 = (f32[33,16,128]{2,1,0:T(8,128)S(1)}, f32[35,16,128]{2,1,0:T(8,128)S(1)}, f32[33,16,128]{2,1,0:T(8,128)S(1)}, f32[35,16,128]{2,1,0:T(8,128)S(1)}) custom-call(s32[64]{0:T(128)S(1)} %bitcast.20, s32[64]{0:T(128)S(1)} %copy-done.13, f32[64,16,128]{2,1,0:T(8,128)S(1)} %copy-done.2, f32[256,16,256]{2,1,0:T(8,128)S(1)} %copy-done), custom_call_target="tpu_custom_call" | custom-call | tf_op jit(solution)/shard_map/pallas_call | solution.py:129
  7.7 3.0 %collective-permute-start.1 = (f32[33,16,128]{2,1,0:T(8,128)S(1)}, f32[33,16,128]{2,1,0:T(8,128)S(1)}, u32[]{:S(2)}, u32[]{:S(2)}) collective-permute-start(f32[33,16,128]{2,1,0:T(8,128)S(1)} %get-tuple-element.41), channel_id=1, source_target_pairs={{0,2},{1,3},{2,0},{3,1},{4,6},{5,7},{6,4},{7,5},{8,10},{9,11},{10,... | collective-permute-start | bytes 811016 | tf_op jit(solution)/shard_map/ppermute | solution.py:602
  10.7 1.5 %collective-permute-start = (f32[35,16,128]{2,1,0:T(8,128)S(1)}, f32[35,16,128]{2,1,0:T(8,128)S(1)}, u32[]{:S(2)}, u32[]{:S(2)}) collective-permute-start(f32[35,16,128]{2,1,0:T(8,128)S(1)} %get-tuple-element.40), channel_id=1, source_target_pairs={{0,1},{1,2},{2,3},{3,0},{4,5},{5,6},{6,7},{7,4},{8,9},{9,10},{10,1... | collective-permute-start | bytes 860168 | tf_op jit(solution)/shard_map/ppermute | solution.py:602
  12.2 1.4 %collective-permute-start.2 = (f32[35,16,128]{2,1,0:T(8,128)S(1)}, f32[35,16,128]{2,1,0:T(8,128)S(1)}, u32[]{:S(2)}, u32[]{:S(2)}) collective-permute-start(f32[35,16,128]{2,1,0:T(8,128)S(1)} %get-tuple-element.42), channel_id=1, source_target_pairs={{0,3},{1,0},{2,1},{3,2},{4,7},{5,4},{6,5},{7,6},{8,11},{9,8},{10,9... | collective-permute-start | bytes 860168 | tf_op jit(solution)/shard_map/ppermute | solution.py:602
  13.7 0.9 %copy-done.5 = f32[256,256]{1,0:T(8,128)S(1)} copy-done((f32[256,256]{1,0:T(8,128)S(1)}, f32[256,256]{1,0:T(8,128)}, u32[]{:S(2)}) %copy-start.5) | copy-done | bytes 262168
  14.6 0.9 %copy-done.6 = f32[256,256]{1,0:T(8,128)S(1)} copy-done((f32[256,256]{1,0:T(8,128)S(1)}, f32[256,256]{1,0:T(8,128)}, u32[]{:S(2)}) %copy-start.6) | copy-done | bytes 262168
  15.6 1.2 %shard_map.127 = (bf16[256,768]{1,0:T(8,128)(2,1)S(1)}, bf16[768,256]{1,0:T(8,128)(2,1)S(1)}, bf16[768,128]{1,0:T(8,128)(2,1)S(1)}, bf16[768,256]{1,0:T(8,128)(2...) custom-call(f32[256,256]{1,0:T(8,128)S(1)} %copy-done.3, ...), custom_call_target="tpu_custom_call" | custom-call | tf_op jit(solution)/shard_map/pallas_call | solution.py:232
  16.8 6.5 %shard_map.128 = (bf16[16,256,256]{2,1,0:T(8,128)(2,1)S(1)}, bf16[16,256,256]{2,1,0:T(8,128)(2,1)S(1)}, f32[256,128]{1,0:T(8,128)S(1)}, f32[2,16,256]{2,1,0:T(8,128)S(1)}) custom-call(f32[2,256]{1,0:T(2,128)S(1)} %slice.15.func_ref, bf16[768,256]{1,0:T(8,128)(2,1)S(1)} %get-tuple-element.34.my_t, bf16[768,128]{1,0:T(8,128)(2,1)S(1)} %get-tuple-element.35.aux_t, ...), custom_call_target="tpu_custom_call" | custom-call | tf_op jit(solution)/shard_map/pallas_call | solution.py:292
  23.3 1.6 %collective-permute-done.2.refs_3_ = f32[35,16,128]{2,1,0:T(8,128)S(1)} collective-permute-done((f32[35,16,128]{2,1,0:T(8,128)S(1)}, f32[35,16,128]{2,1,0:T(8,128)S(1)}, u32[]{:S(2)}, u32[]{:S(2)}) %collective-permute-start.2) | collective-permute-done | bytes 286752 | tf_op jit(solution)/shard_map/ppermute | solution.py:602
  25.1 1.8 %shard_map.131.mine.mine_ref = f32[40,256]{1,0:T(8,128)S(1)} custom-call(s32[128]{0:T(128)S(1)} %maximum_convert_fusion.table_ref, f32[2,256]{1,0:T(2,128)S(1)} %slice.15.func_ref, f32[2,16,256]{2,1,0:T(8,128)S(1)} %get-tuple-element.44.edge_ref, f32[8,256]{1,0:T(8,128)S(1)} %get-tuple-element.33.frows, f32[16,256]{1,0:T(8,128)S(1)} %get-tuple-element.30.scal, ...), custom_call_target="tpu_custom_call" | custom-call | tf_op jit(solution)/shard_map/pallas_call | solution.py:357
  26.9 1.2 %collective-permute-done.3.other.other_ref = f32[40,256]{1,0:T(8,128)S(1)} collective-permute-done((f32[40,256]{1,0:T(8,128)S(1)}, f32[40,256]{1,0:T(8,128)S(1)}, u32[]{:S(2)}, u32[]{:S(2)}) %collective-permute-start.3) | collective-permute-done | bytes 40992 | tf_op jit(solution)/shard_map/ppermute | solution.py:634
  28.2 1.8 %collective-permute-start.4 = (f32[40,256]{1,0:T(8,128)S(1)}, f32[40,256]{1,0:T(8,128)S(1)}, u32[]{:S(2)}, u32[]{:S(2)}) collective-permute-start(f32[40,256]{1,0:T(8,128)S(1)} %shard_map.132.refs_0_), channel_id=1, source_target_pairs={{0,8},{4,12},{8,16},{12,20},{16,24},{20,28},{24,0},{28,4},{1,9},{5... | collective-permute-start | bytes 122888 | tf_op jit(solution)/shard_map/ppermute | solution.py:602
  30.0 2.6 %collective-permute-start.5 = (f32[40,256]{1,0:T(8,128)S(1)}, f32[40,256]{1,0:T(8,128)S(1)}, u32[]{:S(2)}, u32[]{:S(2)}) collective-permute-start(f32[40,256]{1,0:T(8,128)S(1)} %shard_map.132.refs_0_), channel_id=1, source_target_pairs={{0,16},{4,20},{8,24},{12,28},{16,0},{20,4},{24,8},{28,12},{1,17},{... | collective-permute-start | bytes 122888 | tf_op jit(solution)/shard_map/ppermute | solution.py:602
  32.6 1.3 %collective-permute-start.6 = (f32[40,256]{1,0:T(8,128)S(1)}, f32[40,256]{1,0:T(8,128)S(1)}, u32[]{:S(2)}, u32[]{:S(2)}) collective-permute-start(f32[40,256]{1,0:T(8,128)S(1)} %shard_map.132.refs_0_), channel_id=1, source_target_pairs={{0,24},{4,28},{8,0},{12,4},{16,8},{20,12},{24,16},{28,20},{1,25},{... | collective-permute-start | bytes 122888 | tf_op jit(solution)/shard_map/ppermute | solution.py:602
  33.9 5.2 %shard_map.130 = (f32[16,256,256]{2,1,0:T(8,128)S(1)}, f32[32,256]{1,0:T(8,128)S(1)}, f32[32,256]{1,0:T(8,128)S(1)}) custom-call(bf16[256,768]{1,0:T(8,128)(2,1)S(1)} %get-tuple-element.31.mx, bf16[768,256]{1,0:T(8,128)(2,1)S(1)} %get-tuple-element.29.my, bf16[768,128]{1,0:T(8,128)(2,1)S(1)} %get-tuple-element.32.aux, f32[8,256]{1,0:T(8,128)S(1)} %get-tuple-element.28.yrows, ...), custom_call_target="tpu_custom_call" | custom-call | tf_op jit(solution)/shard_map/pallas_call | solution.py:416
  39.4 1.5 %collective-permute-start.7 = (f32[40,256]{1,0:T(8,128)S(1)}, f32[40,256]{1,0:T(8,128)S(1)}, u32[]{:S(2)}, u32[]{:S(2)}) collective-permute-start(f32[40,256]{1,0:T(8,128)S(1)} %get-tuple-element.48.refs_0_), channel_id=1, source_target_pairs={{0,1},{1,2},{2,3},{3,0},{4,5},{5,6},{6,7},{7,4},{8,9},{9,10},{10,1... | collective-permute-start | bytes 122888 | tf_op jit(solution)/shard_map/ppermute | solution.py:602
  40.9 1.5 %collective-permute-start.8 = (f32[40,256]{1,0:T(8,128)S(1)}, f32[40,256]{1,0:T(8,128)S(1)}, u32[]{:S(2)}, u32[]{:S(2)}) collective-permute-start(f32[40,256]{1,0:T(8,128)S(1)} %get-tuple-element.48.refs_0_), channel_id=1, source_target_pairs={{0,2},{1,3},{2,0},{3,1},{4,6},{5,7},{6,4},{7,5},{8,10},{9,11},{10,... | collective-permute-start | bytes 122888 | tf_op jit(solution)/shard_map/ppermute | solution.py:602
  42.4 1.5 %collective-permute-start.9 = (f32[40,256]{1,0:T(8,128)S(1)}, f32[40,256]{1,0:T(8,128)S(1)}, u32[]{:S(2)}, u32[]{:S(2)}) collective-permute-start(f32[40,256]{1,0:T(8,128)S(1)} %get-tuple-element.48.refs_0_), channel_id=1, source_target_pairs={{0,3},{1,0},{2,1},{3,2},{4,7},{5,4},{6,5},{7,6},{8,11},{9,8},{10,9... | collective-permute-start | bytes 122888 | tf_op jit(solution)/shard_map/ppermute | solution.py:602
  43.9 0.7 %collective-permute-done.7.refs_1_ = f32[40,256]{1,0:T(8,128)S(1)} collective-permute-done((f32[40,256]{1,0:T(8,128)S(1)}, f32[40,256]{1,0:T(8,128)S(1)}, u32[]{:S(2)}, u32[]{:S(2)}) %collective-permute-start.7) | collective-permute-done | bytes 40992 | tf_op jit(solution)/shard_map/ppermute | solution.py:602
  45.0 1.4 %collective-permute-done.9.refs_3_ = f32[40,256]{1,0:T(8,128)S(1)} collective-permute-done((f32[40,256]{1,0:T(8,128)S(1)}, f32[40,256]{1,0:T(8,128)S(1)}, u32[]{:S(2)}, u32[]{:S(2)}) %collective-permute-start.9) | collective-permute-done | bytes 40992 | tf_op jit(solution)/shard_map/ppermute | solution.py:602
  46.4 3.2 %shard_map.134 = f32[4096,256]{1,0:T(8,128)} custom-call(f32[8,256]{1,0:T(8,128)S(1)} %get-tuple-element.27.xrows, f32[8,256]{1,0:T(8,128)S(1)} %get-tuple-element.28.yrows, f32[48,256]{1,0:T(8,128)S(1)} %get-tuple-element.45.moved, s32[2,256]{1,0:T(2,128)S(1)} %bitcast.15, f32[32,256]{1,0:T(8,128)S(1)} %get-tuple-element.46.zh_ref, ...), custom_call_target="tpu_custom_call" | custom-call | tf_op jit(solution)/shard_map/pallas_call | solution.py:582
  (38 shorter events, 1.6 us)
Async XLA Ops:
  0.0 13.6 %copy-start.8 = (f32[256]{0:T(256)S(1)}, f32[256]{0:T(256)}, u32[]{:S(2)}) copy-start(f32[256]{0:T(256)} %param.16) | copy-start | bytes 3076
  0.0 2.2 %copy-start = (f32[256,16,256]{2,1,0:T(8,128)S(1)}, f32[256,16,256]{2,1,0:T(8,128)}, u32[]{:S(2)}) copy-start(f32[256,16,256]{2,1,0:T(8,128)} %v_hbm.3) | copy-start | bytes 12582916
  2.2 1.0 %copy-start.2 = (f32[64,16,128]{2,1,0:T(8,128)S(1)}, f32[64,16,128]{2,1,0:T(8,128)}, u32[]{:S(2)}) copy-start(f32[64,16,128]{2,1,0:T(8,128)} %force_hbm.1) | copy-start | bytes 1572868
  3.2 0.7 %copy-start.12 = (s32[64,1]{0,1:T(1,128)S(1)}, s32[64,1]{0,1:T(1,128)}, u32[]{:S(2)}) copy-start(s32[64,1]{0,1:T(1,128)} %param.23) | copy-start | bytes 772
  3.9 0.7 %copy-start.13 = (s32[64]{0:T(128)S(1)}, s32[64]{0:T(128)}, u32[]{:S(2)}) copy-start(s32[64]{0:T(128)} %offset_ref.1) | copy-start | bytes 772
  4.6 9.1 %copy-start.3 = (f32[256,256]{1,0:T(8,128)S(1)}, f32[256,256]{1,0:T(8,128)}, u32[]{:S(2)}) copy-start(f32[256,256]{1,0:T(8,128)} %lx.1) | copy-start | bytes 786436
  4.6 9.1 %copy-start.4 = (f32[256,256]{1,0:T(8,128)S(1)}, f32[256,256]{1,0:T(8,128)}, u32[]{:S(2)}) copy-start(f32[256,256]{1,0:T(8,128)} %ux.1) | copy-start | bytes 786436
  4.6 9.1 %copy-start.9 = (f32[256]{0:T(256)S(1)}, f32[256]{0:T(256)}, u32[]{:S(2)}) copy-start(f32[256]{0:T(256)} %param.17) | copy-start | bytes 3076
  4.6 9.1 %copy-start.10 = (f32[256]{0:T(256)S(1)}, f32[256]{0:T(256)}, u32[]{:S(2)}) copy-start(f32[256]{0:T(256)} %param.20) | copy-start | bytes 3076
  4.6 9.1 %copy-start.11 = (f32[256]{0:T(256)S(1)}, f32[256]{0:T(256)}, u32[]{:S(2)}) copy-start(f32[256]{0:T(256)} %param.21) | copy-start | bytes 3076
  4.6 12.2 %copy-start.1 = (f32[256,16,256]{2,1,0:T(8,128)S(1)}, f32[256,16,256]{2,1,0:T(8,128)}, u32[]{:S(2)}) copy-start(f32[256,16,256]{2,1,0:T(8,128)} %v_hbm.3) | copy-start | bytes 12582916
  7.7 15.7 %collective-permute-start.1 = (f32[33,16,128]{2,1,0:T(8,128)S(1)}, f32[33,16,128]{2,1,0:T(8,128)S(1)}, u32[]{:S(2)}, u32[]{:S(2)}) collective-permute-start(f32[33,16,128]{2,1,0:T(8,128)S(1)} %get-tuple-element.41), channel_id=1, source_target_pairs={{0,2},{1,3},{2,0},{3,1},{4,6},{5,7},{6,4},{7,5},{8,10},{9,11},{10,... | collective-permute-start | bytes 811016 | tf_op jit(solution)/shard_map/ppermute | solution.py:602
  10.7 14.3 %collective-permute-start = (f32[35,16,128]{2,1,0:T(8,128)S(1)}, f32[35,16,128]{2,1,0:T(8,128)S(1)}, u32[]{:S(2)}, u32[]{:S(2)}) collective-permute-start(f32[35,16,128]{2,1,0:T(8,128)S(1)} %get-tuple-element.40), channel_id=1, source_target_pairs={{0,1},{1,2},{2,3},{3,0},{4,5},{5,6},{6,7},{7,4},{8,9},{9,10},{10,1... | collective-permute-start | bytes 860168 | tf_op jit(solution)/shard_map/ppermute | solution.py:602
  12.2 12.8 %collective-permute-start.2 = (f32[35,16,128]{2,1,0:T(8,128)S(1)}, f32[35,16,128]{2,1,0:T(8,128)S(1)}, u32[]{:S(2)}, u32[]{:S(2)}) collective-permute-start(f32[35,16,128]{2,1,0:T(8,128)S(1)} %get-tuple-element.42), channel_id=1, source_target_pairs={{0,3},{1,0},{2,1},{3,2},{4,7},{5,4},{6,5},{7,6},{8,11},{9,8},{10,9... | collective-permute-start | bytes 860168 | tf_op jit(solution)/shard_map/ppermute | solution.py:602
  13.7 1.0 %copy-start.5 = (f32[256,256]{1,0:T(8,128)S(1)}, f32[256,256]{1,0:T(8,128)}, u32[]{:S(2)}) copy-start(f32[256,256]{1,0:T(8,128)} %ly.1) | copy-start | bytes 786436
  14.6 0.9 %copy-start.6 = (f32[256,256]{1,0:T(8,128)S(1)}, f32[256,256]{1,0:T(8,128)}, u32[]{:S(2)}) copy-start(f32[256,256]{1,0:T(8,128)} %uy.1) | copy-start | bytes 786436
  25.1 21.4 %copy-start.7 = (s32[256,2]{0,1:T(2,128)S(1)}, s32[256,2]{0,1:T(2,128)}, u32[]{:S(2)}) copy-start(s32[256,2]{0,1:T(2,128)} %param.25) | copy-start | bytes 6148
  26.9 1.3 %collective-permute-start.3 = (f32[40,256]{1,0:T(8,128)S(1)}, f32[40,256]{1,0:T(8,128)S(1)}, u32[]{:S(2)}, u32[]{:S(2)}) collective-permute-start(f32[40,256]{1,0:T(8,128)S(1)} %shard_map.131.mine.mine_ref), channel_id=1, source_target_pairs={{0,4},{4,0},{8,12},{12,8},{16,20},{20,16},{24,28},{28,24},{1,5},{5... | collective-permute-start | bytes 122888 | tf_op jit(solution)/shard_map/ppermute | solution.py:634
  28.2 11.0 %collective-permute-start.4 = (f32[40,256]{1,0:T(8,128)S(1)}, f32[40,256]{1,0:T(8,128)S(1)}, u32[]{:S(2)}, u32[]{:S(2)}) collective-permute-start(f32[40,256]{1,0:T(8,128)S(1)} %shard_map.132.refs_0_), channel_id=1, source_target_pairs={{0,8},{4,12},{8,16},{12,20},{16,24},{20,28},{24,0},{28,4},{1,9},{5... | collective-permute-start | bytes 122888 | tf_op jit(solution)/shard_map/ppermute | solution.py:602
  30.0 9.2 %collective-permute-start.5 = (f32[40,256]{1,0:T(8,128)S(1)}, f32[40,256]{1,0:T(8,128)S(1)}, u32[]{:S(2)}, u32[]{:S(2)}) collective-permute-start(f32[40,256]{1,0:T(8,128)S(1)} %shard_map.132.refs_0_), channel_id=1, source_target_pairs={{0,16},{4,20},{8,24},{12,28},{16,0},{20,4},{24,8},{28,12},{1,17},{... | collective-permute-start | bytes 122888 | tf_op jit(solution)/shard_map/ppermute | solution.py:602
  32.6 6.6 %collective-permute-start.6 = (f32[40,256]{1,0:T(8,128)S(1)}, f32[40,256]{1,0:T(8,128)S(1)}, u32[]{:S(2)}, u32[]{:S(2)}) collective-permute-start(f32[40,256]{1,0:T(8,128)S(1)} %shard_map.132.refs_0_), channel_id=1, source_target_pairs={{0,24},{4,28},{8,0},{12,4},{16,8},{20,12},{24,16},{28,20},{1,25},{... | collective-permute-start | bytes 122888 | tf_op jit(solution)/shard_map/ppermute | solution.py:602
  39.4 5.2 %collective-permute-start.7 = (f32[40,256]{1,0:T(8,128)S(1)}, f32[40,256]{1,0:T(8,128)S(1)}, u32[]{:S(2)}, u32[]{:S(2)}) collective-permute-start(f32[40,256]{1,0:T(8,128)S(1)} %get-tuple-element.48.refs_0_), channel_id=1, source_target_pairs={{0,1},{1,2},{2,3},{3,0},{4,5},{5,6},{6,7},{7,4},{8,9},{9,10},{10,1... | collective-permute-start | bytes 122888 | tf_op jit(solution)/shard_map/ppermute | solution.py:602
  40.9 4.1 %collective-permute-start.8 = (f32[40,256]{1,0:T(8,128)S(1)}, f32[40,256]{1,0:T(8,128)S(1)}, u32[]{:S(2)}, u32[]{:S(2)}) collective-permute-start(f32[40,256]{1,0:T(8,128)S(1)} %get-tuple-element.48.refs_0_), channel_id=1, source_target_pairs={{0,2},{1,3},{2,0},{3,1},{4,6},{5,7},{6,4},{7,5},{8,10},{9,11},{10,... | collective-permute-start | bytes 122888 | tf_op jit(solution)/shard_map/ppermute | solution.py:602
  42.4 4.0 %collective-permute-start.9 = (f32[40,256]{1,0:T(8,128)S(1)}, f32[40,256]{1,0:T(8,128)S(1)}, u32[]{:S(2)}, u32[]{:S(2)}) collective-permute-start(f32[40,256]{1,0:T(8,128)S(1)} %get-tuple-element.48.refs_0_), channel_id=1, source_target_pairs={{0,3},{1,0},{2,1},{3,2},{4,7},{5,4},{6,5},{7,6},{8,11},{9,8},{10,9... | collective-permute-start | bytes 122888 | tf_op jit(solution)/shard_map/ppermute | solution.py:602

commit v3 on v2

--- a/solution.py
+++ b/solution.py
@@ -41,6 +41,10 @@
 
 def params(vmem_mib, side_effects=False):
     return pltpu.CompilerParams(vmem_limit_bytes=vmem_mib << 20)
+
+
+def pin(value):
+    return pltpu.with_memory_space_constraint(value, pltpu.HBM)
 
 
 def call(kernel, out_shape, in_specs, vmem_mib, out_specs=None, scratch=(), flops=0, moved=0, **more):
@@ -62,7 +66,7 @@
     return jax.ShapeDtypeStruct(shape, dtype)
 
 
-def sort_walls(count, room, me, owner_ref, value_of, table, taken):
+def sort_walls(count, room, me, walls, owner_ref, table, taken):
     for shift in range(count):
         taken[shift] = shift * room
 
@@ -71,35 +75,23 @@
         shift = jnp.where(shift < 0, shift + count, shift)
         slot = taken[shift]
         taken[shift] = slot + 1
-        table[slot] = value_of(entry)
+        table[slot] = entry
         return carry
 
-    lax.fori_loop(0, owner_ref.shape[0], step, 0, unroll=8)
-
-
-def extras(rows, shift, count):
-    return (rows // LANES if shift in (1, count - 1) else 0) + 1
-
-
-def pack_kernel(count, room, chunk, owner_ref, offset_ref, force_hbm, v_hbm, *refs):
-    outs, (force_ref, v_ref, table, taken, sem, v_sem) = refs[:count], refs[count:]
-    walls = owner_ref.shape[0]
-    rows, planes, cols = v_ref.shape
+    lax.fori_loop(0, walls, step, 0, unroll=8)
+
+
+def pack_kernel(count, room, owner_ref, offset_ref, force_hbm, *refs):
+    outs, (force_ref, table, taken, sem) = refs[:count], refs[count:]
+    walls = force_hbm.shape[0]
+    planes, width = force_hbm.shape[1:]
     me = lax.axis_index("gy")
-    steps = rows // chunk
     copy = pltpu.make_async_copy(force_hbm, force_ref.at[pl.ds(0, walls)], sem)
     copy.start()
-
-    def v_copy(k):
-        span = pl.ds(k * chunk, chunk)
-        return pltpu.make_async_copy(v_hbm.at[span], v_ref.at[span], v_sem.at[k])
-
-    for k in range(steps):
-        v_copy(k).start()
     force_ref[walls] = jnp.zeros(force_ref.shape[1:], F32)
     for slot in range(count * room):
         table[slot] = walls
-    sort_walls(count, room, me, owner_ref, lambda entry: entry, table, taken)
+    sort_walls(count, room, me, walls, owner_ref, table, taken)
     copy.wait()
     lane = lax.broadcasted_iota(jnp.int32, (planes, LANES), 1)
     for shift in list(range(1, count)) + [0]:
@@ -109,37 +101,23 @@
             outs[shift][slot] = force_ref[entry]
             place = jnp.where(entry < walls, offset_ref[jnp.minimum(entry, walls - 1)], -1)
             places = jnp.where(lane == slot, place, places)
-        outs[shift][outs[shift].shape[0] - 1] = places.astype(F32)
-    for block in range(rows // LANES):
-        first, last = jnp.zeros((planes, LANES), F32), jnp.zeros((planes, LANES), F32)
-        for x in range(LANES):
-            at = block * LANES + x
-            if at % chunk == 0:
-                v_copy(at // chunk).wait()
-            first = jnp.where(lane == x, pltpu.roll(v_ref[at, :, 0:LANES], x, 1), first)
-            last = jnp.where(lane == x, pltpu.roll(v_ref[at, :, cols - LANES : cols], (x + 1) % LANES, 1), last)
-        outs[1][room + block] = last
-        outs[count - 1][room + block] = first
-
-
-def pack(owner, offset, force, velocity, count, room):
+        outs[shift][room] = places.astype(F32)
+
+
+def pack(owner, offset, force, count, room):
     walls, planes, width = force.shape
-    rows = velocity.shape[0]
-    chunk = 64
     return call(
-        functools.partial(pack_kernel, count, room, chunk),
-        [struct(room + extras(rows, s, count), planes, width) for s in range(count)],
-        [SMEM, SMEM, HBM, HBM],
+        functools.partial(pack_kernel, count, room),
+        [struct(room + 1, planes, width) for s in range(count)],
+        [SMEM, SMEM, HBM],
         8,
         scratch=[
             pltpu.VMEM((walls + 1, planes, width), F32),
-            pltpu.VMEM(velocity.shape, F32),
             pltpu.SMEM((count * room,), jnp.int32),
             pltpu.SMEM((count,), jnp.int32),
             pltpu.SemaphoreType.DMA,
-            pltpu.SemaphoreType.DMA((rows // chunk,)),
         ],
-    )(owner, offset, force, velocity)
+    )(pin(owner), pin(offset), pin(force))
 
 
 def row(ref, index):
@@ -163,15 +141,35 @@
     return 0.5 * (before + after)
 
 
-def factor_kernel(lx, ux, lcx, ucx, ly, uy, lcy, ucy, mx, my, aux, my_t, aux_t, xrows, yrows, frows, scal):
+def factor_kernel(chunk, v_hbm, *refs):
+    given, (mx, my, aux, my_t, aux_t, xrows, yrows, frows, scal) = refs[:8], refs[8:17]
+    v_ref, edge_ref, first_ref, last_ref = refs[17:21]
+    fetched, (weight, sem, v_sem, weight_sem) = refs[21:29], refs[29:]
+    rows, planes, cols = v_ref.shape
+    copies = [pltpu.make_async_copy(given[i], fetched[i], sem.at[i]) for i in range(8)]
+    for copy in copies:
+        copy.start()
+
+    def v_copy(k):
+        span = pl.ds(k * chunk, chunk)
+        return pltpu.make_async_copy(v_hbm.at[span], v_ref.at[span], v_sem.at[k])
+
+    for k in range(rows // chunk):
+        v_copy(k).start()
+    for copy in copies:
+        copy.wait()
+    lx, ux, lcx, ucx, ly, uy, lcy, ucy = fetched
     rows_x, rows_y = lx.shape[0], ly.shape[0]
     both = f32_dot(ux[...], lx[...], ((1,), (0,)))
+    zero = jnp.zeros((1, rows_x), F32)
+    frows[...] = jnp.concatenate([row(lx, rows_x - 1), both[0:8][0:1], zero, zero, zero, zero, zero, zero], 0)
+    to_scalars = pltpu.make_async_copy(frows, weight, weight_sem)
+    to_scalars.start()
     mx[...] = left_of(half_shift_rows(both), 1)
     both_y = f32_dot(uy[...], ly[...], ((1,), (0,)))
     turned = both_y.T
     my[...] = left_of(turned, 0)
     my_t[...] = left_of(half_shift_rows(turned), 0)
-    zero = jnp.zeros((1, rows_x), F32)
     lc, uc = lcx[...], ucx[...]
     pad = jnp.zeros((7, rows_x), F32)
     u_lc = f32_dot(jnp.concatenate([lc, pad], 0), ux[...], ((1,), (1,)))[0:1]
@@ -188,12 +186,11 @@
     zero_y = jnp.zeros((1, rows_y), F32)
     m0, m1 = 0.5 * turned[0:8][0:1], 0.5 * turned[rows_y - 8 : rows_y][7:8]
     yrows[...] = jnp.concatenate([uy_lc, ucv, m0, m1, f0, f1, zero_y, zero_y], 0)
-    lane = lax.broadcasted_iota(jnp.int32, (rows_y, 128), 1)
-    cols = jnp.concatenate([f0, f1, pad_y[:6]], 0).T
-    spread_cols = jnp.where(lane < 64, cols[:, 0:1], cols[:, 1:2])
+    lane_y = lax.broadcasted_iota(jnp.int32, (rows_y, 128), 1)
+    pair_of = jnp.concatenate([f0, f1, pad_y[:6]], 0).T
+    spread_cols = jnp.where(lane_y < 64, pair_of[:, 0:1], pair_of[:, 1:2])
     aux[...] = left_of(spread_cols, 0)
     aux_t[...] = left_of(half_shift_rows(spread_cols), 0)
-    frows[...] = jnp.concatenate([row(lx, rows_x - 1), both[0:8][0:1], zero, zero, zero, zero, zero, zero], 0)
 
     def spread(value, index, width):
         return jnp.broadcast_to(value[:, index : index + 1], (1, width))
@@ -227,10 +224,32 @@
     )
 
 
-def factors(lx, ux, lcx, ucx, ly, uy, lcy, ucy):
-    rows, cols = lx.shape[0], ly.shape[0]
+    to_scalars.wait()
+    lane = lax.broadcasted_iota(jnp.int32, (planes, LANES), 1)
+    lower, upper = jnp.zeros((planes, cols), F32), jnp.zeros((planes, cols), F32)
+    for block in range(rows // LANES):
+        first, last = jnp.zeros((planes, LANES), F32), jnp.zeros((planes, LANES), F32)
+        for x in range(LANES):
+            at = block * LANES + x
+            if at % chunk == 0:
+                v_copy(at // chunk).wait()
+            value = v_ref[at]
+            lower = lower + weight[0, at] * value
+            upper = upper + weight[1, at] * value
+            first = jnp.where(lane == x, pltpu.roll(value[:, 0:LANES], x, 1), first)
+            last = jnp.where(lane == x, pltpu.roll(value[:, cols - LANES : cols], (x + 1) % LANES, 1), last)
+        first_ref[:, block * LANES : (block + 1) * LANES] = first
+        last_ref[:, block * LANES : (block + 1) * LANES] = last
+    edge_ref[0] = half_shift_lanes(lower)
+    edge_ref[1] = half_shift_lanes(upper)
+
+
+def factors(velocity, lx, ux, lcx, ucx, ly, uy, lcy, ucy):
+    rows, planes, cols = velocity.shape
+    chunk = 64
+    given = (lx, ux, lcx[None, :], ucx[None, :], ly, uy, lcy[None, :], ucy[None, :])
     return call(
-        factor_kernel,
+        functools.partial(factor_kernel, chunk),
         [
             struct(rows, 3 * rows, dtype=BF16),
             struct(3 * cols, cols, dtype=BF16),
@@ -241,32 +260,28 @@
             struct(8, cols),
             struct(8, rows),
             struct(16, rows),
+            struct(rows, planes, cols),
+            struct(2, planes, cols),
+            struct(planes, rows),
+            struct(planes, rows),
         ],
-        [VMEM] * 8,
+        [HBM] * 9,
         8,
-    )(lx, ux, lcx[None, :], ucx[None, :], ly, uy, lcy[None, :], ucy[None, :])
-
-
-def velocity_kernel(func_ref, my_t, aux_t, v_hbm, high_ref, low_ref, s_ref, edge_ref, v_ref, sem):
+        scratch=[pltpu.VMEM(g.shape, F32) for g in given]
+        + [
+            pltpu.SMEM((8, rows), F32),
+            pltpu.SemaphoreType.DMA((8,)),
+            pltpu.SemaphoreType.DMA((rows // chunk,)),
+            pltpu.SemaphoreType.DMA,
+        ],
+    )(pin(velocity), *[pin(g) for g in given])
+
+
+def velocity_kernel(chunk, mx, my_t, aux_t, v_ref, w_ref, s_ref, high_ref, low_ref):
     rows, planes, cols = v_ref.shape
-    steps = sem.shape[0]
-    chunk = rows // steps
     group = planes
-
-    def copy(k):
-        span = pl.ds(k * chunk, chunk)
-        return pltpu.make_async_copy(v_hbm.at[span], v_ref.at[span], sem.at[k])
-
-    for k in range(steps):
-        copy(k).start()
     lane = lax.broadcasted_iota(jnp.int32, (group, LANES), 1)
-    lower, upper = jnp.zeros((planes, cols), F32), jnp.zeros((planes, cols), F32)
-    for k in range(steps):
-        copy(k).wait()
-        for i in range(k * chunk, (k + 1) * chunk):
-            value = v_ref[i]
-            lower = lower + func_ref[0, i] * value
-            upper = upper + func_ref[1, i] * value
+    for k in range(rows // chunk):
         flat = right_of(v_ref[k * chunk : (k + 1) * chunk].reshape(chunk * planes, cols), 1)
         r = bf16_dot(flat, my_t[...], ((1,), (0,)))
         t = bf16_dot(flat, aux_t[...], ((1,), (0,)))
@@ -282,126 +297,110 @@
             for p in range(planes):
                 total = jnp.where((lane == p) | (lane == 64 + p), picked[p], total)
             s_ref[x, :] = total
-    edge_ref[0] = half_shift_lanes(lower)
-    edge_ref[1] = half_shift_lanes(upper)
-
-
-def velocity_part(func, my_t, aux_t, velocity):
+    for p in range(planes):
+        high = high_ref[p]
+        w_ref[p] = bf16_dot(mx[...], jnp.concatenate([high, high, low_ref[p]], 0), ((1,), (0,)))
+
+
+def velocity_part(mx, my_t, aux_t, velocity):
     rows, planes, cols = velocity.shape
-    chunk = 64
     return call(
-        velocity_kernel,
-        [
-            struct(planes, rows, cols, dtype=BF16),
-            struct(planes, rows, cols, dtype=BF16),
-            struct(rows, LANES),
-            struct(2, planes, cols),
-        ],
-        [SMEM, VMEM, VMEM, HBM],
+        functools.partial(velocity_kernel, 64),
+        [struct(planes, rows, cols), struct(rows, LANES)],
+        [VMEM] * 4,
         16,
-        scratch=[pltpu.VMEM(velocity.shape, F32), pltpu.SemaphoreType.DMA((rows // chunk,))],
-    )(func, my_t, aux_t, velocity)
-
-
-def halos(count, room, rows, payload):
+        scratch=[pltpu.VMEM((planes, rows, cols), BF16), pltpu.VMEM((planes, rows, cols), BF16)],
+    )(mx, my_t, aux_t, velocity)
+
+
+def halos(count, left_ref, right_ref):
     me = lax.axis_index("gy")
-    blocks = rows // LANES
-
-    def column(s, there):
-        value = jnp.concatenate([payload[s][room + b] for b in range(blocks)], 1)
-        return jnp.where(there, value, 0.0)
-
-    return column(1, me > 0), column(count - 1, me < count - 1)
-
-
-def x_edge_kernel(count, room, table_ref, func_ref, edge_ref, frows, scal, *refs):
-    payload, out = refs[:count], refs[count]
-    planes, cols = edge_ref.shape[1:]
+    return jnp.where(me > 0, left_ref[...], 0.0), jnp.where(me < count - 1, right_ref[...], 0.0)
+
+
+def x_edge_kernel(count, room, edge_ref, frows, scal, left_ref, right_ref, *refs):
+    payload, (out, chosen_ref, wall_ref) = refs[:count], refs[count:]
+    planes, slots, cols = wall_ref.shape
+    rows = frows.shape[1]
     width = payload[0].shape[2]
     nblock = cols // width
-    low, high = edge_ref[0], edge_ref[1]
-    at = lax.broadcasted_iota(jnp.int32, (planes, cols), 1)
-    f0, f1 = frows[0:1, :], frows[1:2, :]
-    hl, hr = halos(count, room, frows.shape[1], payload)
-    for f, which in ((f0, 0), (f1, 1)):
-        first = 0.5 * jnp.sum(hl * f, axis=1, keepdims=True)
-        last = 0.5 * jnp.sum(hr * f, axis=1, keepdims=True)
-        add = jnp.where(at == 0, first, 0.0) + jnp.where(at == cols - 1, last, 0.0)
-        if which == 0:
-            low = low + add
-        else:
-            high = high + add
-    out[2 * planes : 2 * planes + 8, :] = scal[0:8, :]
-    sums = [jnp.zeros((planes, width), F32) for _ in range(2 * nblock)]
-    for s in range(count):
-
-        def step(slot, sums):
-            sums = list(sums)
-            place = jnp.maximum(table_ref[s * room + slot], 0)
-            line, half = place // nblock, place % nblock
-            value = payload[s][slot]
-            for f in range(2):
-                weight = func_ref[f, line]
-                for b in range(nblock):
-                    sums[f * nblock + b] += jnp.where(half == b, weight, 0.0) * value
-            return tuple(sums)
-
-        sums = lax.fori_loop(0, room, step, tuple(sums), unroll=8)
-    out[0:planes, :] = low + jnp.concatenate(sums[:nblock], 1)
-    out[planes : 2 * planes, :] = high + jnp.concatenate(sums[nblock:], 1)
-
-
-def x_edges(table, func, edge, frows, scal, payload, room):
-    planes, cols = edge.shape[1:]
-    count = len(payload)
-    return call(
-        functools.partial(x_edge_kernel, count, room),
-        struct(2 * planes + 8, cols),
-        [SMEM, SMEM] + [VMEM] * (3 + count),
-        8,
-    )(table, func, edge, frows, scal, *payload)
-
-
-def sweep_kernel(count, room, mx, my, aux, yrows, high_ref, low_ref, sv_ref, *refs):
-    payload, (w_ref, s_ref, zh_ref, wall_ref) = refs[:count], refs[count:]
-    planes, rows, cols = w_ref.shape
-    slots, width = wall_ref.shape[1:]
-    nblock = cols // width
-    hl, hr = halos(count, room, rows, payload)
-    m = mx[...]
-    zh = bf16_dot(right_of(jnp.concatenate([hl, hr], 0), 1), m, ((1,), (1,)))
-    zh_ref[...] = zh
-    lane8 = lax.broadcasted_iota(jnp.int32, (8, LANES), 1)
+    lane8 = lax.broadcasted_iota(jnp.int32, (8, slots), 1)
     places = jnp.full((8, slots), -1.0, F32)
     for s in range(count):
-        here = payload[s][payload[s].shape[0] - 1][0:8]
+        here = payload[s][room][0:8]
         if s:
             here = pltpu.roll(here, s * room, 1)
         places = jnp.where((lane8 >= s * room) & (lane8 < (s + 1) * room), here, places)
     line = jnp.floor(places * (1.0 / nblock))
     half = places - nblock * line
-    column = half.T
     row_ids = lax.broadcasted_iota(jnp.int32, (rows, slots), 0).astype(F32)
-    chosen = jnp.where(row_ids == line[0:1], 1.0, 0.0).astype(BF16)
+    chosen = jnp.where(row_ids == line[0:1], 1.0, 0.0)
+    chosen_ref[...] = chosen.astype(BF16)
+    weight = f32_dot(frows[...], chosen, ((1,), (0,)))
+    sub8 = lax.broadcasted_iota(jnp.int32, (8, slots), 0)
+    column = jnp.where(sub8 == 2, half, weight).T
+    step = min(room, 16)
+    for s in range(count):
+        for g in range(room // step):
+            at = slice(s * room + g * step, s * room + (g + 1) * step)
+            value = jnp.swapaxes(payload[s][g * step : (g + 1) * step], 0, 1)
+            for b in range(nblock):
+                keep = jnp.broadcast_to(column[at, 2:3] == b, (step, width))
+                wall_ref[:, at, b * width : (b + 1) * width] = jnp.where(keep[None], value, 0.0)
+    at = lax.broadcasted_iota(jnp.int32, (planes, cols), 1)
+    hl, hr = halos(count, left_ref, right_ref)
+    for f in range(2):
+        func = frows[f : f + 1, :]
+        first = 0.5 * jnp.sum(hl * func, axis=1, keepdims=True)
+        last = 0.5 * jnp.sum(hr * func, axis=1, keepdims=True)
+        out[f * planes : (f + 1) * planes, :] = (
+            edge_ref[f] + jnp.where(at == 0, first, 0.0) + jnp.where(at == cols - 1, last, 0.0)
+        )
+    spread = [jnp.broadcast_to(column[:, f : f + 1], (slots, LANES)) for f in range(2)]
+    for p in range(planes):
+        for b in range(cols // LANES):
+            lanes = slice(b * LANES, (b + 1) * LANES)
+            value = wall_ref[p, :, lanes]
+            for f in range(2):
+                at = f * planes + p
+                out[at : at + 1, lanes] = out[at : at + 1, lanes] + jnp.sum(value * spread[f], axis=0, keepdims=True)
+    out[2 * planes : 2 * planes + 8, :] = scal[0:8, :]
+
+
+def x_edges(edge, frows, scal, left, right, payload, room):
+    planes, cols = edge.shape[1:]
+    count, rows = len(payload), frows.shape[1]
+    slots = count * room
+    return call(
+        functools.partial(x_edge_kernel, count, room),
+        [struct(2 * planes + 8, cols), struct(rows, slots, dtype=BF16), struct(planes, slots, cols)],
+        [VMEM] * (5 + count),
+        8,
+    )(edge, frows, scal, left, right, *payload)
+
+
+def wall_kernel(count, mx, aux, yrows, sv_ref, left_ref, right_ref, chosen_ref, wall_ref, s_ref, zh_ref, sel_ref):
+    planes, slots, cols = wall_ref.shape
+    rows = mx.shape[0]
+    hl, hr = halos(count, left_ref, right_ref)
+    m = mx[...]
+    zh = bf16_dot(right_of(jnp.concatenate([hl, hr], 0), 1), m, ((1,), (1,)))
+    zh_ref[...] = zh
+    chosen = chosen_ref[...]
     sel_high = bf16_dot(m[:, 0:rows], chosen, ((1,), (0,))).astype(BF16)
     sel_low = bf16_dot(m[:, rows : 2 * rows], chosen, ((1,), (0,))).astype(BF16)
-    left = jnp.concatenate([m, sel_high, sel_low, sel_high], 1)
-    keep = [jnp.broadcast_to(column[:, 0:1] == b, (slots, width)) for b in range(nblock)]
-    for s in range(count):
-        step = min(room, 16)
-        for g in range(room // step):
-            value = jnp.swapaxes(payload[s][g * step : (g + 1) * step], 0, 1)
-            wall_ref[:, s * room + g * step : s * room + (g + 1) * step, :] = value
+    sel = jnp.concatenate([sel_high, sel_low, sel_high], 1)
+    sel_ref[...] = sel
     lane = lax.broadcasted_iota(jnp.int32, (slots, LANES), 1)
     total = jnp.zeros((slots, LANES), F32)
-    for p in range(planes):
-        wall = wall_ref[p]
-        wc = right_of(jnp.concatenate([jnp.where(k, wall, 0.0) for k in keep], 1), 1)
-        r = right_of(bf16_dot(wc, my[...], ((1,), (0,))), 0)
-        t = bf16_dot(wc, aux[...], ((1,), (0,)))
-        total = jnp.where((lane == p) | (lane == 64 + p), t, total)
-        high = high_ref[p]
-        w_ref[p] = bf16_dot(left, jnp.concatenate([high, high, low_ref[p], r], 0), ((1,), (0,)))
+    some = 8
+    for q in range(0, planes, some):
+        flat = wall_ref[q : q + some].reshape(some * slots, cols)
+        t = bf16_dot(right_of(flat, 1), aux[...], ((1,), (0,)))
+        for i in range(some):
+            p = q + i
+            total = jnp.where((lane == p) | (lane == 64 + p), t[i * slots : (i + 1) * slots], total)
+    left = jnp.concatenate([m, sel], 1)
     turned = bf16_dot(left, jnp.concatenate([right_of(sv_ref[...], 0), right_of(total, 0)], 0), ((1,), (0,))).T
     low, high = turned[0:planes], turned[64 : 64 + planes]
     f0, f1 = yrows[4:5, :], yrows[5:6, :]
@@ -410,16 +409,36 @@
     s_ref[planes : 2 * planes, :] = high + 0.5 * (zl * f1[:, 0:1] + zr * f1[:, cols - 1 : cols])
 
 
-def sweep(mx, my, aux, yrows, high, low, sv, payload, room):
-    planes, rows, cols = high.shape
-    count, width = len(payload), payload[0].shape[2]
+def wall_edges(count, mx, aux, yrows, sv, left, right, chosen, wall):
+    rows = mx.shape[0]
+    planes, slots, cols = wall.shape
     return call(
-        functools.partial(sweep_kernel, count, room),
-        [struct(planes, rows, cols), struct(2 * planes, rows), struct(2 * planes, rows)],
-        [VMEM] * (7 + count),
-        16,
-        scratch=[pltpu.VMEM((planes, count * room, width), F32)],
-    )(mx, my, aux, yrows, high, low, sv, *payload)
+        functools.partial(wall_kernel, count),
+        [struct(2 * planes, rows), struct(2 * planes, rows), struct(rows, 3 * slots, dtype=BF16)],
+        [VMEM] * 8,
+        8,
+    )(mx, aux, yrows, sv, left, right, chosen, wall)
+
+
+def wall_sweep_kernel(my, sel, wall_ref, v_ref, w_ref):
+    planes, slots, cols = wall_ref.shape
+    some = 8
+    for q in range(0, planes, some):
+        flat = wall_ref[q : q + some].reshape(some * slots, cols)
+        r = bf16_dot(right_of(flat, 1), my[...], ((1,), (0,)))
+        for i in range(some):
+            here = right_of(r[i * slots : (i + 1) * slots], 0)
+            w_ref[q + i] = v_ref[q + i] + bf16_dot(sel[...], here, ((1,), (0,)))
+
+
+def wall_sweep(my, sel, wall, w):
+    return call(
+        wall_sweep_kernel,
+        struct(*w.shape),
+        [VMEM] * 4,
+        8,
+        input_output_aliases={3: 0},
+    )(my, sel, wall, w)
 
 
 def chain(parts, count, me, planes, f_in):
@@ -517,9 +536,11 @@
     planes, rows, cols = w_ref.shape
     halves = out_ref.shape[0]
 
+    piece = 32 * planes
+
     def out_copy(k, b):
-        span = pl.ds(k * part * planes, part * planes)
-        return pltpu.make_async_copy(out_ref.at[b, span, :], out_hbm.at[span, pl.ds(b * 128, 128)], out_sem.at[k, b])
+        span = pl.ds(k * piece, piece)
+        return pltpu.make_async_copy(out_ref.at[b, span, :], out_hbm.at[span, pl.ds(b * LANES, LANES)], out_sem.at[k, b])
 
     steps = rows // part
     gather_parts(me, parts, received)
@@ -562,14 +583,14 @@
             value = w_ref[p, lo : lo + part, :] + bf16_dot(lc, rc, ((0,), (0,)))
             for b in range(halves):
                 value_ref[b, p] = jnp.where(fluid[b], value[:, b * LANES : (b + 1) * LANES], 0.0)
-        for b in range(halves):
-            for g in range(part // planes):
+        for g in range(part // planes):
+            at = (lo + g * planes) * planes
+            for b in range(halves):
                 turned = jnp.swapaxes(value_ref[b, :, g * planes : (g + 1) * planes, :], 0, 1)
-                at = (lo + g * planes) * planes
                 out_ref[b, at : at + planes * planes, :] = turned.reshape(planes * planes, LANES)
-        for b in range(halves):
-            out_copy(k, b).start()
-    for k in range(steps):
+                if (at + planes * planes) % piece == 0:
+                    out_copy(at // piece, b).start()
+    for k in range(rows * planes // piece):
         for b in range(halves):
             out_copy(k, b).wait()
 
@@ -591,7 +612,7 @@
             pltpu.VMEM((2, planes, rows), F32),
             pltpu.VMEM((halves, planes, part, LANES), F32),
             pltpu.VMEM((halves, rows * planes, 128), F32),
-            pltpu.SemaphoreType.DMA((rows // part, halves)),
+            pltpu.SemaphoreType.DMA((rows // 32, halves)),
         ],
     )(xrows, yrows, moved, solid, zh, w, *received)
     return out.reshape(rows, planes, cols)
@@ -621,22 +642,30 @@
     walls = wall_force.shape[0]
     n_x, n_y = lax.axis_size("gx"), lax.axis_size("gy")
     room = 2 * walls // n_y
-    owner = wall_owner[:, 0]
-    packed = pack(owner, wall_offset, wall_force, velocity, n_y, room)
+    packed = pack(wall_owner[:, 0], wall_offset, wall_force, n_y, room)
     payload = [packed[0]] + [rotate(packed[s], "gy", s) for s in range(1, n_y)]
-    table = jnp.concatenate([v[-1, 0, :room] for v in payload]).astype(jnp.int32)
-    mx, my, aux, my_t, aux_t, xrows, yrows, frows, scal = factors(
-        lower_x, upper_x, lower_carry_x, upper_carry_x, lower_y, upper_y, lower_carry_y, upper_carry_y
+    mx, my, aux, my_t, aux_t, xrows, yrows, frows, scal, v, edge, first, last = factors(
+        velocity,
+        lower_x,
+        upper_x,
+        lower_carry_x,
+        upper_carry_x,
+        lower_y,
+        upper_y,
+        lower_carry_y,
+        upper_carry_y,
     )
-    func = frows[0:2]
-    high, low, sv, edge = velocity_part(func, my_t, aux_t, velocity)
-    mine = x_edges(table, func, edge, frows, scal, payload, room)
+    left, right = rotate(last, "gy", 1), rotate(first, "gy", -1)
+    w, sv = velocity_part(mx, my_t, aux_t, v)
+    w, sv, edge = lax.optimization_barrier((w, sv, edge))
+    mine, chosen, wall = x_edges(edge, frows, scal, left, right, payload, room)
     other = lax.ppermute(mine, "gx", [(i, i ^ 1) for i in range(n_x)])
     both = pair(mine, other)
     received = [both] + [rotate(both, "gx", 2 * s) for s in range(1, n_x // 2)]
-    w, s_edge, zh = sweep(mx, my, aux, yrows, high, low, sv, payload, room)
+    s_edge, zh, sel = wall_edges(n_y, mx, aux, yrows, sv, left, right, chosen, wall)
     mine, moved = x_join(my, xrows, yrows, scal, s_edge, mine, other, received)
     received = [mine] + [rotate(mine, "gy", s) for s in range(1, n_y)]
+    w = wall_sweep(my, sel, wall, w)
     return finish(xrows, yrows, moved, solid_mask.T, zh, w, received)
 
 

time: 50 us -> 42 us (0.84)
  local copies, waits for them, and re-layouts: 6.49 us -> 0.01 us
  waiting for transfers between devices: 5.4 us -> 2.45 us
  starting transfers between devices: 16.2 us -> 18 us
    unnamed x28 -> x2, local copies, waits for them, and re-layouts: 6.48 us -> 0.01 us
    ppermute x9 -> x11, waiting for transfers between devices: 4.2 us -> 1.25 us  [rotate(): lax.ppermute(value, axis, [(i, (i + shift) % count) for i in range(count)])]
    ppermute x9 -> x11, starting transfers between devices: 16.2 us -> 17.9 us  [rotate(): lax.ppermute(value, axis, [(i, (i + shift) % count) for i in range(count)])]
    pallas_call x5 -> x6, Pallas kernels: 17.8 us -> 17.7 us  [the longest x1 5.35 us: velocity_part(): call(functools.partial(velocity_kernel, 64), [struct(planes, rows, cols),...]
  transfers between devices with their start and end apart: 10 -> 12, of which waited for: 5 -> 3; matrix products, arithmetic and copies ran while one was open for 0% -> 0% of each run, Pallas kernels for 26% -> 35%
where the time goes in v3:
time: 42 us; the launch traced here: 41.8 us
  Pallas kernels  21.1 us (50%)
  starting transfers between devices  18 us (43%)
  waiting for transfers between devices  2.45 us (6%)
    ppermute x11, starting transfers between devices, rotate(): lax.ppermute(value, axis, [(i, (i + shift) % count) for i in range(count)])  17.9 us
    pallas_call x1, Pallas kernels, velocity_part(): call(functools.partial(velocity_kernel, 64), [struct(planes, rows, cols),...  5.35 us
    pallas_call x1, Pallas kernels, factors(): call(functools.partial(factor_kernel, chunk), [struct(rows, 3 * rows, dty...  4.85 us
    pallas_call x1, Pallas kernels, finish(): call(functools.partial(finish_kernel, count, part), struct(rows * planes,...  3.11 us
    pallas_call x1, Pallas kernels, wall_sweep(): call(wall_sweep_kernel, struct(*w.shape), [VMEM] * 4, 8, input_output_ali...  2.99 us
    pallas_call x1, Pallas kernels, pack(): call(functools.partial(pack_kernel, count, room), [struct(room + 1, plane...  2.04 us
    pallas_call x1, Pallas kernels, wall_edges(): call(functools.partial(wall_kernel, count), [struct(2 * planes, rows), st...  1.41 us
    ppermute x11, waiting for transfers between devices, rotate(): lax.ppermute(value, axis, [(i, (i + shift) % count) for i in range(count)])  1.25 us
  transfers between devices with their start and end apart: 12, of which 3 were waited for; matrix products, arithmetic and copies ran while one was open for 0% of the time, Pallas kernels for 35%

profile of v3, /device:TPU:0, one launch (start us, length us, event | category | flops | bytes accessed | tf_op | source)
XLA Modules:
  0.0 41.8 jit_solution(16931764888976938490)
XLA Ops:
  0.0 2.0 %shard_map.129 = (f32[33,16,128]{2,1,0:T(8,128)S(1)}, f32[33,16,128]{2,1,0:T(8,128)S(1)}, f32[33,16,128]{2,1,0:T(8,128)S(1)}, f32[33,16,128]{2,1,0:T(8,128)S(1)}) custom-call(s32[64]{0:T(128)} %bitcast.12, s32[64]{0:T(128)} %offset_ref.1, f32[64,16,128]{2,1,0:T(8,128)} %force_hbm.1), custom_call_target="tpu_custom_call" | custom-call | tf_op jit(solution)/shard_map/pallas_call | solution.py:109
  2.0 3.0 %collective-permute-start.2 = (f32[33,16,128]{2,1,0:T(8,128)S(1)}, f32[33,16,128]{2,1,0:T(8,128)S(1)}, u32[]{:S(2)}, u32[]{:S(2)}) collective-permute-start(f32[33,16,128]{2,1,0:T(8,128)S(1)} %get-tuple-element.53), channel_id=1, source_target_pairs={{0,1},{1,2},{2,3},{3,0},{4,5},{5,6},{6,7},{7,4},{8,9},{9,10},{10,1... | collective-permute-start | bytes 811016 | tf_op jit(solution)/shard_map/ppermute | solution.py:623
  5.0 1.5 %collective-permute-start.3 = (f32[33,16,128]{2,1,0:T(8,128)S(1)}, f32[33,16,128]{2,1,0:T(8,128)S(1)}, u32[]{:S(2)}, u32[]{:S(2)}) collective-permute-start(f32[33,16,128]{2,1,0:T(8,128)S(1)} %get-tuple-element.54), channel_id=1, source_target_pairs={{0,2},{1,3},{2,0},{3,1},{4,6},{5,7},{6,4},{7,5},{8,10},{9,11},{10,... | collective-permute-start | bytes 811016 | tf_op jit(solution)/shard_map/ppermute | solution.py:623
  6.6 1.4 %collective-permute-start.4 = (f32[33,16,128]{2,1,0:T(8,128)S(1)}, f32[33,16,128]{2,1,0:T(8,128)S(1)}, u32[]{:S(2)}, u32[]{:S(2)}) collective-permute-start(f32[33,16,128]{2,1,0:T(8,128)S(1)} %get-tuple-element.55), channel_id=1, source_target_pairs={{0,3},{1,0},{2,1},{3,2},{4,7},{5,4},{6,5},{7,6},{8,11},{9,8},{10,9... | collective-permute-start | bytes 811016 | tf_op jit(solution)/shard_map/ppermute | solution.py:623
  8.0 4.8 %shard_map.127 = (bf16[256,768]{1,0:T(8,128)(2,1)S(1)}, bf16[768,256]{1,0:T(8,128)(2,1)S(1)}, bf16[768,128]{1,0:T(8,128)(2,1)S(1)}, bf16[768,256]{1,0:T(8,128)(2...) custom-call(f32[256,16,256]{2,1,0:T(8,128)} %v_hbm.1, ...), custom_call_target="tpu_custom_call" | custom-call | tf_op jit(solution)/shard_map/pallas_call | solution.py:251
  12.8 0.6 %collective-permute-start = (f32[16,256]{1,0:T(8,128)S(1)}, f32[16,256]{1,0:T(8,128)S(1)}, u32[]{:S(2)}, u32[]{:S(2)}) collective-permute-start(f32[16,256]{1,0:T(8,128)S(1)} %get-tuple-element.48), channel_id=1, source_target_pairs={{0,1},{1,2},{2,3},{3,0},{4,5},{5,6},{6,7},{7,4},{8,9},{9,10},{10,1... | collective-permute-start | bytes 49160 | tf_op jit(solution)/shard_map/ppermute | solution.py:623
  13.5 2.3 %collective-permute-start.1 = (f32[16,256]{1,0:T(8,128)S(1)}, f32[16,256]{1,0:T(8,128)S(1)}, u32[]{:S(2)}, u32[]{:S(2)}) collective-permute-start(f32[16,256]{1,0:T(8,128)S(1)} %get-tuple-element.49), channel_id=1, source_target_pairs={{0,3},{1,0},{2,1},{3,2},{4,7},{5,4},{6,5},{7,6},{8,11},{9,8},{10,9... | collective-permute-start | bytes 49160 | tf_op jit(solution)/shard_map/ppermute | solution.py:623
  15.8 5.3 %shard_map.128 = (f32[16,256,256]{2,1,0:T(8,128)S(1)}, f32[256,128]{1,0:T(8,128)S(1)}) custom-call(bf16[256,768]{1,0:T(8,128)(2,1)S(1)} %get-tuple-element.39.mx, bf16[768,256]{1,0:T(8,128)(2,1)S(1)} %get-tuple-element.41.my_t, bf16[768,128]{1,0:T(8,128)(2,1)S(1)} %get-tuple-element.42.aux_t, f32[256,16,256]{2,1,0:T(8,128)S(1)} %get-tuple-element.43.v_ref), custom_call_target="tpu_custom_call" | custom-call | tf_op jit(solution)/shard_map/pallas_call | solution.py:307
  21.2 1.1 %shard_map.130 = (f32[40,256]{1,0:T(8,128)S(1)}, bf16[256,128]{1,0:T(8,128)(2,1)S(1)}, f32[16,128,256]{2,1,0:T(8,128)S(1)}) custom-call(f32[2,16,256]{2,1,0:T(8,128)S(1)} %get-tuple-element.50.edge_ref, f32[8,256]{1,0:T(8,128)S(1)} %get-tuple-element.51.frows, f32[16,256]{1,0:T(8,128)S(1)} %get-tuple-element.38.scal, ...), custom_call_target="tpu_custom_call" | custom-call | tf_op jit(solution)/shard_map/pallas_call | solution.py:374
  22.3 0.1 collective-permute-start.5
  22.4 1.2 %collective-permute-done.5.other.other_ref = f32[40,256]{1,0:T(8,128)S(1)} collective-permute-done((f32[40,256]{1,0:T(8,128)S(1)}, f32[40,256]{1,0:T(8,128)S(1)}, u32[]{:S(2)}, u32[]{:S(2)}) %collective-permute-start.5) | collective-permute-done | bytes 40992 | tf_op jit(solution)/shard_map/ppermute | solution.py:662
  23.6 1.6 %collective-permute-start.6 = (f32[40,256]{1,0:T(8,128)S(1)}, f32[40,256]{1,0:T(8,128)S(1)}, u32[]{:S(2)}, u32[]{:S(2)}) collective-permute-start(f32[40,256]{1,0:T(8,128)S(1)} %shard_map.132.refs_0_), channel_id=1, source_target_pairs={{0,8},{4,12},{8,16},{12,20},{16,24},{20,28},{24,0},{28,4},{1,9},{5... | collective-permute-start | bytes 122888 | tf_op jit(solution)/shard_map/ppermute | solution.py:623
  25.3 2.6 %collective-permute-start.7 = (f32[40,256]{1,0:T(8,128)S(1)}, f32[40,256]{1,0:T(8,128)S(1)}, u32[]{:S(2)}, u32[]{:S(2)}) collective-permute-start(f32[40,256]{1,0:T(8,128)S(1)} %shard_map.132.refs_0_), channel_id=1, source_target_pairs={{0,16},{4,20},{8,24},{12,28},{16,0},{20,4},{24,8},{28,12},{1,17},{... | collective-permute-start | bytes 122888 | tf_op jit(solution)/shard_map/ppermute | solution.py:623
  27.8 1.3 %collective-permute-start.8 = (f32[40,256]{1,0:T(8,128)S(1)}, f32[40,256]{1,0:T(8,128)S(1)}, u32[]{:S(2)}, u32[]{:S(2)}) collective-permute-start(f32[40,256]{1,0:T(8,128)S(1)} %shard_map.132.refs_0_), channel_id=1, source_target_pairs={{0,24},{4,28},{8,0},{12,4},{16,8},{20,12},{24,16},{28,20},{1,25},{... | collective-permute-start | bytes 122888 | tf_op jit(solution)/shard_map/ppermute | solution.py:623
  29.2 1.4 %shard_map.131 = (f32[32,256]{1,0:T(8,128)S(1)}, f32[32,256]{1,0:T(8,128)S(1)}, bf16[256,384]{1,0:T(8,128)(2,1)S(1)}) custom-call(bf16[256,768]{1,0:T(8,128)(2,1)S(1)} %get-tuple-element.39.mx, bf16[768,128]{1,0:T(8,128)(2,1)S(1)} %get-tuple-element.40.aux, f32[8,256]{1,0:T(8,128)S(1)} %get-tuple-element.36.yrows, f32[256,128]{1,0:T(8,128)S(1)} %get-tuple-element.47.sv_ref, ...), custom_call_target="tpu_custom_call" | custom-call | tf_op jit(solution)/shard_map/pallas_call | solution.py:415
  30.6 0.0 collective-permute-done.6.refs_1_
  30.6 0.8 %collective-permute-done.7.refs_2_ = f32[40,256]{1,0:T(8,128)S(1)} collective-permute-done((f32[40,256]{1,0:T(8,128)S(1)}, f32[40,256]{1,0:T(8,128)S(1)}, u32[]{:S(2)}, u32[]{:S(2)}) %collective-permute-start.7) | collective-permute-done | bytes 40992 | tf_op jit(solution)/shard_map/ppermute | solution.py:623
  31.4 0.5 %collective-permute-done.8.refs_3_ = f32[40,256]{1,0:T(8,128)S(1)} collective-permute-done((f32[40,256]{1,0:T(8,128)S(1)}, f32[40,256]{1,0:T(8,128)S(1)}, u32[]{:S(2)}, u32[]{:S(2)}) %collective-permute-start.8) | collective-permute-done | bytes 40992 | tf_op jit(solution)/shard_map/ppermute | solution.py:623
  31.8 0.2 shard_map.133
  32.1 0.0 collective-permute-start.9
  32.1 0.6 %collective-permute-start.10 = (f32[40,256]{1,0:T(8,128)S(1)}, f32[40,256]{1,0:T(8,128)S(1)}, u32[]{:S(2)}, u32[]{:S(2)}) collective-permute-start(f32[40,256]{1,0:T(8,128)S(1)} %get-tuple-element.64.refs_0_), channel_id=1, source_target_pairs={{0,2},{1,3},{2,0},{3,1},{4,6},{5,7},{6,4},{7,5},{8,10},{9,11},{10,... | collective-permute-start | bytes 122888 | tf_op jit(solution)/shard_map/ppermute | solution.py:623
  32.7 2.8 %collective-permute-start.11 = (f32[40,256]{1,0:T(8,128)S(1)}, f32[40,256]{1,0:T(8,128)S(1)}, u32[]{:S(2)}, u32[]{:S(2)}) collective-permute-start(f32[40,256]{1,0:T(8,128)S(1)} %get-tuple-element.64.refs_0_), channel_id=1, source_target_pairs={{0,3},{1,0},{2,1},{3,2},{4,7},{5,4},{6,5},{7,6},{8,11},{9,8},{10,9... | collective-permute-start | bytes 122888 | tf_op jit(solution)/shard_map/ppermute | solution.py:623
  35.5 3.0 %shard_map.134.w_ref = f32[16,256,256]{2,1,0:T(8,128)S(1)} custom-call(bf16[768,256]{1,0:T(8,128)(2,1)S(1)} %get-tuple-element.37.my, bf16[256,384]{1,0:T(8,128)(2,1)S(1)} %get-tuple-element.62.sel, f32[16,128,256]{2,1,0:T(8,128)S(1)} %get-tuple-element.57.wall_ref, f32[16,256,256]{2,1,0:T(8,128)S(1)} %get-tuple-element.63.v_ref), custom_call_target="tpu_custom_call", output_to_operand_aliasing={{}: (3, {})} | custom-call | tf_op jit(solution)/shard_map/pallas_call | solution.py:435
  38.6 3.1 %shard_map.135 = f32[4096,256]{1,0:T(8,128)} custom-call(f32[8,256]{1,0:T(8,128)S(1)} %get-tuple-element.35.xrows, f32[8,256]{1,0:T(8,128)S(1)} %get-tuple-element.36.yrows, f32[48,256]{1,0:T(8,128)S(1)} %get-tuple-element.60.moved, s32[2,256]{1,0:T(2,128)S(1)} %bitcast.7, f32[32,256]{1,0:T(8,128)S(1)} %get-tuple-element.61.zh_ref, ...), custom_call_target="tpu_custom_call" | custom-call | tf_op jit(solution)/shard_map/pallas_call | solution.py:603
  (11 shorter events, 0.0 us)
Async XLA Ops:
  2.0 19.2 %collective-permute-start.2 = (f32[33,16,128]{2,1,0:T(8,128)S(1)}, f32[33,16,128]{2,1,0:T(8,128)S(1)}, u32[]{:S(2)}, u32[]{:S(2)}) collective-permute-start(f32[33,16,128]{2,1,0:T(8,128)S(1)} %get-tuple-element.53), channel_id=1, source_target_pairs={{0,1},{1,2},{2,3},{3,0},{4,5},{5,6},{6,7},{7,4},{8,9},{9,10},{10,1... | collective-permute-start | bytes 811016 | tf_op jit(solution)/shard_map/ppermute | solution.py:623
  5.0 16.2 %collective-permute-start.3 = (f32[33,16,128]{2,1,0:T(8,128)S(1)}, f32[33,16,128]{2,1,0:T(8,128)S(1)}, u32[]{:S(2)}, u32[]{:S(2)}) collective-permute-start(f32[33,16,128]{2,1,0:T(8,128)S(1)} %get-tuple-element.54), channel_id=1, source_target_pairs={{0,2},{1,3},{2,0},{3,1},{4,6},{5,7},{6,4},{7,5},{8,10},{9,11},{10,... | collective-permute-start | bytes 811016 | tf_op jit(solution)/shard_map/ppermute | solution.py:623
  6.6 14.7 %collective-permute-start.4 = (f32[33,16,128]{2,1,0:T(8,128)S(1)}, f32[33,16,128]{2,1,0:T(8,128)S(1)}, u32[]{:S(2)}, u32[]{:S(2)}) collective-permute-start(f32[33,16,128]{2,1,0:T(8,128)S(1)} %get-tuple-element.55), channel_id=1, source_target_pairs={{0,3},{1,0},{2,1},{3,2},{4,7},{5,4},{6,5},{7,6},{8,11},{9,8},{10,9... | collective-permute-start | bytes 811016 | tf_op jit(solution)/shard_map/ppermute | solution.py:623
  12.8 8.3 %collective-permute-start = (f32[16,256]{1,0:T(8,128)S(1)}, f32[16,256]{1,0:T(8,128)S(1)}, u32[]{:S(2)}, u32[]{:S(2)}) collective-permute-start(f32[16,256]{1,0:T(8,128)S(1)} %get-tuple-element.48), channel_id=1, source_target_pairs={{0,1},{1,2},{2,3},{3,0},{4,5},{5,6},{6,7},{7,4},{8,9},{9,10},{10,1... | collective-permute-start | bytes 49160 | tf_op jit(solution)/shard_map/ppermute | solution.py:623
  13.5 7.7 %collective-permute-start.1 = (f32[16,256]{1,0:T(8,128)S(1)}, f32[16,256]{1,0:T(8,128)S(1)}, u32[]{:S(2)}, u32[]{:S(2)}) collective-permute-start(f32[16,256]{1,0:T(8,128)S(1)} %get-tuple-element.49), channel_id=1, source_target_pairs={{0,3},{1,0},{2,1},{3,2},{4,7},{5,4},{6,5},{7,6},{8,11},{9,8},{10,9... | collective-permute-start | bytes 49160 | tf_op jit(solution)/shard_map/ppermute | solution.py:623
  22.3 1.3 %collective-permute-start.5 = (f32[40,256]{1,0:T(8,128)S(1)}, f32[40,256]{1,0:T(8,128)S(1)}, u32[]{:S(2)}, u32[]{:S(2)}) collective-permute-start(f32[40,256]{1,0:T(8,128)S(1)} %get-tuple-element.59.mine.mine_ref), channel_id=1, source_target_pairs={{0,4},{4,0},{8,12},{12,8},{16,20},{20,16},{24,28},{28,24},{1,5},{5... | collective-permute-start | bytes 122888 | tf_op jit(solution)/shard_map/ppermute | solution.py:662
  23.6 7.0 %collective-permute-start.6 = (f32[40,256]{1,0:T(8,128)S(1)}, f32[40,256]{1,0:T(8,128)S(1)}, u32[]{:S(2)}, u32[]{:S(2)}) collective-permute-start(f32[40,256]{1,0:T(8,128)S(1)} %shard_map.132.refs_0_), channel_id=1, source_target_pairs={{0,8},{4,12},{8,16},{12,20},{16,24},{20,28},{24,0},{28,4},{1,9},{5... | collective-permute-start | bytes 122888 | tf_op jit(solution)/shard_map/ppermute | solution.py:623
  25.3 6.1 %collective-permute-start.7 = (f32[40,256]{1,0:T(8,128)S(1)}, f32[40,256]{1,0:T(8,128)S(1)}, u32[]{:S(2)}, u32[]{:S(2)}) collective-permute-start(f32[40,256]{1,0:T(8,128)S(1)} %shard_map.132.refs_0_), channel_id=1, source_target_pairs={{0,16},{4,20},{8,24},{12,28},{16,0},{20,4},{24,8},{28,12},{1,17},{... | collective-permute-start | bytes 122888 | tf_op jit(solution)/shard_map/ppermute | solution.py:623
  27.8 4.0 %collective-permute-start.8 = (f32[40,256]{1,0:T(8,128)S(1)}, f32[40,256]{1,0:T(8,128)S(1)}, u32[]{:S(2)}, u32[]{:S(2)}) collective-permute-start(f32[40,256]{1,0:T(8,128)S(1)} %shard_map.132.refs_0_), channel_id=1, source_target_pairs={{0,24},{4,28},{8,0},{12,4},{16,8},{20,12},{24,16},{28,20},{1,25},{... | collective-permute-start | bytes 122888 | tf_op jit(solution)/shard_map/ppermute | solution.py:623
  32.1 6.5 %collective-permute-start.9 = (f32[40,256]{1,0:T(8,128)S(1)}, f32[40,256]{1,0:T(8,128)S(1)}, u32[]{:S(2)}, u32[]{:S(2)}) collective-permute-start(f32[40,256]{1,0:T(8,128)S(1)} %get-tuple-element.64.refs_0_), channel_id=1, source_target_pairs={{0,1},{1,2},{2,3},{3,0},{4,5},{5,6},{6,7},{7,4},{8,9},{9,10},{10,1... | collective-permute-start | bytes 122888 | tf_op jit(solution)/shard_map/ppermute | solution.py:623
  32.1 6.4 %collective-permute-start.10 = (f32[40,256]{1,0:T(8,128)S(1)}, f32[40,256]{1,0:T(8,128)S(1)}, u32[]{:S(2)}, u32[]{:S(2)}) collective-permute-start(f32[40,256]{1,0:T(8,128)S(1)} %get-tuple-element.64.refs_0_), channel_id=1, source_target_pairs={{0,2},{1,3},{2,0},{3,1},{4,6},{5,7},{6,4},{7,5},{8,10},{9,11},{10,... | collective-permute-start | bytes 122888 | tf_op jit(solution)/shard_map/ppermute | solution.py:623
  32.7 5.9 %collective-permute-start.11 = (f32[40,256]{1,0:T(8,128)S(1)}, f32[40,256]{1,0:T(8,128)S(1)}, u32[]{:S(2)}, u32[]{:S(2)}) collective-permute-start(f32[40,256]{1,0:T(8,128)S(1)} %get-tuple-element.64.refs_0_), channel_id=1, source_target_pairs={{0,3},{1,0},{2,1},{3,2},{4,7},{5,4},{6,5},{7,6},{8,11},{9,8},{10,9... | collective-permute-start | bytes 122888 | tf_op jit(solution)/shard_map/ppermute | solution.py:623
  35.5 3.0 %copy-start = (s32[256,2]{0,1:T(2,128)S(1)}, s32[256,2]{0,1:T(2,128)}, u32[]{:S(2)}) copy-start(s32[256,2]{0,1:T(2,128)} %param.25) | copy-start | bytes 6148

commit v4 on v3

--- a/solution.py
+++ b/solution.py
@@ -14,6 +14,7 @@
 SMEM = pl.BlockSpec(memory_space=pltpu.SMEM)
 HBM = pl.BlockSpec(memory_space=pltpu.HBM)
 LANES = 128
+GROUP = 4
 
 
 def f32_dot(left, right, dims):
@@ -141,21 +142,20 @@
     return 0.5 * (before + after)
 
 
-def factor_kernel(chunk, v_hbm, *refs):
+def factor_kernel(v_hbm, *refs):
     given, (mx, my, aux, my_t, aux_t, xrows, yrows, frows, scal) = refs[:8], refs[8:17]
     v_ref, edge_ref, first_ref, last_ref = refs[17:21]
-    fetched, (weight, sem, v_sem, weight_sem) = refs[21:29], refs[29:]
-    rows, planes, cols = v_ref.shape
+    fetched, (sem, v_sem) = refs[21:29], refs[29:]
+    planes, rows, cols = v_ref.shape
     copies = [pltpu.make_async_copy(given[i], fetched[i], sem.at[i]) for i in range(8)]
     for copy in copies:
         copy.start()
 
-    def v_copy(k):
-        span = pl.ds(k * chunk, chunk)
-        return pltpu.make_async_copy(v_hbm.at[span], v_ref.at[span], v_sem.at[k])
-
-    for k in range(rows // chunk):
-        v_copy(k).start()
+    def v_copy(p):
+        return pltpu.make_async_copy(v_hbm.at[:, p, :], v_ref.at[p], v_sem.at[p])
+
+    for p in range(planes):
+        v_copy(p).start()
     for copy in copies:
         copy.wait()
     lx, ux, lcx, ucx, ly, uy, lcy, ucy = fetched
@@ -163,8 +163,6 @@
     both = f32_dot(ux[...], lx[...], ((1,), (0,)))
     zero = jnp.zeros((1, rows_x), F32)
     frows[...] = jnp.concatenate([row(lx, rows_x - 1), both[0:8][0:1], zero, zero, zero, zero, zero, zero], 0)
-    to_scalars = pltpu.make_async_copy(frows, weight, weight_sem)
-    to_scalars.start()
     mx[...] = left_of(half_shift_rows(both), 1)
     both_y = f32_dot(uy[...], ly[...], ((1,), (0,)))
     turned = both_y.T
@@ -224,32 +222,34 @@
     )
 
 
-    to_scalars.wait()
-    lane = lax.broadcasted_iota(jnp.int32, (planes, LANES), 1)
-    lower, upper = jnp.zeros((planes, cols), F32), jnp.zeros((planes, cols), F32)
-    for block in range(rows // LANES):
-        first, last = jnp.zeros((planes, LANES), F32), jnp.zeros((planes, LANES), F32)
-        for x in range(LANES):
-            at = block * LANES + x
-            if at % chunk == 0:
-                v_copy(at // chunk).wait()
-            value = v_ref[at]
-            lower = lower + weight[0, at] * value
-            upper = upper + weight[1, at] * value
-            first = jnp.where(lane == x, pltpu.roll(value[:, 0:LANES], x, 1), first)
-            last = jnp.where(lane == x, pltpu.roll(value[:, cols - LANES : cols], (x + 1) % LANES, 1), last)
-        first_ref[:, block * LANES : (block + 1) * LANES] = first
-        last_ref[:, block * LANES : (block + 1) * LANES] = last
-    edge_ref[0] = half_shift_lanes(lower)
-    edge_ref[1] = half_shift_lanes(upper)
+    column = frows[...].T
+    weights = [jnp.broadcast_to(column[:, f : f + 1], (rows, LANES)) for f in range(2)]
+    lane = lax.broadcasted_iota(jnp.int32, (rows, LANES), 1)
+    ends = jnp.zeros((rows, LANES), F32)
+    for p in range(planes):
+        if p % GROUP == 0:
+            for here in range(p, p + GROUP):
+                v_copy(here).wait()
+        for b in range(cols // LANES):
+            lanes = slice(b * LANES, (b + 1) * LANES)
+            value = v_ref[p, :, lanes]
+            for f in range(2):
+                edge_ref[f, p : p + 1, lanes] = jnp.sum(value * weights[f], axis=0, keepdims=True)
+        ends = jnp.where(lane == p, pltpu.roll(v_ref[p, :, 0:LANES], p, 1), ends)
+        to = planes + p
+        ends = jnp.where(lane == to, pltpu.roll(v_ref[p, :, cols - LANES : cols], (to + 1) % LANES, 1), ends)
+    for f in range(2):
+        edge_ref[f] = half_shift_lanes(edge_ref[f])
+    turned_ends = ends.T
+    first_ref[...] = turned_ends[0:planes]
+    last_ref[...] = turned_ends[planes : 2 * planes]
 
 
 def factors(velocity, lx, ux, lcx, ucx, ly, uy, lcy, ucy):
     rows, planes, cols = velocity.shape
-    chunk = 64
     given = (lx, ux, lcx[None, :], ucx[None, :], ly, uy, lcy[None, :], ucy[None, :])
     return call(
-        functools.partial(factor_kernel, chunk),
+        factor_kernel,
         [
             struct(rows, 3 * rows, dtype=BF16),
             struct(3 * cols, cols, dtype=BF16),
@@ -260,7 +260,7 @@
             struct(8, cols),
             struct(8, rows),
             struct(16, rows),
-            struct(rows, planes, cols),
+            struct(planes, rows, cols),
             struct(2, planes, cols),
             struct(planes, rows),
             struct(planes, rows),
@@ -269,47 +269,35 @@
         8,
         scratch=[pltpu.VMEM(g.shape, F32) for g in given]
         + [
-            pltpu.SMEM((8, rows), F32),
             pltpu.SemaphoreType.DMA((8,)),
-            pltpu.SemaphoreType.DMA((rows // chunk,)),
-            pltpu.SemaphoreType.DMA,
+            pltpu.SemaphoreType.DMA((planes,)),
         ],
     )(pin(velocity), *[pin(g) for g in given])
 
 
-def velocity_kernel(chunk, mx, my_t, aux_t, v_ref, w_ref, s_ref, high_ref, low_ref):
-    rows, planes, cols = v_ref.shape
-    group = planes
-    lane = lax.broadcasted_iota(jnp.int32, (group, LANES), 1)
-    for k in range(rows // chunk):
-        flat = right_of(v_ref[k * chunk : (k + 1) * chunk].reshape(chunk * planes, cols), 1)
+def velocity_kernel(some, mx, my_t, aux_t, v_ref, w_ref, s_ref):
+    planes, rows, cols = v_ref.shape
+    lane = lax.broadcasted_iota(jnp.int32, (rows, LANES), 1)
+    total = jnp.zeros((rows, LANES), F32)
+    for q in range(0, planes, some):
+        flat = right_of(v_ref[q : q + some].reshape(some * rows, cols), 1)
         r = bf16_dot(flat, my_t[...], ((1,), (0,)))
         t = bf16_dot(flat, aux_t[...], ((1,), (0,)))
-        for g in range(chunk // group):
-            here = slice(g * group * planes, (g + 1) * group * planes)
-            x = slice(k * chunk + g * group, k * chunk + (g + 1) * group)
-            turned = jnp.swapaxes(r[here].reshape(group, planes, cols), 0, 1)
-            high, low = split(turned)
-            high_ref[:, x, :] = high
-            low_ref[:, x, :] = low
-            picked = jnp.swapaxes(t[here].reshape(group, planes, LANES), 0, 1)
-            total = jnp.zeros((group, LANES), F32)
-            for p in range(planes):
-                total = jnp.where((lane == p) | (lane == 64 + p), picked[p], total)
-            s_ref[x, :] = total
-    for p in range(planes):
-        high = high_ref[p]
-        w_ref[p] = bf16_dot(mx[...], jnp.concatenate([high, high, low_ref[p]], 0), ((1,), (0,)))
+        for i in range(some):
+            p = q + i
+            here = slice(i * rows, (i + 1) * rows)
+            total = jnp.where((lane == p) | (lane == 64 + p), t[here], total)
+            w_ref[p] = bf16_dot(mx[...], right_of(r[here], 0), ((1,), (0,)))
+    s_ref[...] = total
 
 
 def velocity_part(mx, my_t, aux_t, velocity):
-    rows, planes, cols = velocity.shape
-    return call(
-        functools.partial(velocity_kernel, 64),
+    planes, rows, cols = velocity.shape
+    return call(
+        functools.partial(velocity_kernel, 4),
         [struct(planes, rows, cols), struct(rows, LANES)],
         [VMEM] * 4,
         16,
-        scratch=[pltpu.VMEM((planes, rows, cols), BF16), pltpu.VMEM((planes, rows, cols), BF16)],
     )(mx, my_t, aux_t, velocity)
 
 
@@ -379,7 +367,7 @@
     )(edge, frows, scal, left, right, *payload)
 
 
-def wall_kernel(count, mx, aux, yrows, sv_ref, left_ref, right_ref, chosen_ref, wall_ref, s_ref, zh_ref, sel_ref):
+def wall_kernel(count, mx, my, aux, yrows, sv_ref, left_ref, right_ref, chosen_ref, wall_ref, s_ref, zh_ref, sel_ref, high_ref, low_ref):
     planes, slots, cols = wall_ref.shape
     rows = mx.shape[0]
     hl, hr = halos(count, left_ref, right_ref)
@@ -396,7 +384,11 @@
     some = 8
     for q in range(0, planes, some):
         flat = wall_ref[q : q + some].reshape(some * slots, cols)
-        t = bf16_dot(right_of(flat, 1), aux[...], ((1,), (0,)))
+        wc = right_of(flat, 1)
+        t = bf16_dot(wc, aux[...], ((1,), (0,)))
+        high, low = split(bf16_dot(wc, my[...], ((1,), (0,))))
+        high_ref[q : q + some] = high.reshape(some, slots, cols)
+        low_ref[q : q + some] = low.reshape(some, slots, cols)
         for i in range(some):
             p = q + i
             total = jnp.where((lane == p) | (lane == 64 + p), t[i * slots : (i + 1) * slots], total)
@@ -409,36 +401,32 @@
     s_ref[planes : 2 * planes, :] = high + 0.5 * (zl * f1[:, 0:1] + zr * f1[:, cols - 1 : cols])
 
 
-def wall_edges(count, mx, aux, yrows, sv, left, right, chosen, wall):
+def wall_edges(count, mx, my, aux, yrows, sv, left, right, chosen, wall):
     rows = mx.shape[0]
     planes, slots, cols = wall.shape
     return call(
         functools.partial(wall_kernel, count),
-        [struct(2 * planes, rows), struct(2 * planes, rows), struct(rows, 3 * slots, dtype=BF16)],
-        [VMEM] * 8,
+        [struct(2 * planes, rows), struct(2 * planes, rows), struct(rows, 3 * slots, dtype=BF16)]
+        + [struct(*wall.shape, dtype=BF16)] * 2,
+        [VMEM] * 9,
         8,
-    )(mx, aux, yrows, sv, left, right, chosen, wall)
-
-
-def wall_sweep_kernel(my, sel, wall_ref, v_ref, w_ref):
-    planes, slots, cols = wall_ref.shape
-    some = 8
-    for q in range(0, planes, some):
-        flat = wall_ref[q : q + some].reshape(some * slots, cols)
-        r = bf16_dot(right_of(flat, 1), my[...], ((1,), (0,)))
-        for i in range(some):
-            here = right_of(r[i * slots : (i + 1) * slots], 0)
-            w_ref[q + i] = v_ref[q + i] + bf16_dot(sel[...], here, ((1,), (0,)))
-
-
-def wall_sweep(my, sel, wall, w):
+    )(mx, my, aux, yrows, sv, left, right, chosen, wall)
+
+
+def wall_sweep_kernel(sel, high_ref, low_ref, v_ref, w_ref):
+    for p in range(w_ref.shape[0]):
+        high = high_ref[p]
+        w_ref[p] = v_ref[p] + bf16_dot(sel[...], jnp.concatenate([high, high, low_ref[p]], 0), ((1,), (0,)))
+
+
+def wall_sweep(sel, high, low, w):
     return call(
         wall_sweep_kernel,
         struct(*w.shape),
         [VMEM] * 4,
         8,
         input_output_aliases={3: 0},
-    )(my, sel, wall, w)
+    )(sel, high, low, w)
 
 
 def chain(parts, count, me, planes, f_in):
@@ -530,92 +518,68 @@
     )(my, xrows, yrows, scal, s, mine, other, *received)
 
 
-def finish_kernel(count, part, xrows, yrows, moved, solid, zh_ref, w_ref, *refs):
-    received, (out_hbm, parts, f_in, both, value_ref, out_ref, out_sem) = refs[:count], refs[count:]
+def finish_kernel(count, xrows, yrows, moved, solid, zh_ref, w_ref, *refs):
+    received, (out_hbm, parts, f_in, out_ref, out_sem) = refs[:count], refs[count:]
     me = lax.axis_index("gy")
     planes, rows, cols = w_ref.shape
-    halves = out_ref.shape[0]
-
-    piece = 32 * planes
-
-    def out_copy(k, b):
-        span = pl.ds(k * piece, piece)
-        return pltpu.make_async_copy(out_ref.at[b, span, :], out_hbm.at[span, pl.ds(b * LANES, LANES)], out_sem.at[k, b])
-
-    steps = rows // part
+
+    def out_copy(p):
+        return pltpu.make_async_copy(out_ref.at[p], out_hbm.at[:, p, :], out_sem.at[p])
+
     gather_parts(me, parts, received)
     in_f, in_b = chain(parts, count, me, planes, f_in)
-    both[0] = in_f
-    both[1] = in_b
     y = yrows[0:4, :]
-    width = cols // solid.shape[0]
-    for k in range(steps):
-        lo = k * part
-        c = xrows[0:3, lo : lo + part]
-        marks = jnp.concatenate([solid[:, lo : lo + part].astype(F32), jnp.zeros((8 - solid.shape[0], part), F32)], 0).T
-        fluid = [jnp.broadcast_to(marks[:, b * LANES // width : b * LANES // width + 1] == 0.0, (part, LANES)) for b in range(halves)]
-        for p in range(planes):
-            left = jnp.concatenate(
-                [
-                    c,
-                    both[0, p : p + 1, lo : lo + part],
-                    both[1, p : p + 1, lo : lo + part],
-                    zh_ref[p : p + 1, lo : lo + part],
-                    zh_ref[planes + p : planes + p + 1, lo : lo + part],
-                    jnp.zeros((1, part), F32),
-                ],
-                0,
-            )
-            right = jnp.concatenate(
-                [
-                    moved[p : p + 1, :],
-                    moved[planes + p : planes + p + 1, :],
-                    moved[2 * planes + p : 2 * planes + p + 1, :],
-                    y,
-                    jnp.zeros((1, cols), F32),
-                ],
-                0,
-            )
-            lh = left.astype(BF16).astype(F32)
-            rh = right.astype(BF16).astype(F32)
-            lc = jnp.concatenate([lh, lh, left - lh], 0).astype(BF16)
-            rc = jnp.concatenate([rh, right - rh, rh], 0).astype(BF16)
-            value = w_ref[p, lo : lo + part, :] + bf16_dot(lc, rc, ((0,), (0,)))
-            for b in range(halves):
-                value_ref[b, p] = jnp.where(fluid[b], value[:, b * LANES : (b + 1) * LANES], 0.0)
-        for g in range(part // planes):
-            at = (lo + g * planes) * planes
-            for b in range(halves):
-                turned = jnp.swapaxes(value_ref[b, :, g * planes : (g + 1) * planes, :], 0, 1)
-                out_ref[b, at : at + planes * planes, :] = turned.reshape(planes * planes, LANES)
-                if (at + planes * planes) % piece == 0:
-                    out_copy(at // piece, b).start()
-    for k in range(rows * planes // piece):
-        for b in range(halves):
-            out_copy(k, b).wait()
+    c = xrows[0:3, :]
+    nblock = solid.shape[0]
+    marks = jnp.concatenate([solid[...].astype(F32), jnp.zeros((8 - nblock, rows), F32)], 0).T
+    width = cols // nblock
+    fluid = jnp.concatenate([jnp.broadcast_to(marks[:, b : b + 1] == 0.0, (rows, width)) for b in range(nblock)], 1)
+    zero = jnp.zeros((1, rows), F32)
+    zero_y = jnp.zeros((1, cols), F32)
+    for p in range(planes):
+        left = jnp.concatenate(
+            [c, in_f[p : p + 1], in_b[p : p + 1], zh_ref[p : p + 1, :], zh_ref[planes + p : planes + p + 1, :], zero], 0
+        )
+        right = jnp.concatenate(
+            [
+                moved[p : p + 1, :],
+                moved[planes + p : planes + p + 1, :],
+                moved[2 * planes + p : 2 * planes + p + 1, :],
+                y,
+                zero_y,
+            ],
+            0,
+        )
+        lh = left.astype(BF16).astype(F32)
+        rh = right.astype(BF16).astype(F32)
+        lc = jnp.concatenate([lh, lh, left - lh], 0).astype(BF16)
+        rc = jnp.concatenate([rh, right - rh, rh], 0).astype(BF16)
+        value = w_ref[p] + bf16_dot(lc, rc, ((0,), (0,)))
+        out_ref[p] = jnp.where(fluid, value, 0.0)
+        if (p + 1) % GROUP == 0:
+            for done in range(p + 1 - GROUP, p + 1):
+                out_copy(done).start()
+    for p in range(planes):
+        out_copy(p).wait()
 
 
 def finish(xrows, yrows, moved, solid, zh, w, received):
     count = len(received)
     height = received[0].shape[0]
     planes, rows, cols = w.shape
-    part, halves = 128, cols // 128
-    out = call(
-        functools.partial(finish_kernel, count, part),
-        struct(rows * planes, cols),
+    return call(
+        functools.partial(finish_kernel, count),
+        struct(rows, planes, cols),
         [VMEM] * (6 + count),
         12,
         out_specs=HBM,
         scratch=[
             pltpu.VMEM((count, height, rows), F32),
             pltpu.VMEM((count, planes, rows), F32),
-            pltpu.VMEM((2, planes, rows), F32),
-            pltpu.VMEM((halves, planes, part, LANES), F32),
-            pltpu.VMEM((halves, rows * planes, 128), F32),
-            pltpu.SemaphoreType.DMA((rows // 32, halves)),
+            pltpu.VMEM((planes, rows, cols), F32),
+            pltpu.SemaphoreType.DMA((planes,)),
         ],
     )(xrows, yrows, moved, solid, zh, w, *received)
-    return out.reshape(rows, planes, cols)
 
 
 def rotate(value, axis, shift):
@@ -662,10 +626,10 @@
     other = lax.ppermute(mine, "gx", [(i, i ^ 1) for i in range(n_x)])
     both = pair(mine, other)
     received = [both] + [rotate(both, "gx", 2 * s) for s in range(1, n_x // 2)]
-    s_edge, zh, sel = wall_edges(n_y, mx, aux, yrows, sv, left, right, chosen, wall)
+    s_edge, zh, sel, high, low = wall_edges(n_y, mx, my, aux, yrows, sv, left, right, chosen, wall)
     mine, moved = x_join(my, xrows, yrows, scal, s_edge, mine, other, received)
     received = [mine] + [rotate(mine, "gy", s) for s in range(1, n_y)]
-    w = wall_sweep(my, sel, wall, w)
+    w = wall_sweep(sel, high, low, w)
     return finish(xrows, yrows, moved, solid_mask.T, zh, w, received)
 
 

time: 42 us -> 39.3 us (0.936)
  Pallas kernels: 21.1 us -> 18.7 us
    pallas_call x3, Pallas kernels: 13.3 us -> 11.7 us  [the longest x1 5.04 us: velocity_part(): call(functools.partial(velocity_kernel, 4), [struct(planes, rows, cols),...]
    pallas_call x1, Pallas kernels: 2.99 us -> 1.44 us  [wall_sweep(): call(wall_sweep_kernel, struct(*w.shape), [VMEM] * 4, 8, input_output_ali...]
    pallas_call x1, Pallas kernels: 1.41 us -> 2.2 us  [wall_edges(): call(functools.partial(wall_kernel, count), [struct(2 * planes, rows), st...]
  transfers between devices with their start and end apart: 12 -> 12, of which waited for: 3 -> 4; matrix products, arithmetic and copies ran while one was open for 0% -> 0% of each run, Pallas kernels for 35% -> 33%
where the time goes in v4:
time: 39.3 us; the launch traced here: 39.1 us
  Pallas kernels  18.7 us (48%)
  starting transfers between devices  18 us (46%)
  waiting for transfers between devices  2.23 us (6%)
    ppermute x11, starting transfers between devices, rotate(): lax.ppermute(value, axis, [(i, (i + shift) % count) for i in range(count)])  18 us
    pallas_call x1, Pallas kernels, velocity_part(): call(functools.partial(velocity_kernel, 4), [struct(planes, rows, cols),...  5.04 us
    pallas_call x1, Pallas kernels, factors(): call(factor_kernel, [struct(rows, 3 * rows, dtype=BF16), struct(3 * cols,...  4.14 us
    pallas_call x1, Pallas kernels, finish(): call(functools.partial(finish_kernel, count), struct(rows, planes, cols),...  2.58 us
    pallas_call x1, Pallas kernels, wall_edges(): call(functools.partial(wall_kernel, count), [struct(2 * planes, rows), st...  2.2 us
    pallas_call x1, Pallas kernels, pack(): call(functools.partial(pack_kernel, count, room), [struct(room + 1, plane...  2.04 us
    pallas_call x1, Pallas kernels, wall_sweep(): call(wall_sweep_kernel, struct(*w.shape), [VMEM] * 4, 8, input_output_ali...  1.44 us
    ppermute x1, waiting for transfers between devices, on_device(): other = lax.ppermute(mine, 'gx', [(i, i ^ 1) for i in range(n_x)])  1.21 us
  transfers between devices with their start and end apart: 12, of which 4 were waited for; matrix products, arithmetic and copies ran while one was open for 0% of the time, Pallas kernels for 33%

profile of v4, /device:TPU:0, one launch (start us, length us, event | category | flops | bytes accessed | tf_op | source)
XLA Modules:
  0.0 39.1 jit_solution(2874157544351665450)
XLA Ops:
  0.0 2.0 %shard_map.129 = (f32[33,16,128]{2,1,0:T(8,128)S(1)}, f32[33,16,128]{2,1,0:T(8,128)S(1)}, f32[33,16,128]{2,1,0:T(8,128)S(1)}, f32[33,16,128]{2,1,0:T(8,128)S(1)}) custom-call(s32[64]{0:T(128)} %bitcast.11, s32[64]{0:T(128)} %offset_ref.1, f32[64,16,128]{2,1,0:T(8,128)} %force_hbm.1), custom_call_target="tpu_custom_call" | custom-call | tf_op jit(solution)/shard_map/pallas_call | solution.py:110
  2.0 3.0 %collective-permute-start.2 = (f32[33,16,128]{2,1,0:T(8,128)S(1)}, f32[33,16,128]{2,1,0:T(8,128)S(1)}, u32[]{:S(2)}, u32[]{:S(2)}) collective-permute-start(f32[33,16,128]{2,1,0:T(8,128)S(1)} %get-tuple-element.55), channel_id=1, source_target_pairs={{0,1},{1,2},{2,3},{3,0},{4,5},{5,6},{6,7},{7,4},{8,9},{9,10},{10,1... | collective-permute-start | bytes 811016 | tf_op jit(solution)/shard_map/ppermute | solution.py:587
  5.0 1.5 %collective-permute-start.3 = (f32[33,16,128]{2,1,0:T(8,128)S(1)}, f32[33,16,128]{2,1,0:T(8,128)S(1)}, u32[]{:S(2)}, u32[]{:S(2)}) collective-permute-start(f32[33,16,128]{2,1,0:T(8,128)S(1)} %get-tuple-element.56), channel_id=1, source_target_pairs={{0,2},{1,3},{2,0},{3,1},{4,6},{5,7},{6,4},{7,5},{8,10},{9,11},{10,... | collective-permute-start | bytes 811016 | tf_op jit(solution)/shard_map/ppermute | solution.py:587
  6.6 1.4 %collective-permute-start.4 = (f32[33,16,128]{2,1,0:T(8,128)S(1)}, f32[33,16,128]{2,1,0:T(8,128)S(1)}, u32[]{:S(2)}, u32[]{:S(2)}) collective-permute-start(f32[33,16,128]{2,1,0:T(8,128)S(1)} %get-tuple-element.57), channel_id=1, source_target_pairs={{0,3},{1,0},{2,1},{3,2},{4,7},{5,4},{6,5},{7,6},{8,11},{9,8},{10,9... | collective-permute-start | bytes 811016 | tf_op jit(solution)/shard_map/ppermute | solution.py:587
  8.0 4.1 %shard_map.127 = (bf16[256,768]{1,0:T(8,128)(2,1)S(1)}, bf16[768,256]{1,0:T(8,128)(2,1)S(1)}, bf16[768,128]{1,0:T(8,128)(2,1)S(1)}, bf16[768,256]{1,0:T(8,128)(2...) custom-call(f32[256,16,256]{2,1,0:T(8,128)} %v_hbm.1, ...), custom_call_target="tpu_custom_call" | custom-call | tf_op jit(solution)/shard_map/pallas_call | solution.py:251
  12.1 0.6 %collective-permute-start = (f32[16,256]{1,0:T(8,128)S(1)}, f32[16,256]{1,0:T(8,128)S(1)}, u32[]{:S(2)}, u32[]{:S(2)}) collective-permute-start(f32[16,256]{1,0:T(8,128)S(1)} %get-tuple-element.50), channel_id=1, source_target_pairs={{0,1},{1,2},{2,3},{3,0},{4,5},{5,6},{6,7},{7,4},{8,9},{9,10},{10,1... | collective-permute-start | bytes 49160 | tf_op jit(solution)/shard_map/ppermute | solution.py:587
  12.8 2.3 %collective-permute-start.1 = (f32[16,256]{1,0:T(8,128)S(1)}, f32[16,256]{1,0:T(8,128)S(1)}, u32[]{:S(2)}, u32[]{:S(2)}) collective-permute-start(f32[16,256]{1,0:T(8,128)S(1)} %get-tuple-element.51), channel_id=1, source_target_pairs={{0,3},{1,0},{2,1},{3,2},{4,7},{5,4},{6,5},{7,6},{8,11},{9,8},{10,9... | collective-permute-start | bytes 49160 | tf_op jit(solution)/shard_map/ppermute | solution.py:587
  15.1 5.0 %shard_map.128 = (f32[16,256,256]{2,1,0:T(8,128)S(1)}, f32[256,128]{1,0:T(8,128)S(1)}) custom-call(bf16[256,768]{1,0:T(8,128)(2,1)S(1)} %get-tuple-element.41.mx, bf16[768,256]{1,0:T(8,128)(2,1)S(1)} %get-tuple-element.43.my_t, bf16[768,128]{1,0:T(8,128)(2,1)S(1)} %get-tuple-element.44.aux_t, f32[16,256,256]{2,1,0:T(8,128)S(1)} %get-tuple-element.45.v_ref), custom_call_target="tpu_custom_call" | custom-call | tf_op jit(solution)/shard_map/pallas_call | solution.py:296
  20.2 1.1 %shard_map.130 = (f32[40,256]{1,0:T(8,128)S(1)}, bf16[256,128]{1,0:T(8,128)(2,1)S(1)}, f32[16,128,256]{2,1,0:T(8,128)S(1)}) custom-call(f32[2,16,256]{2,1,0:T(8,128)S(1)} %get-tuple-element.52.edge_ref, f32[8,256]{1,0:T(8,128)S(1)} %get-tuple-element.53.frows, f32[16,256]{1,0:T(8,128)S(1)} %get-tuple-element.40.scal, ...), custom_call_target="tpu_custom_call" | custom-call | tf_op jit(solution)/shard_map/pallas_call | solution.py:362
  21.3 0.1 collective-permute-start.5
  21.4 1.2 %collective-permute-done.5.other.other_ref = f32[40,256]{1,0:T(8,128)S(1)} collective-permute-done((f32[40,256]{1,0:T(8,128)S(1)}, f32[40,256]{1,0:T(8,128)S(1)}, u32[]{:S(2)}, u32[]{:S(2)}) %collective-permute-start.5) | collective-permute-done | bytes 40992 | tf_op jit(solution)/shard_map/ppermute | solution.py:626
  22.6 1.6 %collective-permute-start.6 = (f32[40,256]{1,0:T(8,128)S(1)}, f32[40,256]{1,0:T(8,128)S(1)}, u32[]{:S(2)}, u32[]{:S(2)}) collective-permute-start(f32[40,256]{1,0:T(8,128)S(1)} %shard_map.132.refs_0_), channel_id=1, source_target_pairs={{0,8},{4,12},{8,16},{12,20},{16,24},{20,28},{24,0},{28,4},{1,9},{5... | collective-permute-start | bytes 122888 | tf_op jit(solution)/shard_map/ppermute | solution.py:587
  24.2 2.6 %collective-permute-start.7 = (f32[40,256]{1,0:T(8,128)S(1)}, f32[40,256]{1,0:T(8,128)S(1)}, u32[]{:S(2)}, u32[]{:S(2)}) collective-permute-start(f32[40,256]{1,0:T(8,128)S(1)} %shard_map.132.refs_0_), channel_id=1, source_target_pairs={{0,16},{4,20},{8,24},{12,28},{16,0},{20,4},{24,8},{28,12},{1,17},{... | collective-permute-start | bytes 122888 | tf_op jit(solution)/shard_map/ppermute | solution.py:587
  26.8 1.3 %collective-permute-start.8 = (f32[40,256]{1,0:T(8,128)S(1)}, f32[40,256]{1,0:T(8,128)S(1)}, u32[]{:S(2)}, u32[]{:S(2)}) collective-permute-start(f32[40,256]{1,0:T(8,128)S(1)} %shard_map.132.refs_0_), channel_id=1, source_target_pairs={{0,24},{4,28},{8,0},{12,4},{16,8},{20,12},{24,16},{28,20},{1,25},{... | collective-permute-start | bytes 122888 | tf_op jit(solution)/shard_map/ppermute | solution.py:587
  28.2 2.2 %shard_map.131 = (f32[32,256]{1,0:T(8,128)S(1)}, f32[32,256]{1,0:T(8,128)S(1)}, bf16[256,384]{1,0:T(8,128)(2,1)S(1)}, bf16[16,128,256]{2,1,0:T(8,128)(2,1)S(1)}, bf16[16,128,256]{2,1,0:T(8,128)(2,1)S(1)}) custom-call(bf16[256,768]{1,0:T(8,128)(2,1)S(1)} %get-tuple-element.41.mx, bf16[768,256]{1,0:T(8,128)(2,1)S(1)} %get-tuple-element.39.my, ...), custom_call_target="tpu_custom_call" | custom-call | tf_op jit(solution)/shard_map/pallas_call | solution.py:407
  30.4 0.4 %collective-permute-done.8.refs_3_ = f32[40,256]{1,0:T(8,128)S(1)} collective-permute-done((f32[40,256]{1,0:T(8,128)S(1)}, f32[40,256]{1,0:T(8,128)S(1)}, u32[]{:S(2)}, u32[]{:S(2)}) %collective-permute-start.8) | collective-permute-done | bytes 40992 | tf_op jit(solution)/shard_map/ppermute | solution.py:587
  30.8 0.2 shard_map.133
  31.0 0.6 %collective-permute-start.9 = (f32[40,256]{1,0:T(8,128)S(1)}, f32[40,256]{1,0:T(8,128)S(1)}, u32[]{:S(2)}, u32[]{:S(2)}) collective-permute-start(f32[40,256]{1,0:T(8,128)S(1)} %get-tuple-element.68.refs_0_), channel_id=1, source_target_pairs={{0,1},{1,2},{2,3},{3,0},{4,5},{5,6},{6,7},{7,4},{8,9},{9,10},{10,1... | collective-permute-start | bytes 122888 | tf_op jit(solution)/shard_map/ppermute | solution.py:587
  31.6 0.5 %collective-permute-start.10 = (f32[40,256]{1,0:T(8,128)S(1)}, f32[40,256]{1,0:T(8,128)S(1)}, u32[]{:S(2)}, u32[]{:S(2)}) collective-permute-start(f32[40,256]{1,0:T(8,128)S(1)} %get-tuple-element.68.refs_0_), channel_id=1, source_target_pairs={{0,2},{1,3},{2,0},{3,1},{4,6},{5,7},{6,4},{7,5},{8,10},{9,11},{10,... | collective-permute-start | bytes 122888 | tf_op jit(solution)/shard_map/ppermute | solution.py:587
  32.2 2.4 %collective-permute-start.11 = (f32[40,256]{1,0:T(8,128)S(1)}, f32[40,256]{1,0:T(8,128)S(1)}, u32[]{:S(2)}, u32[]{:S(2)}) collective-permute-start(f32[40,256]{1,0:T(8,128)S(1)} %get-tuple-element.68.refs_0_), channel_id=1, source_target_pairs={{0,3},{1,0},{2,1},{3,2},{4,7},{5,4},{6,5},{7,6},{8,11},{9,8},{10,9... | collective-permute-start | bytes 122888 | tf_op jit(solution)/shard_map/ppermute | solution.py:587
  34.5 1.4 %shard_map.134.w_ref = f32[16,256,256]{2,1,0:T(8,128)S(1)} custom-call(bf16[256,384]{1,0:T(8,128)(2,1)S(1)} %get-tuple-element.64.sel, bf16[16,128,256]{2,1,0:T(8,128)(2,1)S(1)} %get-tuple-element.65.high_ref, bf16[16,128,256]{2,1,0:T(8,128)(2,1)S(1)} %get-tuple-element.66.low_ref, ...), custom_call_target="tpu_custom_call", output_to_operand_aliasing={{}: (3, {})} | custom-call | tf_op jit(solution)/shard_map/pallas_call | solution.py:423
  36.0 0.1 collective-permute-done.9.refs_1_
  36.1 0.5 %collective-permute-done.11.refs_3_ = f32[40,256]{1,0:T(8,128)S(1)} collective-permute-done((f32[40,256]{1,0:T(8,128)S(1)}, f32[40,256]{1,0:T(8,128)S(1)}, u32[]{:S(2)}, u32[]{:S(2)}) %collective-permute-start.11) | collective-permute-done | bytes 40992 | tf_op jit(solution)/shard_map/ppermute | solution.py:587
  36.6 2.6 %shard_map.135 = f32[256,16,256]{2,1,0:T(8,128)} custom-call(f32[8,256]{1,0:T(8,128)S(1)} %get-tuple-element.37.xrows, f32[8,256]{1,0:T(8,128)S(1)} %get-tuple-element.38.yrows, f32[48,256]{1,0:T(8,128)S(1)} %get-tuple-element.62.moved, s32[2,256]{1,0:T(2,128)S(1)} %bitcast.6, f32[32,256]{1,0:T(8,128)S(1)} %get-tuple-element.63.zh_ref, ...), custom_call_target="tpu_custom_call" | custom-call | tf_op jit(solution)/shard_map/pallas_call | solution.py:570
  (11 shorter events, 0.0 us)
Async XLA Ops:
  2.0 18.1 %collective-permute-start.2 = (f32[33,16,128]{2,1,0:T(8,128)S(1)}, f32[33,16,128]{2,1,0:T(8,128)S(1)}, u32[]{:S(2)}, u32[]{:S(2)}) collective-permute-start(f32[33,16,128]{2,1,0:T(8,128)S(1)} %get-tuple-element.55), channel_id=1, source_target_pairs={{0,1},{1,2},{2,3},{3,0},{4,5},{5,6},{6,7},{7,4},{8,9},{9,10},{10,1... | collective-permute-start | bytes 811016 | tf_op jit(solution)/shard_map/ppermute | solution.py:587
  5.0 15.2 %collective-permute-start.3 = (f32[33,16,128]{2,1,0:T(8,128)S(1)}, f32[33,16,128]{2,1,0:T(8,128)S(1)}, u32[]{:S(2)}, u32[]{:S(2)}) collective-permute-start(f32[33,16,128]{2,1,0:T(8,128)S(1)} %get-tuple-element.56), channel_id=1, source_target_pairs={{0,2},{1,3},{2,0},{3,1},{4,6},{5,7},{6,4},{7,5},{8,10},{9,11},{10,... | collective-permute-start | bytes 811016 | tf_op jit(solution)/shard_map/ppermute | solution.py:587
  6.6 13.6 %collective-permute-start.4 = (f32[33,16,128]{2,1,0:T(8,128)S(1)}, f32[33,16,128]{2,1,0:T(8,128)S(1)}, u32[]{:S(2)}, u32[]{:S(2)}) collective-permute-start(f32[33,16,128]{2,1,0:T(8,128)S(1)} %get-tuple-element.57), channel_id=1, source_target_pairs={{0,3},{1,0},{2,1},{3,2},{4,7},{5,4},{6,5},{7,6},{8,11},{9,8},{10,9... | collective-permute-start | bytes 811016 | tf_op jit(solution)/shard_map/ppermute | solution.py:587
  12.1 8.0 %collective-permute-start = (f32[16,256]{1,0:T(8,128)S(1)}, f32[16,256]{1,0:T(8,128)S(1)}, u32[]{:S(2)}, u32[]{:S(2)}) collective-permute-start(f32[16,256]{1,0:T(8,128)S(1)} %get-tuple-element.50), channel_id=1, source_target_pairs={{0,1},{1,2},{2,3},{3,0},{4,5},{5,6},{6,7},{7,4},{8,9},{9,10},{10,1... | collective-permute-start | bytes 49160 | tf_op jit(solution)/shard_map/ppermute | solution.py:587
  12.8 7.4 %collective-permute-start.1 = (f32[16,256]{1,0:T(8,128)S(1)}, f32[16,256]{1,0:T(8,128)S(1)}, u32[]{:S(2)}, u32[]{:S(2)}) collective-permute-start(f32[16,256]{1,0:T(8,128)S(1)} %get-tuple-element.51), channel_id=1, source_target_pairs={{0,3},{1,0},{2,1},{3,2},{4,7},{5,4},{6,5},{7,6},{8,11},{9,8},{10,9... | collective-permute-start | bytes 49160 | tf_op jit(solution)/shard_map/ppermute | solution.py:587
  21.3 1.3 %collective-permute-start.5 = (f32[40,256]{1,0:T(8,128)S(1)}, f32[40,256]{1,0:T(8,128)S(1)}, u32[]{:S(2)}, u32[]{:S(2)}) collective-permute-start(f32[40,256]{1,0:T(8,128)S(1)} %get-tuple-element.61.mine.mine_ref), channel_id=1, source_target_pairs={{0,4},{4,0},{8,12},{12,8},{16,20},{20,16},{24,28},{28,24},{1,5},{5... | collective-permute-start | bytes 122888 | tf_op jit(solution)/shard_map/ppermute | solution.py:626
  22.6 7.8 %collective-permute-start.6 = (f32[40,256]{1,0:T(8,128)S(1)}, f32[40,256]{1,0:T(8,128)S(1)}, u32[]{:S(2)}, u32[]{:S(2)}) collective-permute-start(f32[40,256]{1,0:T(8,128)S(1)} %shard_map.132.refs_0_), channel_id=1, source_target_pairs={{0,8},{4,12},{8,16},{12,20},{16,24},{20,28},{24,0},{28,4},{1,9},{5... | collective-permute-start | bytes 122888 | tf_op jit(solution)/shard_map/ppermute | solution.py:587
  24.2 6.2 %collective-permute-start.7 = (f32[40,256]{1,0:T(8,128)S(1)}, f32[40,256]{1,0:T(8,128)S(1)}, u32[]{:S(2)}, u32[]{:S(2)}) collective-permute-start(f32[40,256]{1,0:T(8,128)S(1)} %shard_map.132.refs_0_), channel_id=1, source_target_pairs={{0,16},{4,20},{8,24},{12,28},{16,0},{20,4},{24,8},{28,12},{1,17},{... | collective-permute-start | bytes 122888 | tf_op jit(solution)/shard_map/ppermute | solution.py:587
  26.8 4.0 %collective-permute-start.8 = (f32[40,256]{1,0:T(8,128)S(1)}, f32[40,256]{1,0:T(8,128)S(1)}, u32[]{:S(2)}, u32[]{:S(2)}) collective-permute-start(f32[40,256]{1,0:T(8,128)S(1)} %shard_map.132.refs_0_), channel_id=1, source_target_pairs={{0,24},{4,28},{8,0},{12,4},{16,8},{20,12},{24,16},{28,20},{1,25},{... | collective-permute-start | bytes 122888 | tf_op jit(solution)/shard_map/ppermute | solution.py:587
  31.0 5.0 %collective-permute-start.9 = (f32[40,256]{1,0:T(8,128)S(1)}, f32[40,256]{1,0:T(8,128)S(1)}, u32[]{:S(2)}, u32[]{:S(2)}) collective-permute-start(f32[40,256]{1,0:T(8,128)S(1)} %get-tuple-element.68.refs_0_), channel_id=1, source_target_pairs={{0,1},{1,2},{2,3},{3,0},{4,5},{5,6},{6,7},{7,4},{8,9},{9,10},{10,1... | collective-permute-start | bytes 122888 | tf_op jit(solution)/shard_map/ppermute | solution.py:587
  31.6 4.4 %collective-permute-start.10 = (f32[40,256]{1,0:T(8,128)S(1)}, f32[40,256]{1,0:T(8,128)S(1)}, u32[]{:S(2)}, u32[]{:S(2)}) collective-permute-start(f32[40,256]{1,0:T(8,128)S(1)} %get-tuple-element.68.refs_0_), channel_id=1, source_target_pairs={{0,2},{1,3},{2,0},{3,1},{4,6},{5,7},{6,4},{7,5},{8,10},{9,11},{10,... | collective-permute-start | bytes 122888 | tf_op jit(solution)/shard_map/ppermute | solution.py:587
  32.2 4.4 %collective-permute-start.11 = (f32[40,256]{1,0:T(8,128)S(1)}, f32[40,256]{1,0:T(8,128)S(1)}, u32[]{:S(2)}, u32[]{:S(2)}) collective-permute-start(f32[40,256]{1,0:T(8,128)S(1)} %get-tuple-element.68.refs_0_), channel_id=1, source_target_pairs={{0,3},{1,0},{2,1},{3,2},{4,7},{5,4},{6,5},{7,6},{8,11},{9,8},{10,9... | collective-permute-start | bytes 122888 | tf_op jit(solution)/shard_map/ppermute | solution.py:587
  34.5 2.0 %copy-start = (s32[256,2]{0,1:T(2,128)S(1)}, s32[256,2]{0,1:T(2,128)}, u32[]{:S(2)}) copy-start(s32[256,2]{0,1:T(2,128)} %param.25) | copy-start | bytes 6148

commit v5 on v4

--- a/solution.py
+++ b/solution.py
@@ -72,8 +72,7 @@
         taken[shift] = shift * room
 
     def step(entry, carry):
-        shift = owner_ref[entry] - me
-        shift = jnp.where(shift < 0, shift + count, shift)
+        shift = owner_ref[entry] ^ me
         slot = taken[shift]
         taken[shift] = slot + 1
         table[slot] = entry
@@ -82,26 +81,21 @@
     lax.fori_loop(0, walls, step, 0, unroll=8)
 
 
-def pack_kernel(count, room, owner_ref, offset_ref, force_hbm, *refs):
-    outs, (force_ref, table, taken, sem) = refs[:count], refs[count:]
-    walls = force_hbm.shape[0]
-    planes, width = force_hbm.shape[1:]
+def pack_kernel(count, room, owner_ref, offset_ref, force_ref, *refs):
+    outs, (table, taken) = refs[:count], refs[count:]
+    walls, planes, width = force_ref.shape
     me = lax.axis_index("gy")
-    copy = pltpu.make_async_copy(force_hbm, force_ref.at[pl.ds(0, walls)], sem)
-    copy.start()
-    force_ref[walls] = jnp.zeros(force_ref.shape[1:], F32)
     for slot in range(count * room):
         table[slot] = walls
     sort_walls(count, room, me, walls, owner_ref, table, taken)
-    copy.wait()
     lane = lax.broadcasted_iota(jnp.int32, (planes, LANES), 1)
     for shift in list(range(1, count)) + [0]:
         places = jnp.full((planes, LANES), -1, jnp.int32)
         for slot in range(room):
             entry = table[shift * room + slot]
-            outs[shift][slot] = force_ref[entry]
-            place = jnp.where(entry < walls, offset_ref[jnp.minimum(entry, walls - 1)], -1)
-            places = jnp.where(lane == slot, place, places)
+            real = jnp.minimum(entry, walls - 1)
+            outs[shift][slot] = jnp.where(entry < walls, force_ref[real], 0.0)
+            places = jnp.where(lane == slot, jnp.where(entry < walls, offset_ref[real], -1), places)
         outs[shift][room] = places.astype(F32)
 
 
@@ -110,14 +104,9 @@
     return call(
         functools.partial(pack_kernel, count, room),
         [struct(room + 1, planes, width) for s in range(count)],
-        [SMEM, SMEM, HBM],
+        [SMEM, SMEM, VMEM],
         8,
-        scratch=[
-            pltpu.VMEM((walls + 1, planes, width), F32),
-            pltpu.SMEM((count * room,), jnp.int32),
-            pltpu.SMEM((count,), jnp.int32),
-            pltpu.SemaphoreType.DMA,
-        ],
+        scratch=[pltpu.SMEM((count * room,), jnp.int32), pltpu.SMEM((count,), jnp.int32)],
     )(pin(owner), pin(offset), pin(force))
 
 
@@ -160,11 +149,11 @@
         copy.wait()
     lx, ux, lcx, ucx, ly, uy, lcy, ucy = fetched
     rows_x, rows_y = lx.shape[0], ly.shape[0]
-    both = f32_dot(ux[...], lx[...], ((1,), (0,)))
+    both = bf16_dot(right_of(ux[...], 1), left_of(lx[...], 0), ((1,), (0,)))
     zero = jnp.zeros((1, rows_x), F32)
     frows[...] = jnp.concatenate([row(lx, rows_x - 1), both[0:8][0:1], zero, zero, zero, zero, zero, zero], 0)
     mx[...] = left_of(half_shift_rows(both), 1)
-    both_y = f32_dot(uy[...], ly[...], ((1,), (0,)))
+    both_y = bf16_dot(right_of(uy[...], 1), left_of(ly[...], 0), ((1,), (0,)))
     turned = both_y.T
     my[...] = left_of(turned, 0)
     my_t[...] = left_of(half_shift_rows(turned), 0)
@@ -468,19 +457,19 @@
     return call(pair_kernel, struct(*mine.shape), [VMEM, VMEM], 8)(mine, other)
 
 
-def gather_parts(me, parts, received):
+def gather_parts(me, parts, received, shifts):
     count = len(received)
-    for shift in range(count):
-        parts[pl.ds(lax.rem(me - shift + count, count), 1)] = received[shift][...][None]
-
-
-def x_join_kernel(count, my, xrows, yrows, scal, s_ref, mine_ref, other_ref, *refs):
+    for shift, value in zip(shifts, received, strict=True):
+        parts[pl.ds(lax.rem(me - shift + count, count), 1)] = value[...][None]
+
+
+def x_join_kernel(count, shifts, my, xrows, yrows, scal, s_ref, mine_ref, other_ref, *refs):
     received, (out, moved, parts, f_in) = refs[:count], refs[count:]
     me = lax.axis_index("gx")
     place = lax.div(me, 2)
     odd = lax.rem(me, 2) == 1
     planes = s_ref.shape[0] // 2
-    gather_parts(place, parts, received)
+    gather_parts(place, parts, received, shifts)
     f, g = chain(parts, count, place, planes, f_in)
     mine, other = mine_ref[...], other_ref[...]
     left, right = jnp.where(odd, other, mine), jnp.where(odd, mine, other)
@@ -505,12 +494,12 @@
     moved[...] = bf16_dot(right_of(jnp.concatenate([in_f, in_b, before], 0), 1), my[...], ((1,), (0,)))
 
 
-def x_join(my, xrows, yrows, scal, s, mine, other, received):
+def x_join(my, xrows, yrows, scal, s, mine, other, received, shifts):
     count = len(received)
     height, cols = received[0].shape
     planes, rows = s.shape[0] // 2, s.shape[1]
     return call(
-        functools.partial(x_join_kernel, count),
+        functools.partial(x_join_kernel, count, shifts),
         [struct(2 * planes + 8, rows), struct(3 * planes, cols)],
         [VMEM] * (7 + count),
         8,
@@ -518,7 +507,7 @@
     )(my, xrows, yrows, scal, s, mine, other, *received)
 
 
-def finish_kernel(count, xrows, yrows, moved, solid, zh_ref, w_ref, *refs):
+def finish_kernel(count, shifts, xrows, yrows, moved, solid, zh_ref, w_ref, *refs):
     received, (out_hbm, parts, f_in, out_ref, out_sem) = refs[:count], refs[count:]
     me = lax.axis_index("gy")
     planes, rows, cols = w_ref.shape
@@ -526,7 +515,7 @@
     def out_copy(p):
         return pltpu.make_async_copy(out_ref.at[p], out_hbm.at[:, p, :], out_sem.at[p])
 
-    gather_parts(me, parts, received)
+    gather_parts(me, parts, received, shifts)
     in_f, in_b = chain(parts, count, me, planes, f_in)
     y = yrows[0:4, :]
     c = xrows[0:3, :]
@@ -563,12 +552,12 @@
         out_copy(p).wait()
 
 
-def finish(xrows, yrows, moved, solid, zh, w, received):
+def finish(xrows, yrows, moved, solid, zh, w, received, shifts):
     count = len(received)
     height = received[0].shape[0]
     planes, rows, cols = w.shape
     return call(
-        functools.partial(finish_kernel, count),
+        functools.partial(finish_kernel, count, shifts),
         struct(rows, planes, cols),
         [VMEM] * (6 + count),
         12,
@@ -580,6 +569,10 @@
             pltpu.SemaphoreType.DMA((planes,)),
         ],
     )(xrows, yrows, moved, solid, zh, w, *received)
+
+
+def swap(value, axis, mask):
+    return lax.ppermute(value, axis, [(i, i ^ mask) for i in range(lax.axis_size(axis))])
 
 
 def rotate(value, axis, shift):
@@ -607,7 +600,7 @@
     n_x, n_y = lax.axis_size("gx"), lax.axis_size("gy")
     room = 2 * walls // n_y
     packed = pack(wall_owner[:, 0], wall_offset, wall_force, n_y, room)
-    payload = [packed[0]] + [rotate(packed[s], "gy", s) for s in range(1, n_y)]
+    payload = [packed[0]] + [swap(packed[s], "gy", s) for s in range(1, n_y)]
     mx, my, aux, my_t, aux_t, xrows, yrows, frows, scal, v, edge, first, last = factors(
         velocity,
         lower_x,
@@ -623,14 +616,16 @@
     w, sv = velocity_part(mx, my_t, aux_t, v)
     w, sv, edge = lax.optimization_barrier((w, sv, edge))
     mine, chosen, wall = x_edges(edge, frows, scal, left, right, payload, room)
-    other = lax.ppermute(mine, "gx", [(i, i ^ 1) for i in range(n_x)])
+    other = swap(mine, "gx", 1)
     both = pair(mine, other)
-    received = [both] + [rotate(both, "gx", 2 * s) for s in range(1, n_x // 2)]
+    shifts = list(range(n_x // 2))
+    received = [rotate(both, "gx", 2 * s) if s else both for s in shifts]
     s_edge, zh, sel, high, low = wall_edges(n_y, mx, my, aux, yrows, sv, left, right, chosen, wall)
-    mine, moved = x_join(my, xrows, yrows, scal, s_edge, mine, other, received)
-    received = [mine] + [rotate(mine, "gy", s) for s in range(1, n_y)]
+    mine, moved = x_join(my, xrows, yrows, scal, s_edge, mine, other, received, shifts)
+    shifts = list(range(n_y))
+    received = [rotate(mine, "gy", s) if s else mine for s in shifts]
     w = wall_sweep(sel, high, low, w)
-    return finish(xrows, yrows, moved, solid_mask.T, zh, w, received)
+    return finish(xrows, yrows, moved, solid_mask.T, zh, w, received, shifts)
 
 
 def solution(mesh):

time: 39.3 us -> 38.7 us (0.985)
  Pallas kernels: 18.7 us -> 18.3 us
    ppermute x11 -> x8, starting transfers between devices: 18 us -> 13.1 us  [rotate(): lax.ppermute(value, axis, [(i, (i + shift) % count) for i in range(count)])]
    ppermute x1 -> x4, starting transfers between devices: 0.07 us -> 4.62 us  [swap(): lax.ppermute(value, axis, [(i, i ^ mask) for i in range(lax.axis_size(axi...]
    ppermute x11 -> x8, waiting for transfers between devices: 1.03 us -> 1.28 us  [rotate(): lax.ppermute(value, axis, [(i, (i + shift) % count) for i in range(count)])]
    ppermute x1 -> x4, waiting for transfers between devices: 1.21 us -> 1.21 us  [swap(): lax.ppermute(value, axis, [(i, i ^ mask) for i in range(lax.axis_size(axi...]
where the time goes in v5:
time: 38.7 us; the launch traced here: 38.6 us
  Pallas kernels  18.3 us (47%)
  starting transfers between devices  17.7 us (46%)
  waiting for transfers between devices  2.49 us (6%)
    ppermute x8, starting transfers between devices, rotate(): lax.ppermute(value, axis, [(i, (i + shift) % count) for i in range(count)])  13.1 us
    pallas_call x1, Pallas kernels, velocity_part(): call(functools.partial(velocity_kernel, 4), [struct(planes, rows, cols),...  5.04 us
    ppermute x4, starting transfers between devices, swap(): lax.ppermute(value, axis, [(i, i ^ mask) for i in range(lax.axis_size(axi...  4.62 us
    pallas_call x1, Pallas kernels, factors(): call(factor_kernel, [struct(rows, 3 * rows, dtype=BF16), struct(3 * cols,...  3.88 us
    pallas_call x1, Pallas kernels, finish(): call(functools.partial(finish_kernel, count, shifts), struct(rows, planes...  2.58 us
    pallas_call x1, Pallas kernels, wall_edges(): call(functools.partial(wall_kernel, count), [struct(2 * planes, rows), st...  2.2 us
    pallas_call x1, Pallas kernels, pack(): call(functools.partial(pack_kernel, count, room), [struct(room + 1, plane...  1.85 us
    pallas_call x1, Pallas kernels, wall_sweep(): call(wall_sweep_kernel, struct(*w.shape), [VMEM] * 4, 8, input_output_ali...  1.44 us
  transfers between devices with their start and end apart: 12, of which 4 were waited for; matrix products, arithmetic and copies ran while one was open for 0% of the time, Pallas kernels for 33%

profile of v5, /device:TPU:0, one launch (start us, length us, event | category | flops | bytes accessed | tf_op | source)
XLA Modules:
  0.0 38.6 jit_solution(14118976757666435497)
XLA Ops:
  0.0 1.8 %shard_map.129 = (f32[33,16,128]{2,1,0:T(8,128)S(1)}, f32[33,16,128]{2,1,0:T(8,128)S(1)}, f32[33,16,128]{2,1,0:T(8,128)S(1)}, f32[33,16,128]{2,1,0:T(8,128)S(1)}) custom-call(s32[64]{0:T(128)} %bitcast.11, s32[64]{0:T(128)} %offset_ref.1, f32[64,16,128]{2,1,0:T(8,128)} %force_ref.1), custom_call_target="tpu_custom_call" | custom-call | tf_op jit(solution)/shard_map/pallas_call | solution.py:104
  1.9 3.0 %collective-permute-start.2 = (f32[33,16,128]{2,1,0:T(8,128)S(1)}, f32[33,16,128]{2,1,0:T(8,128)S(1)}, u32[]{:S(2)}, u32[]{:S(2)}) collective-permute-start(f32[33,16,128]{2,1,0:T(8,128)S(1)} %get-tuple-element.55), channel_id=1, source_target_pairs={{0,1},{1,0},{2,3},{3,2},{4,5},{5,4},{6,7},{7,6},{8,9},{9,8},{10,11... | collective-permute-start | bytes 811016 | tf_op jit(solution)/shard_map/ppermute | solution.py:575
  4.9 1.5 %collective-permute-start.3 = (f32[33,16,128]{2,1,0:T(8,128)S(1)}, f32[33,16,128]{2,1,0:T(8,128)S(1)}, u32[]{:S(2)}, u32[]{:S(2)}) collective-permute-start(f32[33,16,128]{2,1,0:T(8,128)S(1)} %get-tuple-element.56), channel_id=1, source_target_pairs={{0,2},{1,3},{2,0},{3,1},{4,6},{5,7},{6,4},{7,5},{8,10},{9,11},{10,... | collective-permute-start | bytes 811016 | tf_op jit(solution)/shard_map/ppermute | solution.py:575
  6.4 0.0 collective-permute-start.4
  6.4 3.9 %shard_map.127 = (bf16[256,768]{1,0:T(8,128)(2,1)S(1)}, bf16[768,256]{1,0:T(8,128)(2,1)S(1)}, bf16[768,128]{1,0:T(8,128)(2,1)S(1)}, bf16[768,256]{1,0:T(8,128)(2...) custom-call(f32[256,16,256]{2,1,0:T(8,128)} %v_hbm.1, ...), custom_call_target="tpu_custom_call" | custom-call | tf_op jit(solution)/shard_map/pallas_call | solution.py:240
  10.3 2.0 %collective-permute-start = (f32[16,256]{1,0:T(8,128)S(1)}, f32[16,256]{1,0:T(8,128)S(1)}, u32[]{:S(2)}, u32[]{:S(2)}) collective-permute-start(f32[16,256]{1,0:T(8,128)S(1)} %get-tuple-element.50), channel_id=1, source_target_pairs={{0,1},{1,2},{2,3},{3,0},{4,5},{5,6},{6,7},{7,4},{8,9},{9,10},{10,1... | collective-permute-start | bytes 49160 | tf_op jit(solution)/shard_map/ppermute | solution.py:580
  12.3 1.0 %collective-permute-start.1 = (f32[16,256]{1,0:T(8,128)S(1)}, f32[16,256]{1,0:T(8,128)S(1)}, u32[]{:S(2)}, u32[]{:S(2)}) collective-permute-start(f32[16,256]{1,0:T(8,128)S(1)} %get-tuple-element.51), channel_id=1, source_target_pairs={{0,3},{1,0},{2,1},{3,2},{4,7},{5,4},{6,5},{7,6},{8,11},{9,8},{10,9... | collective-permute-start | bytes 49160 | tf_op jit(solution)/shard_map/ppermute | solution.py:580
  13.3 5.0 %shard_map.128 = (f32[16,256,256]{2,1,0:T(8,128)S(1)}, f32[256,128]{1,0:T(8,128)S(1)}) custom-call(bf16[256,768]{1,0:T(8,128)(2,1)S(1)} %get-tuple-element.41.mx, bf16[768,256]{1,0:T(8,128)(2,1)S(1)} %get-tuple-element.43.my_t, bf16[768,128]{1,0:T(8,128)(2,1)S(1)} %get-tuple-element.44.aux_t, f32[16,256,256]{2,1,0:T(8,128)S(1)} %get-tuple-element.45.v_ref), custom_call_target="tpu_custom_call" | custom-call | tf_op jit(solution)/shard_map/pallas_call | solution.py:285
  18.4 0.6 %collective-permute-done.left_ref = f32[16,256]{1,0:T(8,128)S(1)} collective-permute-done((f32[16,256]{1,0:T(8,128)S(1)}, f32[16,256]{1,0:T(8,128)S(1)}, u32[]{:S(2)}, u32[]{:S(2)}) %collective-permute-start) | collective-permute-done | bytes 16416 | tf_op jit(solution)/shard_map/ppermute | solution.py:580
  19.0 1.1 %shard_map.130 = (f32[40,256]{1,0:T(8,128)S(1)}, bf16[256,128]{1,0:T(8,128)(2,1)S(1)}, f32[16,128,256]{2,1,0:T(8,128)S(1)}) custom-call(f32[2,16,256]{2,1,0:T(8,128)S(1)} %get-tuple-element.52.edge_ref, f32[8,256]{1,0:T(8,128)S(1)} %get-tuple-element.53.frows, f32[16,256]{1,0:T(8,128)S(1)} %get-tuple-element.40.scal, ...), custom_call_target="tpu_custom_call" | custom-call | tf_op jit(solution)/shard_map/pallas_call | solution.py:351
  20.1 0.1 collective-permute-start.5
  20.1 1.2 %collective-permute-done.5.other.other_ref = f32[40,256]{1,0:T(8,128)S(1)} collective-permute-done((f32[40,256]{1,0:T(8,128)S(1)}, f32[40,256]{1,0:T(8,128)S(1)}, u32[]{:S(2)}, u32[]{:S(2)}) %collective-permute-start.5) | collective-permute-done | bytes 40992 | tf_op jit(solution)/shard_map/ppermute | solution.py:575
  21.4 1.6 %collective-permute-start.6 = (f32[40,256]{1,0:T(8,128)S(1)}, f32[40,256]{1,0:T(8,128)S(1)}, u32[]{:S(2)}, u32[]{:S(2)}) collective-permute-start(f32[40,256]{1,0:T(8,128)S(1)} %shard_map.132.refs_0_), channel_id=1, source_target_pairs={{0,8},{4,12},{8,16},{12,20},{16,24},{20,28},{24,0},{28,4},{1,9},{5... | collective-permute-start | bytes 122888 | tf_op jit(solution)/shard_map/ppermute | solution.py:580
  23.0 2.6 %collective-permute-start.7 = (f32[40,256]{1,0:T(8,128)S(1)}, f32[40,256]{1,0:T(8,128)S(1)}, u32[]{:S(2)}, u32[]{:S(2)}) collective-permute-start(f32[40,256]{1,0:T(8,128)S(1)} %shard_map.132.refs_0_), channel_id=1, source_target_pairs={{0,16},{4,20},{8,24},{12,28},{16,0},{20,4},{24,8},{28,12},{1,17},{... | collective-permute-start | bytes 122888 | tf_op jit(solution)/shard_map/ppermute | solution.py:580
  25.6 1.3 %collective-permute-start.8 = (f32[40,256]{1,0:T(8,128)S(1)}, f32[40,256]{1,0:T(8,128)S(1)}, u32[]{:S(2)}, u32[]{:S(2)}) collective-permute-start(f32[40,256]{1,0:T(8,128)S(1)} %shard_map.132.refs_0_), channel_id=1, source_target_pairs={{0,24},{4,28},{8,0},{12,4},{16,8},{20,12},{24,16},{28,20},{1,25},{... | collective-permute-start | bytes 122888 | tf_op jit(solution)/shard_map/ppermute | solution.py:580
  26.9 2.2 %shard_map.131 = (f32[32,256]{1,0:T(8,128)S(1)}, f32[32,256]{1,0:T(8,128)S(1)}, bf16[256,384]{1,0:T(8,128)(2,1)S(1)}, bf16[16,128,256]{2,1,0:T(8,128)(2,1)S(1)}, bf16[16,128,256]{2,1,0:T(8,128)(2,1)S(1)}) custom-call(bf16[256,768]{1,0:T(8,128)(2,1)S(1)} %get-tuple-element.41.mx, bf16[768,256]{1,0:T(8,128)(2,1)S(1)} %get-tuple-element.39.my, ...), custom_call_target="tpu_custom_call" | custom-call | tf_op jit(solution)/shard_map/pallas_call | solution.py:396
  29.2 0.4 %collective-permute-done.8.refs_3_ = f32[40,256]{1,0:T(8,128)S(1)} collective-permute-done((f32[40,256]{1,0:T(8,128)S(1)}, f32[40,256]{1,0:T(8,128)S(1)}, u32[]{:S(2)}, u32[]{:S(2)}) %collective-permute-start.8) | collective-permute-done | bytes 40992 | tf_op jit(solution)/shard_map/ppermute | solution.py:580
  29.6 0.2 shard_map.133
  29.8 1.6 %collective-permute-start.9 = (f32[40,256]{1,0:T(8,128)S(1)}, f32[40,256]{1,0:T(8,128)S(1)}, u32[]{:S(2)}, u32[]{:S(2)}) collective-permute-start(f32[40,256]{1,0:T(8,128)S(1)} %get-tuple-element.68.refs_0_), channel_id=1, source_target_pairs={{0,1},{1,2},{2,3},{3,0},{4,5},{5,6},{6,7},{7,4},{8,9},{9,10},{10,1... | collective-permute-start | bytes 122888 | tf_op jit(solution)/shard_map/ppermute | solution.py:580
  31.4 0.6 %collective-permute-start.10 = (f32[40,256]{1,0:T(8,128)S(1)}, f32[40,256]{1,0:T(8,128)S(1)}, u32[]{:S(2)}, u32[]{:S(2)}) collective-permute-start(f32[40,256]{1,0:T(8,128)S(1)} %get-tuple-element.68.refs_0_), channel_id=1, source_target_pairs={{0,2},{1,3},{2,0},{3,1},{4,6},{5,7},{6,4},{7,5},{8,10},{9,11},{10,... | collective-permute-start | bytes 122888 | tf_op jit(solution)/shard_map/ppermute | solution.py:580
  32.0 2.3 %collective-permute-start.11 = (f32[40,256]{1,0:T(8,128)S(1)}, f32[40,256]{1,0:T(8,128)S(1)}, u32[]{:S(2)}, u32[]{:S(2)}) collective-permute-start(f32[40,256]{1,0:T(8,128)S(1)} %get-tuple-element.68.refs_0_), channel_id=1, source_target_pairs={{0,3},{1,0},{2,1},{3,2},{4,7},{5,4},{6,5},{7,6},{8,11},{9,8},{10,9... | collective-permute-start | bytes 122888 | tf_op jit(solution)/shard_map/ppermute | solution.py:580
  34.3 1.4 %shard_map.134.w_ref = f32[16,256,256]{2,1,0:T(8,128)S(1)} custom-call(bf16[256,384]{1,0:T(8,128)(2,1)S(1)} %get-tuple-element.64.sel, bf16[16,128,256]{2,1,0:T(8,128)(2,1)S(1)} %get-tuple-element.65.high_ref, bf16[16,128,256]{2,1,0:T(8,128)(2,1)S(1)} %get-tuple-element.66.low_ref, ...), custom_call_target="tpu_custom_call", output_to_operand_aliasing={{}: (3, {})} | custom-call | tf_op jit(solution)/shard_map/pallas_call | solution.py:412
  35.7 0.2 collective-permute-done.11.refs_3_
  36.0 2.6 %shard_map.135 = f32[256,16,256]{2,1,0:T(8,128)} custom-call(f32[8,256]{1,0:T(8,128)S(1)} %get-tuple-element.37.xrows, f32[8,256]{1,0:T(8,128)S(1)} %get-tuple-element.38.yrows, f32[48,256]{1,0:T(8,128)S(1)} %get-tuple-element.62.moved, s32[2,256]{1,0:T(2,128)S(1)} %bitcast.6, f32[32,256]{1,0:T(8,128)S(1)} %get-tuple-element.63.zh_ref, ...), custom_call_target="tpu_custom_call" | custom-call | tf_op jit(solution)/shard_map/pallas_call | solution.py:559
  (11 shorter events, 0.0 us)
Async XLA Ops:
  1.9 17.1 %collective-permute-start.2 = (f32[33,16,128]{2,1,0:T(8,128)S(1)}, f32[33,16,128]{2,1,0:T(8,128)S(1)}, u32[]{:S(2)}, u32[]{:S(2)}) collective-permute-start(f32[33,16,128]{2,1,0:T(8,128)S(1)} %get-tuple-element.55), channel_id=1, source_target_pairs={{0,1},{1,0},{2,3},{3,2},{4,5},{5,4},{6,7},{7,6},{8,9},{9,8},{10,11... | collective-permute-start | bytes 811016 | tf_op jit(solution)/shard_map/ppermute | solution.py:575
  4.9 14.1 %collective-permute-start.3 = (f32[33,16,128]{2,1,0:T(8,128)S(1)}, f32[33,16,128]{2,1,0:T(8,128)S(1)}, u32[]{:S(2)}, u32[]{:S(2)}) collective-permute-start(f32[33,16,128]{2,1,0:T(8,128)S(1)} %get-tuple-element.56), channel_id=1, source_target_pairs={{0,2},{1,3},{2,0},{3,1},{4,6},{5,7},{6,4},{7,5},{8,10},{9,11},{10,... | collective-permute-start | bytes 811016 | tf_op jit(solution)/shard_map/ppermute | solution.py:575
  6.4 12.6 %collective-permute-start.4 = (f32[33,16,128]{2,1,0:T(8,128)S(1)}, f32[33,16,128]{2,1,0:T(8,128)S(1)}, u32[]{:S(2)}, u32[]{:S(2)}) collective-permute-start(f32[33,16,128]{2,1,0:T(8,128)S(1)} %get-tuple-element.57), channel_id=1, source_target_pairs={{0,3},{1,2},{2,1},{3,0},{4,7},{5,6},{6,5},{7,4},{8,11},{9,10},{10,... | collective-permute-start | bytes 811016 | tf_op jit(solution)/shard_map/ppermute | solution.py:575
  10.3 8.7 %collective-permute-start = (f32[16,256]{1,0:T(8,128)S(1)}, f32[16,256]{1,0:T(8,128)S(1)}, u32[]{:S(2)}, u32[]{:S(2)}) collective-permute-start(f32[16,256]{1,0:T(8,128)S(1)} %get-tuple-element.50), channel_id=1, source_target_pairs={{0,1},{1,2},{2,3},{3,0},{4,5},{5,6},{6,7},{7,4},{8,9},{9,10},{10,1... | collective-permute-start | bytes 49160 | tf_op jit(solution)/shard_map/ppermute | solution.py:580
  12.3 6.7 %collective-permute-start.1 = (f32[16,256]{1,0:T(8,128)S(1)}, f32[16,256]{1,0:T(8,128)S(1)}, u32[]{:S(2)}, u32[]{:S(2)}) collective-permute-start(f32[16,256]{1,0:T(8,128)S(1)} %get-tuple-element.51), channel_id=1, source_target_pairs={{0,3},{1,0},{2,1},{3,2},{4,7},{5,4},{6,5},{7,6},{8,11},{9,8},{10,9... | collective-permute-start | bytes 49160 | tf_op jit(solution)/shard_map/ppermute | solution.py:580
  20.1 1.3 %collective-permute-start.5 = (f32[40,256]{1,0:T(8,128)S(1)}, f32[40,256]{1,0:T(8,128)S(1)}, u32[]{:S(2)}, u32[]{:S(2)}) collective-permute-start(f32[40,256]{1,0:T(8,128)S(1)} %get-tuple-element.61.mine.mine_ref), channel_id=1, source_target_pairs={{0,4},{4,0},{8,12},{12,8},{16,20},{20,16},{24,28},{28,24},{1,5},{5... | collective-permute-start | bytes 122888 | tf_op jit(solution)/shard_map/ppermute | solution.py:575
  21.4 7.8 %collective-permute-start.6 = (f32[40,256]{1,0:T(8,128)S(1)}, f32[40,256]{1,0:T(8,128)S(1)}, u32[]{:S(2)}, u32[]{:S(2)}) collective-permute-start(f32[40,256]{1,0:T(8,128)S(1)} %shard_map.132.refs_0_), channel_id=1, source_target_pairs={{0,8},{4,12},{8,16},{12,20},{16,24},{20,28},{24,0},{28,4},{1,9},{5... | collective-permute-start | bytes 122888 | tf_op jit(solution)/shard_map/ppermute | solution.py:580
  23.0 6.2 %collective-permute-start.7 = (f32[40,256]{1,0:T(8,128)S(1)}, f32[40,256]{1,0:T(8,128)S(1)}, u32[]{:S(2)}, u32[]{:S(2)}) collective-permute-start(f32[40,256]{1,0:T(8,128)S(1)} %shard_map.132.refs_0_), channel_id=1, source_target_pairs={{0,16},{4,20},{8,24},{12,28},{16,0},{20,4},{24,8},{28,12},{1,17},{... | collective-permute-start | bytes 122888 | tf_op jit(solution)/shard_map/ppermute | solution.py:580
  25.6 4.0 %collective-permute-start.8 = (f32[40,256]{1,0:T(8,128)S(1)}, f32[40,256]{1,0:T(8,128)S(1)}, u32[]{:S(2)}, u32[]{:S(2)}) collective-permute-start(f32[40,256]{1,0:T(8,128)S(1)} %shard_map.132.refs_0_), channel_id=1, source_target_pairs={{0,24},{4,28},{8,0},{12,4},{16,8},{20,12},{24,16},{28,20},{1,25},{... | collective-permute-start | bytes 122888 | tf_op jit(solution)/shard_map/ppermute | solution.py:580
  29.8 5.9 %collective-permute-start.9 = (f32[40,256]{1,0:T(8,128)S(1)}, f32[40,256]{1,0:T(8,128)S(1)}, u32[]{:S(2)}, u32[]{:S(2)}) collective-permute-start(f32[40,256]{1,0:T(8,128)S(1)} %get-tuple-element.68.refs_0_), channel_id=1, source_target_pairs={{0,1},{1,2},{2,3},{3,0},{4,5},{5,6},{6,7},{7,4},{8,9},{9,10},{10,1... | collective-permute-start | bytes 122888 | tf_op jit(solution)/shard_map/ppermute | solution.py:580
  31.4 4.3 %collective-permute-start.10 = (f32[40,256]{1,0:T(8,128)S(1)}, f32[40,256]{1,0:T(8,128)S(1)}, u32[]{:S(2)}, u32[]{:S(2)}) collective-permute-start(f32[40,256]{1,0:T(8,128)S(1)} %get-tuple-element.68.refs_0_), channel_id=1, source_target_pairs={{0,2},{1,3},{2,0},{3,1},{4,6},{5,7},{6,4},{7,5},{8,10},{9,11},{10,... | collective-permute-start | bytes 122888 | tf_op jit(solution)/shard_map/ppermute | solution.py:580
  32.0 4.0 %collective-permute-start.11 = (f32[40,256]{1,0:T(8,128)S(1)}, f32[40,256]{1,0:T(8,128)S(1)}, u32[]{:S(2)}, u32[]{:S(2)}) collective-permute-start(f32[40,256]{1,0:T(8,128)S(1)} %get-tuple-element.68.refs_0_), channel_id=1, source_target_pairs={{0,3},{1,0},{2,1},{3,2},{4,7},{5,4},{6,5},{7,6},{8,11},{9,8},{10,9... | collective-permute-start | bytes 122888 | tf_op jit(solution)/shard_map/ppermute | solution.py:580
  34.3 1.7 %copy-start = (s32[256,2]{0,1:T(2,128)S(1)}, s32[256,2]{0,1:T(2,128)}, u32[]{:S(2)}) copy-start(s32[256,2]{0,1:T(2,128)} %param.25) | copy-start | bytes 6148

commit v6 on v5

--- a/solution.py
+++ b/solution.py
@@ -301,6 +301,7 @@
     rows = frows.shape[1]
     width = payload[0].shape[2]
     nblock = cols // width
+    blocks = cols // LANES
     lane8 = lax.broadcasted_iota(jnp.int32, (8, slots), 1)
     places = jnp.full((8, slots), -1.0, F32)
     for s in range(count):
@@ -330,18 +331,19 @@
         func = frows[f : f + 1, :]
         first = 0.5 * jnp.sum(hl * func, axis=1, keepdims=True)
         last = 0.5 * jnp.sum(hr * func, axis=1, keepdims=True)
-        out[f * planes : (f + 1) * planes, :] = (
-            edge_ref[f] + jnp.where(at == 0, first, 0.0) + jnp.where(at == cols - 1, last, 0.0)
-        )
+        edge = edge_ref[f] + jnp.where(at == 0, first, 0.0) + jnp.where(at == cols - 1, last, 0.0)
+        for b in range(blocks):
+            row = (f * blocks + b) * planes
+            out[row : row + planes, :] = edge[:, b * LANES : (b + 1) * LANES]
     spread = [jnp.broadcast_to(column[:, f : f + 1], (slots, LANES)) for f in range(2)]
     for p in range(planes):
-        for b in range(cols // LANES):
+        for b in range(blocks):
             lanes = slice(b * LANES, (b + 1) * LANES)
             value = wall_ref[p, :, lanes]
             for f in range(2):
-                at = f * planes + p
-                out[at : at + 1, lanes] = out[at : at + 1, lanes] + jnp.sum(value * spread[f], axis=0, keepdims=True)
-    out[2 * planes : 2 * planes + 8, :] = scal[0:8, :]
+                at = (f * blocks + b) * planes + p
+                out[at : at + 1, :] = out[at : at + 1, :] + jnp.sum(value * spread[f], axis=0, keepdims=True)
+    out[2 * blocks * planes : 2 * blocks * planes + 8, :] = scal[0:8, 0:LANES]
 
 
 def x_edges(edge, frows, scal, left, right, payload, room):
@@ -350,7 +352,7 @@
     slots = count * room
     return call(
         functools.partial(x_edge_kernel, count, room),
-        [struct(2 * planes + 8, cols), struct(rows, slots, dtype=BF16), struct(planes, slots, cols)],
+        [struct(2 * planes * (cols // LANES) + 8, LANES), struct(rows, slots, dtype=BF16), struct(planes, slots, cols)],
         [VMEM] * (5 + count),
         8,
     )(edge, frows, scal, left, right, *payload)
@@ -418,24 +420,36 @@
     )(sel, high, low, w)
 
 
+def pack_edges(first, second, scalars):
+    blocks = range(first.shape[1] // LANES)
+    pieces = [value[:, b * LANES : (b + 1) * LANES] for value in (first, second) for b in blocks]
+    return jnp.concatenate(pieces + [scalars[:, 0:LANES]], 0)
+
+
+def unpack_edges(flat, planes):
+    blocks = (flat.shape[0] - 8) // (2 * planes)
+    pieces = [flat[b * planes : (b + 1) * planes] for b in range(2 * blocks)]
+    scalars = jnp.concatenate([flat[2 * blocks * planes :]] * blocks, 1)
+    return jnp.concatenate(pieces[:blocks], 1), jnp.concatenate(pieces[blocks:], 1), scalars
+
+
 def chain(parts, count, me, planes, f_in):
-    lanes = parts.shape[2]
-    zero = jnp.zeros((planes, lanes), F32)
+    zero = jnp.zeros(f_in.shape[1:], F32)
+    edges = [unpack_edges(parts[k], planes) for k in range(count)]
     f, mine_f = zero, zero
     for k in range(count):
         f_in[k] = f
         mine_f = jnp.where(k == me, f, mine_f)
-        f = parts[k, 0:planes, :] + parts[k, 2 * planes : 2 * planes + 1, :] * f
+        f = edges[k][0] + edges[k][2][0:1] * f
     g, mine_g = zero, zero
     for k in range(count - 1, -1, -1):
-        scal = parts[k, 2 * planes : 2 * planes + 8, :]
+        scal = edges[k][2]
         mine_g = jnp.where(k == me, g, mine_g)
-        g = parts[k, planes : 2 * planes, :] + scal[1:2] * f_in[k] + scal[2:3] * g
+        g = edges[k][1] + scal[1:2] * f_in[k] + scal[2:3] * g
     return mine_f, mine_g
 
 
-def pair_kernel(mine, other, out):
-    planes = (mine.shape[0] - 8) // 2
+def pair_kernel(planes, mine, other, out):
     odd = lax.rem(lax.axis_index("gx"), 2) == 1
     left = jnp.where(odd, other[...], mine[...])
     right = jnp.where(odd, mine[...], other[...])
@@ -443,18 +457,16 @@
 
 
 def joined(left, right, planes):
-    a, b, s = left[0:planes], left[planes : 2 * planes], left[2 * planes :]
-    c, d, t = right[0:planes], right[planes : 2 * planes], right[2 * planes :]
+    a, b, s = unpack_edges(left, planes)
+    c, d, t = unpack_edges(right, planes)
     l0, c0, u0 = s[0:1], s[1:2], s[2:3]
     l1, c1, u1 = t[0:1], t[1:2], t[2:3]
-    return jnp.concatenate(
-        [c + l1 * a, b + u0 * (d + c1 * a), l0 * l1, c0 + u0 * c1 * l0, u0 * u1, t[3:8]],
-        0,
-    )
-
-
-def pair(mine, other):
-    return call(pair_kernel, struct(*mine.shape), [VMEM, VMEM], 8)(mine, other)
+    scalars = jnp.concatenate([l0 * l1, c0 + u0 * c1 * l0, u0 * u1, t[3:8]], 0)
+    return pack_edges(c + l1 * a, b + u0 * (d + c1 * a), scalars)
+
+
+def pair(mine, other, planes):
+    return call(functools.partial(pair_kernel, planes), struct(*mine.shape), [VMEM, VMEM], 8)(mine, other)
 
 
 def gather_parts(me, parts, received, shifts):
@@ -473,14 +485,14 @@
     f, g = chain(parts, count, place, planes, f_in)
     mine, other = mine_ref[...], other_ref[...]
     left, right = jnp.where(odd, other, mine), jnp.where(odd, mine, other)
-    a, ls = left[0:planes], left[2 * planes :]
-    d, rs = right[planes : 2 * planes], right[2 * planes :]
+    a, _, ls = unpack_edges(left, planes)
+    _, d, rs = unpack_edges(right, planes)
     f_mid = a + ls[0:1] * f
     g_mid = d + rs[1:2] * f_mid + rs[2:3] * g
     in_f, in_b = jnp.where(odd, f_mid, f), jnp.where(odd, g, g_mid)
-    ms = mine[2 * planes :]
-    first = mine[planes : 2 * planes] + ms[1:2] * in_f + ms[2:3] * in_b
-    before_s = jnp.where(odd, ls, parts[jnp.maximum(place - 1, 0), 2 * planes : 2 * planes + 8, :])
+    _, mine_b, ms = unpack_edges(mine, planes)
+    first = mine_b + ms[1:2] * in_f + ms[2:3] * in_b
+    before_s = jnp.where(odd, ls, unpack_edges(parts[jnp.maximum(place - 1, 0)], planes)[2])
     before = jnp.where(me > 0, before_s[3:4] * in_f + before_s[4:5] * first, 0.0)
     low, high = s_ref[0:planes, :], s_ref[planes : 2 * planes, :]
     f0, f1 = yrows[4:5, :], yrows[5:6, :]
@@ -488,22 +500,20 @@
         c = xrows[index : index + 1, :]
         low = low + jnp.sum(value * f0, axis=1, keepdims=True) * c
         high = high + jnp.sum(value * f1, axis=1, keepdims=True) * c
-    out[0:planes, :] = low
-    out[planes : 2 * planes, :] = high
-    out[2 * planes : 2 * planes + 8, :] = scal[8:16, :]
+    out[...] = pack_edges(low, high, scal[8:16, :])
     moved[...] = bf16_dot(right_of(jnp.concatenate([in_f, in_b, before], 0), 1), my[...], ((1,), (0,)))
 
 
 def x_join(my, xrows, yrows, scal, s, mine, other, received, shifts):
     count = len(received)
-    height, cols = received[0].shape
+    height, cols = received[0].shape[0], my.shape[1]
     planes, rows = s.shape[0] // 2, s.shape[1]
     return call(
         functools.partial(x_join_kernel, count, shifts),
-        [struct(2 * planes + 8, rows), struct(3 * planes, cols)],
+        [struct(2 * planes * (rows // LANES) + 8, LANES), struct(3 * planes, cols)],
         [VMEM] * (7 + count),
         8,
-        scratch=[pltpu.VMEM((count, height, cols), F32), pltpu.VMEM((count, planes, cols), F32)],
+        scratch=[pltpu.VMEM((count, height, LANES), F32), pltpu.VMEM((count, planes, cols), F32)],
     )(my, xrows, yrows, scal, s, mine, other, *received)
 
 
@@ -563,7 +573,7 @@
         12,
         out_specs=HBM,
         scratch=[
-            pltpu.VMEM((count, height, rows), F32),
+            pltpu.VMEM((count, height, LANES), F32),
             pltpu.VMEM((count, planes, rows), F32),
             pltpu.VMEM((planes, rows, cols), F32),
             pltpu.SemaphoreType.DMA((planes,)),
@@ -617,7 +627,7 @@
     w, sv, edge = lax.optimization_barrier((w, sv, edge))
     mine, chosen, wall = x_edges(edge, frows, scal, left, right, payload, room)
     other = swap(mine, "gx", 1)
-    both = pair(mine, other)
+    both = pair(mine, other, planes)
     shifts = list(range(n_x // 2))
     received = [rotate(both, "gx", 2 * s) if s else both for s in shifts]
     s_edge, zh, sel, high, low = wall_edges(n_y, mx, my, aux, yrows, sv, left, right, chosen, wall)

time: 38.7 us -> 38.6 us (level)
  no operation moved by 1% of the time
where the time goes in v6:
time: 38.6 us; the launch traced here: 38.5 us
  Pallas kernels  18.3 us (47%)
  starting transfers between devices  17.7 us (46%)
  waiting for transfers between devices  2.39 us (6%)
    ppermute x8, starting transfers between devices, rotate(): lax.ppermute(value, axis, [(i, (i + shift) % count) for i in range(count)])  13.1 us
    pallas_call x1, Pallas kernels, velocity_part(): call(functools.partial(velocity_kernel, 4), [struct(planes, rows, cols),...  5.04 us
    ppermute x4, starting transfers between devices, swap(): lax.ppermute(value, axis, [(i, i ^ mask) for i in range(lax.axis_size(axi...  4.62 us
    pallas_call x1, Pallas kernels, factors(): call(factor_kernel, [struct(rows, 3 * rows, dtype=BF16), struct(3 * cols,...  3.88 us
    pallas_call x1, Pallas kernels, finish(): call(functools.partial(finish_kernel, count, shifts), struct(rows, planes...  2.58 us
    pallas_call x1, Pallas kernels, wall_edges(): call(functools.partial(wall_kernel, count), [struct(2 * planes, rows), st...  2.19 us
    pallas_call x1, Pallas kernels, pack(): call(functools.partial(pack_kernel, count, room), [struct(room + 1, plane...  1.85 us
    pallas_call x1, Pallas kernels, wall_sweep(): call(wall_sweep_kernel, struct(*w.shape), [VMEM] * 4, 8, input_output_ali...  1.44 us
  transfers between devices with their start and end apart: 12, of which 4 were waited for; matrix products, arithmetic and copies ran while one was open for 0% of the time, Pallas kernels for 33%

profile of v6, /device:TPU:0, one launch (start us, length us, event | category | flops | bytes accessed | tf_op | source)
XLA Modules:
  0.0 38.5 jit_solution(15014282766619551623)
XLA Ops:
  0.0 1.8 %shard_map.129 = (f32[33,16,128]{2,1,0:T(8,128)S(1)}, f32[33,16,128]{2,1,0:T(8,128)S(1)}, f32[33,16,128]{2,1,0:T(8,128)S(1)}, f32[33,16,128]{2,1,0:T(8,128)S(1)}) custom-call(s32[64]{0:T(128)} %bitcast.11, s32[64]{0:T(128)} %offset_ref.1, f32[64,16,128]{2,1,0:T(8,128)} %force_ref.1), custom_call_target="tpu_custom_call" | custom-call | tf_op jit(solution)/shard_map/pallas_call | solution.py:104
  1.9 3.0 %collective-permute-start.2 = (f32[33,16,128]{2,1,0:T(8,128)S(1)}, f32[33,16,128]{2,1,0:T(8,128)S(1)}, u32[]{:S(2)}, u32[]{:S(2)}) collective-permute-start(f32[33,16,128]{2,1,0:T(8,128)S(1)} %get-tuple-element.55), channel_id=1, source_target_pairs={{0,1},{1,0},{2,3},{3,2},{4,5},{5,4},{6,7},{7,6},{8,9},{9,8},{10,11... | collective-permute-start | bytes 811016 | tf_op jit(solution)/shard_map/ppermute | solution.py:585
  4.9 1.5 %collective-permute-start.3 = (f32[33,16,128]{2,1,0:T(8,128)S(1)}, f32[33,16,128]{2,1,0:T(8,128)S(1)}, u32[]{:S(2)}, u32[]{:S(2)}) collective-permute-start(f32[33,16,128]{2,1,0:T(8,128)S(1)} %get-tuple-element.56), channel_id=1, source_target_pairs={{0,2},{1,3},{2,0},{3,1},{4,6},{5,7},{6,4},{7,5},{8,10},{9,11},{10,... | collective-permute-start | bytes 811016 | tf_op jit(solution)/shard_map/ppermute | solution.py:585
  6.4 0.0 collective-permute-start.4
  6.4 3.9 %shard_map.127 = (bf16[256,768]{1,0:T(8,128)(2,1)S(1)}, bf16[768,256]{1,0:T(8,128)(2,1)S(1)}, bf16[768,128]{1,0:T(8,128)(2,1)S(1)}, bf16[768,256]{1,0:T(8,128)(2...) custom-call(f32[256,16,256]{2,1,0:T(8,128)} %v_hbm.1, ...), custom_call_target="tpu_custom_call" | custom-call | tf_op jit(solution)/shard_map/pallas_call | solution.py:240
  10.3 2.0 %collective-permute-start = (f32[16,256]{1,0:T(8,128)S(1)}, f32[16,256]{1,0:T(8,128)S(1)}, u32[]{:S(2)}, u32[]{:S(2)}) collective-permute-start(f32[16,256]{1,0:T(8,128)S(1)} %get-tuple-element.50), channel_id=1, source_target_pairs={{0,1},{1,2},{2,3},{3,0},{4,5},{5,6},{6,7},{7,4},{8,9},{9,10},{10,1... | collective-permute-start | bytes 49160 | tf_op jit(solution)/shard_map/ppermute | solution.py:590
  12.3 1.0 %collective-permute-start.1 = (f32[16,256]{1,0:T(8,128)S(1)}, f32[16,256]{1,0:T(8,128)S(1)}, u32[]{:S(2)}, u32[]{:S(2)}) collective-permute-start(f32[16,256]{1,0:T(8,128)S(1)} %get-tuple-element.51), channel_id=1, source_target_pairs={{0,3},{1,0},{2,1},{3,2},{4,7},{5,4},{6,5},{7,6},{8,11},{9,8},{10,9... | collective-permute-start | bytes 49160 | tf_op jit(solution)/shard_map/ppermute | solution.py:590
  13.3 5.0 %shard_map.128 = (f32[16,256,256]{2,1,0:T(8,128)S(1)}, f32[256,128]{1,0:T(8,128)S(1)}) custom-call(bf16[256,768]{1,0:T(8,128)(2,1)S(1)} %get-tuple-element.41.mx, bf16[768,256]{1,0:T(8,128)(2,1)S(1)} %get-tuple-element.43.my_t, bf16[768,128]{1,0:T(8,128)(2,1)S(1)} %get-tuple-element.44.aux_t, f32[16,256,256]{2,1,0:T(8,128)S(1)} %get-tuple-element.45.v_ref), custom_call_target="tpu_custom_call" | custom-call | tf_op jit(solution)/shard_map/pallas_call | solution.py:285
  18.4 0.6 %collective-permute-done.left_ref = f32[16,256]{1,0:T(8,128)S(1)} collective-permute-done((f32[16,256]{1,0:T(8,128)S(1)}, f32[16,256]{1,0:T(8,128)S(1)}, u32[]{:S(2)}, u32[]{:S(2)}) %collective-permute-start) | collective-permute-done | bytes 16416 | tf_op jit(solution)/shard_map/ppermute | solution.py:590
  19.0 1.1 %shard_map.130 = (f32[72,128]{1,0:T(8,128)S(1)}, bf16[256,128]{1,0:T(8,128)(2,1)S(1)}, f32[16,128,256]{2,1,0:T(8,128)S(1)}) custom-call(f32[2,16,256]{2,1,0:T(8,128)S(1)} %get-tuple-element.52.edge_ref, f32[8,256]{1,0:T(8,128)S(1)} %get-tuple-element.53.frows, f32[16,256]{1,0:T(8,128)S(1)} %get-tuple-element.40.scal, ...), custom_call_target="tpu_custom_call" | custom-call | tf_op jit(solution)/shard_map/pallas_call | solution.py:353
  20.1 0.1 collective-permute-start.5
  20.1 1.2 %collective-permute-done.5.other.other_ref = f32[72,128]{1,0:T(8,128)S(1)} collective-permute-done((f32[72,128]{1,0:T(8,128)S(1)}, f32[72,128]{1,0:T(8,128)S(1)}, u32[]{:S(2)}, u32[]{:S(2)}) %collective-permute-start.5) | collective-permute-done | bytes 36896 | tf_op jit(solution)/shard_map/ppermute | solution.py:585
  21.4 1.6 %collective-permute-start.6 = (f32[72,128]{1,0:T(8,128)S(1)}, f32[72,128]{1,0:T(8,128)S(1)}, u32[]{:S(2)}, u32[]{:S(2)}) collective-permute-start(f32[72,128]{1,0:T(8,128)S(1)} %shard_map.132.refs_0_), channel_id=1, source_target_pairs={{0,8},{4,12},{8,16},{12,20},{16,24},{20,28},{24,0},{28,4},{1,9},{5... | collective-permute-start | bytes 110600 | tf_op jit(solution)/shard_map/ppermute | solution.py:590
  23.0 2.6 %collective-permute-start.7 = (f32[72,128]{1,0:T(8,128)S(1)}, f32[72,128]{1,0:T(8,128)S(1)}, u32[]{:S(2)}, u32[]{:S(2)}) collective-permute-start(f32[72,128]{1,0:T(8,128)S(1)} %shard_map.132.refs_0_), channel_id=1, source_target_pairs={{0,16},{4,20},{8,24},{12,28},{16,0},{20,4},{24,8},{28,12},{1,17},{... | collective-permute-start | bytes 110600 | tf_op jit(solution)/shard_map/ppermute | solution.py:590
  25.6 1.3 %collective-permute-start.8 = (f32[72,128]{1,0:T(8,128)S(1)}, f32[72,128]{1,0:T(8,128)S(1)}, u32[]{:S(2)}, u32[]{:S(2)}) collective-permute-start(f32[72,128]{1,0:T(8,128)S(1)} %shard_map.132.refs_0_), channel_id=1, source_target_pairs={{0,24},{4,28},{8,0},{12,4},{16,8},{20,12},{24,16},{28,20},{1,25},{... | collective-permute-start | bytes 110600 | tf_op jit(solution)/shard_map/ppermute | solution.py:590
  26.9 2.2 %shard_map.131 = (f32[32,256]{1,0:T(8,128)S(1)}, f32[32,256]{1,0:T(8,128)S(1)}, bf16[256,384]{1,0:T(8,128)(2,1)S(1)}, bf16[16,128,256]{2,1,0:T(8,128)(2,1)S(1)}, bf16[16,128,256]{2,1,0:T(8,128)(2,1)S(1)}) custom-call(bf16[256,768]{1,0:T(8,128)(2,1)S(1)} %get-tuple-element.41.mx, bf16[768,256]{1,0:T(8,128)(2,1)S(1)} %get-tuple-element.39.my, ...), custom_call_target="tpu_custom_call" | custom-call | tf_op jit(solution)/shard_map/pallas_call | solution.py:398
  29.2 0.4 %collective-permute-done.8.refs_3_ = f32[72,128]{1,0:T(8,128)S(1)} collective-permute-done((f32[72,128]{1,0:T(8,128)S(1)}, f32[72,128]{1,0:T(8,128)S(1)}, u32[]{:S(2)}, u32[]{:S(2)}) %collective-permute-start.8) | collective-permute-done | bytes 36896 | tf_op jit(solution)/shard_map/ppermute | solution.py:590
  29.5 0.2 shard_map.133
  29.7 1.6 %collective-permute-start.9 = (f32[72,128]{1,0:T(8,128)S(1)}, f32[72,128]{1,0:T(8,128)S(1)}, u32[]{:S(2)}, u32[]{:S(2)}) collective-permute-start(f32[72,128]{1,0:T(8,128)S(1)} %get-tuple-element.68.refs_0_), channel_id=1, source_target_pairs={{0,1},{1,2},{2,3},{3,0},{4,5},{5,6},{6,7},{7,4},{8,9},{9,10},{10,1... | collective-permute-start | bytes 110600 | tf_op jit(solution)/shard_map/ppermute | solution.py:590
  31.4 0.6 %collective-permute-start.10 = (f32[72,128]{1,0:T(8,128)S(1)}, f32[72,128]{1,0:T(8,128)S(1)}, u32[]{:S(2)}, u32[]{:S(2)}) collective-permute-start(f32[72,128]{1,0:T(8,128)S(1)} %get-tuple-element.68.refs_0_), channel_id=1, source_target_pairs={{0,2},{1,3},{2,0},{3,1},{4,6},{5,7},{6,4},{7,5},{8,10},{9,11},{10,... | collective-permute-start | bytes 110600 | tf_op jit(solution)/shard_map/ppermute | solution.py:590
  31.9 2.3 %collective-permute-start.11 = (f32[72,128]{1,0:T(8,128)S(1)}, f32[72,128]{1,0:T(8,128)S(1)}, u32[]{:S(2)}, u32[]{:S(2)}) collective-permute-start(f32[72,128]{1,0:T(8,128)S(1)} %get-tuple-element.68.refs_0_), channel_id=1, source_target_pairs={{0,3},{1,0},{2,1},{3,2},{4,7},{5,4},{6,5},{7,6},{8,11},{9,8},{10,9... | collective-permute-start | bytes 110600 | tf_op jit(solution)/shard_map/ppermute | solution.py:590
  34.2 1.4 %shard_map.134.w_ref = f32[16,256,256]{2,1,0:T(8,128)S(1)} custom-call(bf16[256,384]{1,0:T(8,128)(2,1)S(1)} %get-tuple-element.64.sel, bf16[16,128,256]{2,1,0:T(8,128)(2,1)S(1)} %get-tuple-element.65.high_ref, bf16[16,128,256]{2,1,0:T(8,128)(2,1)S(1)} %get-tuple-element.66.low_ref, ...), custom_call_target="tpu_custom_call", output_to_operand_aliasing={{}: (3, {})} | custom-call | tf_op jit(solution)/shard_map/pallas_call | solution.py:414
  35.7 0.2 collective-permute-done.11.refs_3_
  35.9 2.6 %shard_map.135 = f32[256,16,256]{2,1,0:T(8,128)} custom-call(f32[8,256]{1,0:T(8,128)S(1)} %get-tuple-element.37.xrows, f32[8,256]{1,0:T(8,128)S(1)} %get-tuple-element.38.yrows, f32[48,256]{1,0:T(8,128)S(1)} %get-tuple-element.62.moved, s32[2,256]{1,0:T(2,128)S(1)} %bitcast.6, f32[32,256]{1,0:T(8,128)S(1)} %get-tuple-element.63.zh_ref, ...), custom_call_target="tpu_custom_call" | custom-call | tf_op jit(solution)/shard_map/pallas_call | solution.py:569
  (11 shorter events, 0.0 us)
Async XLA Ops:
  1.9 17.1 %collective-permute-start.2 = (f32[33,16,128]{2,1,0:T(8,128)S(1)}, f32[33,16,128]{2,1,0:T(8,128)S(1)}, u32[]{:S(2)}, u32[]{:S(2)}) collective-permute-start(f32[33,16,128]{2,1,0:T(8,128)S(1)} %get-tuple-element.55), channel_id=1, source_target_pairs={{0,1},{1,0},{2,3},{3,2},{4,5},{5,4},{6,7},{7,6},{8,9},{9,8},{10,11... | collective-permute-start | bytes 811016 | tf_op jit(solution)/shard_map/ppermute | solution.py:585
  4.9 14.1 %collective-permute-start.3 = (f32[33,16,128]{2,1,0:T(8,128)S(1)}, f32[33,16,128]{2,1,0:T(8,128)S(1)}, u32[]{:S(2)}, u32[]{:S(2)}) collective-permute-start(f32[33,16,128]{2,1,0:T(8,128)S(1)} %get-tuple-element.56), channel_id=1, source_target_pairs={{0,2},{1,3},{2,0},{3,1},{4,6},{5,7},{6,4},{7,5},{8,10},{9,11},{10,... | collective-permute-start | bytes 811016 | tf_op jit(solution)/shard_map/ppermute | solution.py:585
  6.4 12.6 %collective-permute-start.4 = (f32[33,16,128]{2,1,0:T(8,128)S(1)}, f32[33,16,128]{2,1,0:T(8,128)S(1)}, u32[]{:S(2)}, u32[]{:S(2)}) collective-permute-start(f32[33,16,128]{2,1,0:T(8,128)S(1)} %get-tuple-element.57), channel_id=1, source_target_pairs={{0,3},{1,2},{2,1},{3,0},{4,7},{5,6},{6,5},{7,4},{8,11},{9,10},{10,... | collective-permute-start | bytes 811016 | tf_op jit(solution)/shard_map/ppermute | solution.py:585
  10.3 8.7 %collective-permute-start = (f32[16,256]{1,0:T(8,128)S(1)}, f32[16,256]{1,0:T(8,128)S(1)}, u32[]{:S(2)}, u32[]{:S(2)}) collective-permute-start(f32[16,256]{1,0:T(8,128)S(1)} %get-tuple-element.50), channel_id=1, source_target_pairs={{0,1},{1,2},{2,3},{3,0},{4,5},{5,6},{6,7},{7,4},{8,9},{9,10},{10,1... | collective-permute-start | bytes 49160 | tf_op jit(solution)/shard_map/ppermute | solution.py:590
  12.3 6.7 %collective-permute-start.1 = (f32[16,256]{1,0:T(8,128)S(1)}, f32[16,256]{1,0:T(8,128)S(1)}, u32[]{:S(2)}, u32[]{:S(2)}) collective-permute-start(f32[16,256]{1,0:T(8,128)S(1)} %get-tuple-element.51), channel_id=1, source_target_pairs={{0,3},{1,0},{2,1},{3,2},{4,7},{5,4},{6,5},{7,6},{8,11},{9,8},{10,9... | collective-permute-start | bytes 49160 | tf_op jit(solution)/shard_map/ppermute | solution.py:590
  20.1 1.3 %collective-permute-start.5 = (f32[72,128]{1,0:T(8,128)S(1)}, f32[72,128]{1,0:T(8,128)S(1)}, u32[]{:S(2)}, u32[]{:S(2)}) collective-permute-start(f32[72,128]{1,0:T(8,128)S(1)} %get-tuple-element.61.mine.mine_ref), channel_id=1, source_target_pairs={{0,4},{4,0},{8,12},{12,8},{16,20},{20,16},{24,28},{28,24},{1,5},{5... | collective-permute-start | bytes 110600 | tf_op jit(solution)/shard_map/ppermute | solution.py:585
  21.4 7.8 %collective-permute-start.6 = (f32[72,128]{1,0:T(8,128)S(1)}, f32[72,128]{1,0:T(8,128)S(1)}, u32[]{:S(2)}, u32[]{:S(2)}) collective-permute-start(f32[72,128]{1,0:T(8,128)S(1)} %shard_map.132.refs_0_), channel_id=1, source_target_pairs={{0,8},{4,12},{8,16},{12,20},{16,24},{20,28},{24,0},{28,4},{1,9},{5... | collective-permute-start | bytes 110600 | tf_op jit(solution)/shard_map/ppermute | solution.py:590
  23.0 6.2 %collective-permute-start.7 = (f32[72,128]{1,0:T(8,128)S(1)}, f32[72,128]{1,0:T(8,128)S(1)}, u32[]{:S(2)}, u32[]{:S(2)}) collective-permute-start(f32[72,128]{1,0:T(8,128)S(1)} %shard_map.132.refs_0_), channel_id=1, source_target_pairs={{0,16},{4,20},{8,24},{12,28},{16,0},{20,4},{24,8},{28,12},{1,17},{... | collective-permute-start | bytes 110600 | tf_op jit(solution)/shard_map/ppermute | solution.py:590
  25.6 4.0 %collective-permute-start.8 = (f32[72,128]{1,0:T(8,128)S(1)}, f32[72,128]{1,0:T(8,128)S(1)}, u32[]{:S(2)}, u32[]{:S(2)}) collective-permute-start(f32[72,128]{1,0:T(8,128)S(1)} %shard_map.132.refs_0_), channel_id=1, source_target_pairs={{0,24},{4,28},{8,0},{12,4},{16,8},{20,12},{24,16},{28,20},{1,25},{... | collective-permute-start | bytes 110600 | tf_op jit(solution)/shard_map/ppermute | solution.py:590
  29.7 5.9 %collective-permute-start.9 = (f32[72,128]{1,0:T(8,128)S(1)}, f32[72,128]{1,0:T(8,128)S(1)}, u32[]{:S(2)}, u32[]{:S(2)}) collective-permute-start(f32[72,128]{1,0:T(8,128)S(1)} %get-tuple-element.68.refs_0_), channel_id=1, source_target_pairs={{0,1},{1,2},{2,3},{3,0},{4,5},{5,6},{6,7},{7,4},{8,9},{9,10},{10,1... | collective-permute-start | bytes 110600 | tf_op jit(solution)/shard_map/ppermute | solution.py:590
  31.4 4.3 %collective-permute-start.10 = (f32[72,128]{1,0:T(8,128)S(1)}, f32[72,128]{1,0:T(8,128)S(1)}, u32[]{:S(2)}, u32[]{:S(2)}) collective-permute-start(f32[72,128]{1,0:T(8,128)S(1)} %get-tuple-element.68.refs_0_), channel_id=1, source_target_pairs={{0,2},{1,3},{2,0},{3,1},{4,6},{5,7},{6,4},{7,5},{8,10},{9,11},{10,... | collective-permute-start | bytes 110600 | tf_op jit(solution)/shard_map/ppermute | solution.py:590
  31.9 4.0 %collective-permute-start.11 = (f32[72,128]{1,0:T(8,128)S(1)}, f32[72,128]{1,0:T(8,128)S(1)}, u32[]{:S(2)}, u32[]{:S(2)}) collective-permute-start(f32[72,128]{1,0:T(8,128)S(1)} %get-tuple-element.68.refs_0_), channel_id=1, source_target_pairs={{0,3},{1,0},{2,1},{3,2},{4,7},{5,4},{6,5},{7,6},{8,11},{9,8},{10,9... | collective-permute-start | bytes 110600 | tf_op jit(solution)/shard_map/ppermute | solution.py:590
  34.2 1.7 %copy-start = (s32[256,2]{0,1:T(2,128)S(1)}, s32[256,2]{0,1:T(2,128)}, u32[]{:S(2)}) copy-start(s32[256,2]{0,1:T(2,128)} %param.25) | copy-start | bytes 6148

commit v7 on v6

--- a/solution.py
+++ b/solution.py
@@ -132,9 +132,9 @@
 
 
 def factor_kernel(v_hbm, *refs):
-    given, (mx, my, aux, my_t, aux_t, xrows, yrows, frows, scal) = refs[:8], refs[8:17]
-    v_ref, edge_ref, first_ref, last_ref = refs[17:21]
-    fetched, (sem, v_sem) = refs[21:29], refs[29:]
+    given, (mx, my, my_t, xrows, yrows, frows, scal) = refs[:8], refs[8:15]
+    v_ref, edge_ref, first_ref, last_ref = refs[15:19]
+    fetched, (sem, v_sem) = refs[19:27], refs[27:]
     planes, rows, cols = v_ref.shape
     copies = [pltpu.make_async_copy(given[i], fetched[i], sem.at[i]) for i in range(8)]
     for copy in copies:
@@ -173,11 +173,6 @@
     zero_y = jnp.zeros((1, rows_y), F32)
     m0, m1 = 0.5 * turned[0:8][0:1], 0.5 * turned[rows_y - 8 : rows_y][7:8]
     yrows[...] = jnp.concatenate([uy_lc, ucv, m0, m1, f0, f1, zero_y, zero_y], 0)
-    lane_y = lax.broadcasted_iota(jnp.int32, (rows_y, 128), 1)
-    pair_of = jnp.concatenate([f0, f1, pad_y[:6]], 0).T
-    spread_cols = jnp.where(lane_y < 64, pair_of[:, 0:1], pair_of[:, 1:2])
-    aux[...] = left_of(spread_cols, 0)
-    aux_t[...] = left_of(half_shift_rows(spread_cols), 0)
 
     def spread(value, index, width):
         return jnp.broadcast_to(value[:, index : index + 1], (1, width))
@@ -242,9 +237,7 @@
         [
             struct(rows, 3 * rows, dtype=BF16),
             struct(3 * cols, cols, dtype=BF16),
-            struct(3 * cols, 128, dtype=BF16),
             struct(3 * cols, cols, dtype=BF16),
-            struct(3 * cols, 128, dtype=BF16),
             struct(8, rows),
             struct(8, cols),
             struct(8, rows),
@@ -264,30 +257,31 @@
     )(pin(velocity), *[pin(g) for g in given])
 
 
-def velocity_kernel(some, mx, my_t, aux_t, v_ref, w_ref, s_ref):
+def velocity_kernel(some, mx, my_t, yrows, v_ref, w_ref, s_ref):
     planes, rows, cols = v_ref.shape
     lane = lax.broadcasted_iota(jnp.int32, (rows, LANES), 1)
     total = jnp.zeros((rows, LANES), F32)
+    last = half_shift_lanes(yrows[4:5, :])
     for q in range(0, planes, some):
         flat = right_of(v_ref[q : q + some].reshape(some * rows, cols), 1)
         r = bf16_dot(flat, my_t[...], ((1,), (0,)))
-        t = bf16_dot(flat, aux_t[...], ((1,), (0,)))
         for i in range(some):
             p = q + i
             here = slice(i * rows, (i + 1) * rows)
-            total = jnp.where((lane == p) | (lane == 64 + p), t[here], total)
+            total = jnp.where(lane == p, jnp.sum(v_ref[p] * last, axis=1, keepdims=True), total)
+            total = jnp.where(lane == 64 + p, r[here][:, 0:1], total)
             w_ref[p] = bf16_dot(mx[...], right_of(r[here], 0), ((1,), (0,)))
     s_ref[...] = total
 
 
-def velocity_part(mx, my_t, aux_t, velocity):
+def velocity_part(mx, my_t, yrows, velocity):
     planes, rows, cols = velocity.shape
     return call(
         functools.partial(velocity_kernel, 4),
         [struct(planes, rows, cols), struct(rows, LANES)],
         [VMEM] * 4,
         16,
-    )(mx, my_t, aux_t, velocity)
+    )(mx, my_t, yrows, velocity)
 
 
 def halos(count, left_ref, right_ref):
@@ -358,7 +352,7 @@
     )(edge, frows, scal, left, right, *payload)
 
 
-def wall_kernel(count, mx, my, aux, yrows, sv_ref, left_ref, right_ref, chosen_ref, wall_ref, s_ref, zh_ref, sel_ref, high_ref, low_ref):
+def wall_kernel(count, mx, my, yrows, sv_ref, left_ref, right_ref, chosen_ref, wall_ref, s_ref, zh_ref, sel_ref, high_ref, low_ref):
     planes, slots, cols = wall_ref.shape
     rows = mx.shape[0]
     hl, hr = halos(count, left_ref, right_ref)
@@ -376,13 +370,14 @@
     for q in range(0, planes, some):
         flat = wall_ref[q : q + some].reshape(some * slots, cols)
         wc = right_of(flat, 1)
-        t = bf16_dot(wc, aux[...], ((1,), (0,)))
-        high, low = split(bf16_dot(wc, my[...], ((1,), (0,))))
+        r = bf16_dot(wc, my[...], ((1,), (0,)))
+        high, low = split(r)
         high_ref[q : q + some] = high.reshape(some, slots, cols)
         low_ref[q : q + some] = low.reshape(some, slots, cols)
         for i in range(some):
             p = q + i
-            total = jnp.where((lane == p) | (lane == 64 + p), t[i * slots : (i + 1) * slots], total)
+            total = jnp.where(lane == p, jnp.sum(wall_ref[p] * yrows[4:5, :], axis=1, keepdims=True), total)
+            total = jnp.where(lane == 64 + p, r[i * slots : (i + 1) * slots, 0:1], total)
     left = jnp.concatenate([m, sel], 1)
     turned = bf16_dot(left, jnp.concatenate([right_of(sv_ref[...], 0), right_of(total, 0)], 0), ((1,), (0,))).T
     low, high = turned[0:planes], turned[64 : 64 + planes]
@@ -392,16 +387,16 @@
     s_ref[planes : 2 * planes, :] = high + 0.5 * (zl * f1[:, 0:1] + zr * f1[:, cols - 1 : cols])
 
 
-def wall_edges(count, mx, my, aux, yrows, sv, left, right, chosen, wall):
+def wall_edges(count, mx, my, yrows, sv, left, right, chosen, wall):
     rows = mx.shape[0]
     planes, slots, cols = wall.shape
     return call(
         functools.partial(wall_kernel, count),
         [struct(2 * planes, rows), struct(2 * planes, rows), struct(rows, 3 * slots, dtype=BF16)]
         + [struct(*wall.shape, dtype=BF16)] * 2,
-        [VMEM] * 9,
+        [VMEM] * 8,
         8,
-    )(mx, my, aux, yrows, sv, left, right, chosen, wall)
+    )(mx, my, yrows, sv, left, right, chosen, wall)
 
 
 def wall_sweep_kernel(sel, high_ref, low_ref, v_ref, w_ref):
@@ -611,7 +606,7 @@
     room = 2 * walls // n_y
     packed = pack(wall_owner[:, 0], wall_offset, wall_force, n_y, room)
     payload = [packed[0]] + [swap(packed[s], "gy", s) for s in range(1, n_y)]
-    mx, my, aux, my_t, aux_t, xrows, yrows, frows, scal, v, edge, first, last = factors(
+    mx, my, my_t, xrows, yrows, frows, scal, v, edge, first, last = factors(
         velocity,
         lower_x,
         upper_x,
@@ -623,14 +618,14 @@
         upper_carry_y,
     )
     left, right = rotate(last, "gy", 1), rotate(first, "gy", -1)
-    w, sv = velocity_part(mx, my_t, aux_t, v)
+    w, sv = velocity_part(mx, my_t, yrows, v)
     w, sv, edge = lax.optimization_barrier((w, sv, edge))
     mine, chosen, wall = x_edges(edge, frows, scal, left, right, payload, room)
     other = swap(mine, "gx", 1)
     both = pair(mine, other, planes)
     shifts = list(range(n_x // 2))
     received = [rotate(both, "gx", 2 * s) if s else both for s in shifts]
-    s_edge, zh, sel, high, low = wall_edges(n_y, mx, my, aux, yrows, sv, left, right, chosen, wall)
+    s_edge, zh, sel, high, low = wall_edges(n_y, mx, my, yrows, sv, left, right, chosen, wall)
     mine, moved = x_join(my, xrows, yrows, scal, s_edge, mine, other, received, shifts)
     shifts = list(range(n_y))
     received = [rotate(mine, "gy", s) if s else mine for s in shifts]

time: 38.6 us -> 38.6 us (level)
  waiting for transfers between devices: 2.39 us -> 3.32 us
  Pallas kernels: 18.3 us -> 17.4 us
    ppermute x8, waiting for transfers between devices: 1.18 us -> 2.11 us  [rotate(): lax.ppermute(value, axis, [(i, (i + shift) % count) for i in range(count)])]
    pallas_call x1, Pallas kernels: 5.04 us -> 4.35 us  [velocity_part(): call(functools.partial(velocity_kernel, 4), [struct(planes, rows, cols),...]
    pallas_call x1, Pallas kernels: 2.19 us -> 1.65 us  [wall_edges(): call(functools.partial(wall_kernel, count), [struct(2 * planes, rows), st...]
  transfers between devices with their start and end apart: 12 -> 12, of which waited for: 4 -> 4; matrix products, arithmetic and copies ran while one was open for 0% -> 0% of each run, Pallas kernels for 33% -> 30%
where the time goes in v7:
time: 38.6 us; the launch traced here: 38.5 us
  starting transfers between devices  17.7 us (46%)
  Pallas kernels  17.4 us (45%)
  waiting for transfers between devices  3.32 us (9%)
    ppermute x8, starting transfers between devices, rotate(): lax.ppermute(value, axis, [(i, (i + shift) % count) for i in range(count)])  13.1 us
    ppermute x4, starting transfers between devices, swap(): lax.ppermute(value, axis, [(i, i ^ mask) for i in range(lax.axis_size(axi...  4.62 us
    pallas_call x1, Pallas kernels, velocity_part(): call(functools.partial(velocity_kernel, 4), [struct(planes, rows, cols),...  4.35 us
    pallas_call x1, Pallas kernels, factors(): call(factor_kernel, [struct(rows, 3 * rows, dtype=BF16), struct(3 * cols,...  4.13 us
    pallas_call x1, Pallas kernels, finish(): call(functools.partial(finish_kernel, count, shifts), struct(rows, planes...  2.59 us
    ppermute x8, waiting for transfers between devices, rotate(): lax.ppermute(value, axis, [(i, (i + shift) % count) for i in range(count)])  2.11 us
    pallas_call x1, Pallas kernels, pack(): call(functools.partial(pack_kernel, count, room), [struct(room + 1, plane...  1.85 us
    pallas_call x1, Pallas kernels, wall_edges(): call(functools.partial(wall_kernel, count), [struct(2 * planes, rows), st...  1.65 us
  transfers between devices with their start and end apart: 12, of which 4 were waited for; matrix products, arithmetic and copies ran while one was open for 0% of the time, Pallas kernels for 30%

profile of v7, /device:TPU:0, one launch (start us, length us, event | category | flops | bytes accessed | tf_op | source)
XLA Modules:
  0.0 38.5 jit_solution(6385123242086798926)
XLA Ops:
  0.0 1.8 %shard_map.129 = (f32[33,16,128]{2,1,0:T(8,128)S(1)}, f32[33,16,128]{2,1,0:T(8,128)S(1)}, f32[33,16,128]{2,1,0:T(8,128)S(1)}, f32[33,16,128]{2,1,0:T(8,128)S(1)}) custom-call(s32[64]{0:T(128)} %bitcast.11, s32[64]{0:T(128)} %offset_ref.1, f32[64,16,128]{2,1,0:T(8,128)} %force_ref.1), custom_call_target="tpu_custom_call" | custom-call | tf_op jit(solution)/shard_map/pallas_call | solution.py:104
  1.9 3.0 %collective-permute-start.2 = (f32[33,16,128]{2,1,0:T(8,128)S(1)}, f32[33,16,128]{2,1,0:T(8,128)S(1)}, u32[]{:S(2)}, u32[]{:S(2)}) collective-permute-start(f32[33,16,128]{2,1,0:T(8,128)S(1)} %get-tuple-element.51), channel_id=1, source_target_pairs={{0,1},{1,0},{2,3},{3,2},{4,5},{5,4},{6,7},{7,6},{8,9},{9,8},{10,11... | collective-permute-start | bytes 811016 | tf_op jit(solution)/shard_map/ppermute | solution.py:580
  4.9 1.5 %collective-permute-start.3 = (f32[33,16,128]{2,1,0:T(8,128)S(1)}, f32[33,16,128]{2,1,0:T(8,128)S(1)}, u32[]{:S(2)}, u32[]{:S(2)}) collective-permute-start(f32[33,16,128]{2,1,0:T(8,128)S(1)} %get-tuple-element.52), channel_id=1, source_target_pairs={{0,2},{1,3},{2,0},{3,1},{4,6},{5,7},{6,4},{7,5},{8,10},{9,11},{10,... | collective-permute-start | bytes 811016 | tf_op jit(solution)/shard_map/ppermute | solution.py:580
  6.4 0.0 collective-permute-start.4
  6.4 4.1 %shard_map.127 = (bf16[256,768]{1,0:T(8,128)(2,1)S(1)}, bf16[768,256]{1,0:T(8,128)(2,1)S(1)}, bf16[768,256]{1,0:T(8,128)(2,1)S(1)}, f32[8,256]{1,0:T(8,128)S(1)}...) custom-call(f32[256,16,256]{2,1,0:T(8,128)} %v_hbm.1, ...), custom_call_target="tpu_custom_call" | custom-call | tf_op jit(solution)/shard_map/pallas_call | solution.py:235
  10.5 2.0 %collective-permute-start = (f32[16,256]{1,0:T(8,128)S(1)}, f32[16,256]{1,0:T(8,128)S(1)}, u32[]{:S(2)}, u32[]{:S(2)}) collective-permute-start(f32[16,256]{1,0:T(8,128)S(1)} %get-tuple-element.46), channel_id=1, source_target_pairs={{0,1},{1,2},{2,3},{3,0},{4,5},{5,6},{6,7},{7,4},{8,9},{9,10},{10,1... | collective-permute-start | bytes 49160 | tf_op jit(solution)/shard_map/ppermute | solution.py:585
  12.5 1.0 %collective-permute-start.1 = (f32[16,256]{1,0:T(8,128)S(1)}, f32[16,256]{1,0:T(8,128)S(1)}, u32[]{:S(2)}, u32[]{:S(2)}) collective-permute-start(f32[16,256]{1,0:T(8,128)S(1)} %get-tuple-element.47), channel_id=1, source_target_pairs={{0,3},{1,0},{2,1},{3,2},{4,7},{5,4},{6,5},{7,6},{8,11},{9,8},{10,9... | collective-permute-start | bytes 49160 | tf_op jit(solution)/shard_map/ppermute | solution.py:585
  13.6 4.3 %shard_map.128 = (f32[16,256,256]{2,1,0:T(8,128)S(1)}, f32[256,128]{1,0:T(8,128)S(1)}) custom-call(bf16[256,768]{1,0:T(8,128)(2,1)S(1)} %get-tuple-element.39.mx, bf16[768,256]{1,0:T(8,128)(2,1)S(1)} %get-tuple-element.40.my_t, f32[8,256]{1,0:T(8,128)S(1)} %get-tuple-element.36.yrows, f32[16,256,256]{2,1,0:T(8,128)S(1)} %get-tuple-element.41.v_ref), custom_call_target="tpu_custom_call" | custom-call | tf_op jit(solution)/shard_map/pallas_call | solution.py:279
  17.9 1.0 %collective-permute-done.left_ref = f32[16,256]{1,0:T(8,128)S(1)} collective-permute-done((f32[16,256]{1,0:T(8,128)S(1)}, f32[16,256]{1,0:T(8,128)S(1)}, u32[]{:S(2)}, u32[]{:S(2)}) %collective-permute-start) | collective-permute-done | bytes 16416 | tf_op jit(solution)/shard_map/ppermute | solution.py:585
  19.0 1.1 %shard_map.130 = (f32[72,128]{1,0:T(8,128)S(1)}, bf16[256,128]{1,0:T(8,128)(2,1)S(1)}, f32[16,128,256]{2,1,0:T(8,128)S(1)}) custom-call(f32[2,16,256]{2,1,0:T(8,128)S(1)} %get-tuple-element.48.edge_ref, f32[8,256]{1,0:T(8,128)S(1)} %get-tuple-element.49.frows, f32[16,256]{1,0:T(8,128)S(1)} %get-tuple-element.38.scal, ...), custom_call_target="tpu_custom_call" | custom-call | tf_op jit(solution)/shard_map/pallas_call | solution.py:347
  20.1 0.1 collective-permute-start.5
  20.1 1.2 %collective-permute-done.5.other.other_ref = f32[72,128]{1,0:T(8,128)S(1)} collective-permute-done((f32[72,128]{1,0:T(8,128)S(1)}, f32[72,128]{1,0:T(8,128)S(1)}, u32[]{:S(2)}, u32[]{:S(2)}) %collective-permute-start.5) | collective-permute-done | bytes 36896 | tf_op jit(solution)/shard_map/ppermute | solution.py:580
  21.4 1.6 %collective-permute-start.6 = (f32[72,128]{1,0:T(8,128)S(1)}, f32[72,128]{1,0:T(8,128)S(1)}, u32[]{:S(2)}, u32[]{:S(2)}) collective-permute-start(f32[72,128]{1,0:T(8,128)S(1)} %shard_map.132.refs_0_), channel_id=1, source_target_pairs={{0,8},{4,12},{8,16},{12,20},{16,24},{20,28},{24,0},{28,4},{1,9},{5... | collective-permute-start | bytes 110600 | tf_op jit(solution)/shard_map/ppermute | solution.py:585
  23.0 2.6 %collective-permute-start.7 = (f32[72,128]{1,0:T(8,128)S(1)}, f32[72,128]{1,0:T(8,128)S(1)}, u32[]{:S(2)}, u32[]{:S(2)}) collective-permute-start(f32[72,128]{1,0:T(8,128)S(1)} %shard_map.132.refs_0_), channel_id=1, source_target_pairs={{0,16},{4,20},{8,24},{12,28},{16,0},{20,4},{24,8},{28,12},{1,17},{... | collective-permute-start | bytes 110600 | tf_op jit(solution)/shard_map/ppermute | solution.py:585
  25.6 1.3 %collective-permute-start.8 = (f32[72,128]{1,0:T(8,128)S(1)}, f32[72,128]{1,0:T(8,128)S(1)}, u32[]{:S(2)}, u32[]{:S(2)}) collective-permute-start(f32[72,128]{1,0:T(8,128)S(1)} %shard_map.132.refs_0_), channel_id=1, source_target_pairs={{0,24},{4,28},{8,0},{12,4},{16,8},{20,12},{24,16},{28,20},{1,25},{... | collective-permute-start | bytes 110600 | tf_op jit(solution)/shard_map/ppermute | solution.py:585
  26.9 1.6 %shard_map.131 = (f32[32,256]{1,0:T(8,128)S(1)}, f32[32,256]{1,0:T(8,128)S(1)}, bf16[256,384]{1,0:T(8,128)(2,1)S(1)}, bf16[16,128,256]{2,1,0:T(8,128)(2,1)S(1)}, bf16[16,128,256]{2,1,0:T(8,128)(2,1)S(1)}) custom-call(bf16[256,768]{1,0:T(8,128)(2,1)S(1)} %get-tuple-element.39.mx, bf16[768,256]{1,0:T(8,128)(2,1)S(1)} %get-tuple-element.37.my, ...), custom_call_target="tpu_custom_call" | custom-call | tf_op jit(solution)/shard_map/pallas_call | solution.py:393
  28.6 0.9 %collective-permute-done.8.refs_3_ = f32[72,128]{1,0:T(8,128)S(1)} collective-permute-done((f32[72,128]{1,0:T(8,128)S(1)}, f32[72,128]{1,0:T(8,128)S(1)}, u32[]{:S(2)}, u32[]{:S(2)}) %collective-permute-start.8) | collective-permute-done | bytes 36896 | tf_op jit(solution)/shard_map/ppermute | solution.py:585
  29.5 0.2 shard_map.133
  29.7 1.6 %collective-permute-start.9 = (f32[72,128]{1,0:T(8,128)S(1)}, f32[72,128]{1,0:T(8,128)S(1)}, u32[]{:S(2)}, u32[]{:S(2)}) collective-permute-start(f32[72,128]{1,0:T(8,128)S(1)} %get-tuple-element.64.refs_0_), channel_id=1, source_target_pairs={{0,1},{1,2},{2,3},{3,0},{4,5},{5,6},{6,7},{7,4},{8,9},{9,10},{10,1... | collective-permute-start | bytes 110600 | tf_op jit(solution)/shard_map/ppermute | solution.py:585
  31.4 0.6 %collective-permute-start.10 = (f32[72,128]{1,0:T(8,128)S(1)}, f32[72,128]{1,0:T(8,128)S(1)}, u32[]{:S(2)}, u32[]{:S(2)}) collective-permute-start(f32[72,128]{1,0:T(8,128)S(1)} %get-tuple-element.64.refs_0_), channel_id=1, source_target_pairs={{0,2},{1,3},{2,0},{3,1},{4,6},{5,7},{6,4},{7,5},{8,10},{9,11},{10,... | collective-permute-start | bytes 110600 | tf_op jit(solution)/shard_map/ppermute | solution.py:585
  31.9 2.3 %collective-permute-start.11 = (f32[72,128]{1,0:T(8,128)S(1)}, f32[72,128]{1,0:T(8,128)S(1)}, u32[]{:S(2)}, u32[]{:S(2)}) collective-permute-start(f32[72,128]{1,0:T(8,128)S(1)} %get-tuple-element.64.refs_0_), channel_id=1, source_target_pairs={{0,3},{1,0},{2,1},{3,2},{4,7},{5,4},{6,5},{7,6},{8,11},{9,8},{10,9... | collective-permute-start | bytes 110600 | tf_op jit(solution)/shard_map/ppermute | solution.py:585
  34.2 1.5 %shard_map.134.w_ref = f32[16,256,256]{2,1,0:T(8,128)S(1)} custom-call(bf16[256,384]{1,0:T(8,128)(2,1)S(1)} %get-tuple-element.60.sel, bf16[16,128,256]{2,1,0:T(8,128)(2,1)S(1)} %get-tuple-element.61.high_ref, bf16[16,128,256]{2,1,0:T(8,128)(2,1)S(1)} %get-tuple-element.62.low_ref, ...), custom_call_target="tpu_custom_call", output_to_operand_aliasing={{}: (3, {})} | custom-call | tf_op jit(solution)/shard_map/pallas_call | solution.py:409
  35.7 0.1 collective-permute-done.11.refs_3_
  35.9 2.6 %shard_map.135 = f32[256,16,256]{2,1,0:T(8,128)} custom-call(f32[8,256]{1,0:T(8,128)S(1)} %get-tuple-element.35.xrows, f32[8,256]{1,0:T(8,128)S(1)} %get-tuple-element.36.yrows, f32[48,256]{1,0:T(8,128)S(1)} %get-tuple-element.58.moved, s32[2,256]{1,0:T(2,128)S(1)} %bitcast.6, f32[32,256]{1,0:T(8,128)S(1)} %get-tuple-element.59.zh_ref, ...), custom_call_target="tpu_custom_call" | custom-call | tf_op jit(solution)/shard_map/pallas_call | solution.py:564
  (11 shorter events, 0.0 us)
Async XLA Ops:
  1.9 17.1 %collective-permute-start.2 = (f32[33,16,128]{2,1,0:T(8,128)S(1)}, f32[33,16,128]{2,1,0:T(8,128)S(1)}, u32[]{:S(2)}, u32[]{:S(2)}) collective-permute-start(f32[33,16,128]{2,1,0:T(8,128)S(1)} %get-tuple-element.51), channel_id=1, source_target_pairs={{0,1},{1,0},{2,3},{3,2},{4,5},{5,4},{6,7},{7,6},{8,9},{9,8},{10,11... | collective-permute-start | bytes 811016 | tf_op jit(solution)/shard_map/ppermute | solution.py:580
  4.9 14.1 %collective-permute-start.3 = (f32[33,16,128]{2,1,0:T(8,128)S(1)}, f32[33,16,128]{2,1,0:T(8,128)S(1)}, u32[]{:S(2)}, u32[]{:S(2)}) collective-permute-start(f32[33,16,128]{2,1,0:T(8,128)S(1)} %get-tuple-element.52), channel_id=1, source_target_pairs={{0,2},{1,3},{2,0},{3,1},{4,6},{5,7},{6,4},{7,5},{8,10},{9,11},{10,... | collective-permute-start | bytes 811016 | tf_op jit(solution)/shard_map/ppermute | solution.py:580
  6.4 12.6 %collective-permute-start.4 = (f32[33,16,128]{2,1,0:T(8,128)S(1)}, f32[33,16,128]{2,1,0:T(8,128)S(1)}, u32[]{:S(2)}, u32[]{:S(2)}) collective-permute-start(f32[33,16,128]{2,1,0:T(8,128)S(1)} %get-tuple-element.53), channel_id=1, source_target_pairs={{0,3},{1,2},{2,1},{3,0},{4,7},{5,6},{6,5},{7,4},{8,11},{9,10},{10,... | collective-permute-start | bytes 811016 | tf_op jit(solution)/shard_map/ppermute | solution.py:580
  10.5 8.4 %collective-permute-start = (f32[16,256]{1,0:T(8,128)S(1)}, f32[16,256]{1,0:T(8,128)S(1)}, u32[]{:S(2)}, u32[]{:S(2)}) collective-permute-start(f32[16,256]{1,0:T(8,128)S(1)} %get-tuple-element.46), channel_id=1, source_target_pairs={{0,1},{1,2},{2,3},{3,0},{4,5},{5,6},{6,7},{7,4},{8,9},{9,10},{10,1... | collective-permute-start | bytes 49160 | tf_op jit(solution)/shard_map/ppermute | solution.py:585
  12.5 6.4 %collective-permute-start.1 = (f32[16,256]{1,0:T(8,128)S(1)}, f32[16,256]{1,0:T(8,128)S(1)}, u32[]{:S(2)}, u32[]{:S(2)}) collective-permute-start(f32[16,256]{1,0:T(8,128)S(1)} %get-tuple-element.47), channel_id=1, source_target_pairs={{0,3},{1,0},{2,1},{3,2},{4,7},{5,4},{6,5},{7,6},{8,11},{9,8},{10,9... | collective-permute-start | bytes 49160 | tf_op jit(solution)/shard_map/ppermute | solution.py:585
  20.1 1.3 %collective-permute-start.5 = (f32[72,128]{1,0:T(8,128)S(1)}, f32[72,128]{1,0:T(8,128)S(1)}, u32[]{:S(2)}, u32[]{:S(2)}) collective-permute-start(f32[72,128]{1,0:T(8,128)S(1)} %get-tuple-element.57.mine.mine_ref), channel_id=1, source_target_pairs={{0,4},{4,0},{8,12},{12,8},{16,20},{20,16},{24,28},{28,24},{1,5},{5... | collective-permute-start | bytes 110600 | tf_op jit(solution)/shard_map/ppermute | solution.py:580
  21.4 7.2 %collective-permute-start.6 = (f32[72,128]{1,0:T(8,128)S(1)}, f32[72,128]{1,0:T(8,128)S(1)}, u32[]{:S(2)}, u32[]{:S(2)}) collective-permute-start(f32[72,128]{1,0:T(8,128)S(1)} %shard_map.132.refs_0_), channel_id=1, source_target_pairs={{0,8},{4,12},{8,16},{12,20},{16,24},{20,28},{24,0},{28,4},{1,9},{5... | collective-permute-start | bytes 110600 | tf_op jit(solution)/shard_map/ppermute | solution.py:585
  23.0 5.6 %collective-permute-start.7 = (f32[72,128]{1,0:T(8,128)S(1)}, f32[72,128]{1,0:T(8,128)S(1)}, u32[]{:S(2)}, u32[]{:S(2)}) collective-permute-start(f32[72,128]{1,0:T(8,128)S(1)} %shard_map.132.refs_0_), channel_id=1, source_target_pairs={{0,16},{4,20},{8,24},{12,28},{16,0},{20,4},{24,8},{28,12},{1,17},{... | collective-permute-start | bytes 110600 | tf_op jit(solution)/shard_map/ppermute | solution.py:585
  25.6 4.0 %collective-permute-start.8 = (f32[72,128]{1,0:T(8,128)S(1)}, f32[72,128]{1,0:T(8,128)S(1)}, u32[]{:S(2)}, u32[]{:S(2)}) collective-permute-start(f32[72,128]{1,0:T(8,128)S(1)} %shard_map.132.refs_0_), channel_id=1, source_target_pairs={{0,24},{4,28},{8,0},{12,4},{16,8},{20,12},{24,16},{28,20},{1,25},{... | collective-permute-start | bytes 110600 | tf_op jit(solution)/shard_map/ppermute | solution.py:585
  29.7 6.0 %collective-permute-start.9 = (f32[72,128]{1,0:T(8,128)S(1)}, f32[72,128]{1,0:T(8,128)S(1)}, u32[]{:S(2)}, u32[]{:S(2)}) collective-permute-start(f32[72,128]{1,0:T(8,128)S(1)} %get-tuple-element.64.refs_0_), channel_id=1, source_target_pairs={{0,1},{1,2},{2,3},{3,0},{4,5},{5,6},{6,7},{7,4},{8,9},{9,10},{10,1... | collective-permute-start | bytes 110600 | tf_op jit(solution)/shard_map/ppermute | solution.py:585
  31.4 4.4 %collective-permute-start.10 = (f32[72,128]{1,0:T(8,128)S(1)}, f32[72,128]{1,0:T(8,128)S(1)}, u32[]{:S(2)}, u32[]{:S(2)}) collective-permute-start(f32[72,128]{1,0:T(8,128)S(1)} %get-tuple-element.64.refs_0_), channel_id=1, source_target_pairs={{0,2},{1,3},{2,0},{3,1},{4,6},{5,7},{6,4},{7,5},{8,10},{9,11},{10,... | collective-permute-start | bytes 110600 | tf_op jit(solution)/shard_map/ppermute | solution.py:585
  31.9 4.0 %collective-permute-start.11 = (f32[72,128]{1,0:T(8,128)S(1)}, f32[72,128]{1,0:T(8,128)S(1)}, u32[]{:S(2)}, u32[]{:S(2)}) collective-permute-start(f32[72,128]{1,0:T(8,128)S(1)} %get-tuple-element.64.refs_0_), channel_id=1, source_target_pairs={{0,3},{1,0},{2,1},{3,2},{4,7},{5,4},{6,5},{7,6},{8,11},{9,8},{10,9... | collective-permute-start | bytes 110600 | tf_op jit(solution)/shard_map/ppermute | solution.py:585
  34.2 1.7 %copy-start = (s32[256,2]{0,1:T(2,128)S(1)}, s32[256,2]{0,1:T(2,128)}, u32[]{:S(2)}) copy-start(s32[256,2]{0,1:T(2,128)} %param.25) | copy-start | bytes 6148
